TPU v7x, 32 devices: a whole 2x2x4 slice. The times are simulated.
32 devices in a mesh: dp: 4 (over x, core), ctx: 8 (over z, y).
Axes of the slice: x: 2, y: 2, z: 4, core: 2. Of those that a mesh axis runs over, the one named last changes fastest.
Arguments:
- queries: bfloat16 [4, 1024, 1024], P('dp', 'ctx'), may hold values from -60 to 60
- keys: bfloat16 [4, 1024, 128], P('dp', 'ctx'), may hold values from -6 to 6
- values: bfloat16 [4, 1024, 192], P('dp', 'ctx'), may hold values from -96 to 96
- features_fine: bfloat16 [4, 2048, 1536], P('dp', 'ctx'), may hold values from -6 to 6
- rc_state: bfloat16 [4, 1024, 1536], P('dp', 'ctx'), may hold values from -6 to 6
- conv_weight: float32 [5, 1536], replicated, may hold values from -2.5 to 2.5
Outputs:
- d_fine: bfloat16 [4, 2048, 1536], P('dp', 'ctx')
- d_weight: float32 [5, 1536], replicated
All inputs are finite; a program needn't handle non-finite values.
Results may differ from a plain program's by a relative error of at most 0.0085.
Values may be sent and summed in bfloat16 or wider, within the bound.
No kernel may reach another device: no remote copies, remote signals or barrier semaphores. Data moves between devices by JAX's collectives and lax.ppermute only.
A program may use at most 64 MiB of HBM per device.

v0:
```python
import math

import jax
import jax.numpy as jnp
from jax import lax
from jax.sharding import PartitionSpec as P

HEADS = 8
KW = 5


def padded_2(cells, sides, width):
    for axis, dim in sides:
        count = lax.axis_size(axis)
        ends = count - 1
        head = lax.slice_in_dim(cells, 0, width, axis=dim)
        tail = lax.slice_in_dim(cells, cells.shape[dim] - width, cells.shape[dim], axis=dim)
        cells = jnp.concatenate(
            [
                lax.ppermute(tail, axis, [(i, (i + 1) % count) for i in range(ends)]),
                cells,
                lax.ppermute(head, axis, [((i + 1) % count, i) for i in range(ends)]),
            ],
            axis=dim,
        )
    return cells


def from_partner(value, axis, distance):
    mask = 2**distance
    pairs = [(source, source ^ mask) for source in range(lax.axis_size(axis))]
    return lax.ppermute(value, axis, pairs)


def body(queries, keys, values, features_fine, rc_state, conv_weight):
    tok_rows = queries.shape[1]
    key_size = keys.shape[2]
    value_size = values.shape[2]
    q_heads = queries[0].reshape(tok_rows, HEADS, key_size)
    ctx_count = lax.axis_size("ctx")
    bit_count = ctx_count.bit_length() - 1
    run_top = jnp.full((tok_rows, HEADS), -1e30, jnp.float32)
    key_piece = lax.all_gather(keys, "ctx", axis=1, tiled=True)
    value_piece = lax.all_gather(values, "ctx", axis=1, tiled=True)
    scores = jnp.einsum(
        "qhd,kd->qhk", q_heads, key_piece[0], preferred_element_type=jnp.float32
    ) * key_size ** (-0.5)
    new_top = jnp.maximum(run_top, jnp.max(scores, axis=-1))
    expd = jnp.exp(scores - new_top[..., None])
    new_total = jnp.sum(expd, axis=-1)
    mixed = jnp.einsum(
        "qhk,kv->qhv", expd.astype(jnp.bfloat16), value_piece[0], preferred_element_type=jnp.float32
    )
    attended = (mixed / new_total[..., None]).reshape(tok_rows, HEADS * value_size)[None]
    padded = padded_2(features_fine, (("ctx", 1),), 2)
    taps = [padded[:, k : k + 2 * tok_rows : 2, :].astype(jnp.float32) for k in range(KW)]
    coarse = conv_weight[0] * taps[0]
    for k in range(1, KW):
        coarse = coarse + conv_weight[k] * taps[k]
    mirrored = rc_state
    for bit in range(bit_count):
        mirrored = from_partner(mirrored, "ctx", bit)
    grad = coarse + attended - mirrored[:, ::-1, :].astype(jnp.float32)
    gpad = padded_2(grad.astype(jnp.bfloat16), (("ctx", 1),), 1).astype(grad.dtype)
    even = (
        conv_weight[0] * gpad[:, 2:]
        + conv_weight[2] * gpad[:, 1:-1]
        + conv_weight[4] * gpad[:, :-2]
    )
    odd = conv_weight[1] * gpad[:, 2:] + conv_weight[3] * gpad[:, 1:-1]
    d_fine = (
        jnp.stack([even, odd], axis=2)
        .reshape(grad.shape[0], 2 * tok_rows, grad.shape[2])
        .astype(jnp.bfloat16)
    )
    partial_grad = jnp.stack([jnp.sum(grad * taps[k], axis=(0, 1)) for k in range(KW)])
    summed = lax.psum(partial_grad, ("dp", "ctx"))
    scale = 1.0 / math.sqrt(lax.axis_size("dp") * tok_rows * ctx_count)
    return (d_fine, summed * scale)


def solution(mesh):
    placed = (
        P("dp", "ctx", None),
        P("dp", "ctx", None),
        P("dp", "ctx", None),
        P("dp", "ctx", None),
        P("dp", "ctx", None),
        P(),
    )
    return jax.shard_map(
        body, mesh=mesh, in_specs=placed, out_specs=(P("dp", "ctx", None), P()), check_vma=False
    )
```

profile of v0, /device:TPU:0, one launch (start us, length us, event | category | flops | bytes accessed | tf_op | source)
XLA Modules:
  0.0 148.6 jit_solution(15062111440598943341)
XLA Ops:
  0.6 0.0 copy-start.1
  0.6 0.8 fusion.30
  1.4 4.9 %collective-permute-start = (bf16[1,2,1536]{2,1,0:T(2,128)(2,1)S(1)}, bf16[1,2,1536]{2,1,0:T(2,128)(2,1)S(1)}, u32[]{:S(2)}, u32[]{:S(2)}) collective-permute-start(bf16[1,2,1536]{2,1,0:T(2,128)(2,1)S(1)} %get-tuple-element.15), channel_id=1, source_target_pairs={{0,1},{1,2},{2,3},{3,4},{4,5},{5,6},{6,7},{8,9},{9,10},{10,11},{11... | collective-permute-start | bytes 18440 | tf_op jit(solution)/shard_map/ppermute | solution.py:20
  6.3 1.3 collective-permute-start.1
  7.6 2.7 %collective-permute-start.2 = (bf16[1,128,1536]{2,1,0:T(8,128)(2,1)}, bf16[1,128,1536]{2,1,0:T(8,128)(2,1)S(1)}, u32[]{:S(2)}, u32[]{:S(2)}) collective-permute-start(bf16[1,128,1536]{2,1,0:T(8,128)(2,1)} %param.10), channel_id=1, source_target_pairs={{0,1},{1,0},{2,3},{3,2},{4,5},{5,4},{6,7},{7,6},{8,9},{9,8},{10,11... | collective-permute-start | bytes 1179656 | tf_op jit(solution)/shard_map/ppermute | solution.py:32
  10.3 35.2 %all_gather.6 = bf16[1,1024,128]{2,1,0:T(8,128)(2,1)S(1)} all-gather(bf16[1,128,128]{2,1,0:T(8,128)(2,1)} %param.7), channel_id=1, replica_groups=mesh['dp'=4,'ctx'=8] {'ctx'}, dimensions={1}, use_global_device_ids=true | all-gather | bytes 294912 | tf_op jit(solution)/shard_map/all_gather | solution.py:43
  45.5 1.0 copy.11
  46.5 0.8 multiply_reduce_fusion
  47.3 0.0 collective-permute-done.2
  47.3 0.1 collective-permute-start.3
  47.4 0.0 copy-done.1
  47.4 30.8 %all_gather.7 = bf16[1,1024,192]{1,2,0:T(8,128)(2,1)S(1)} all-gather(bf16[1,128,192]{1,2,0:T(8,128)(2,1)S(1)} %copy-done.1), channel_id=1, replica_groups=mesh['dp'=4,'ctx'=8] {'ctx'}, dimensions={1}, use_global_device_ids=true | all-gather | bytes 442368 | tf_op jit(solution)/shard_map/all_gather | solution.py:44
  78.2 0.9 fusion
  79.1 0.0 copy-start.2
  79.1 0.0 copy-start
  79.2 0.0 collective-permute-done.3
  79.2 0.6 collective-permute-start.4
  79.8 1.1 fusion.6
  80.9 0.0 copy-done.2
  80.9 0.1 slice_reduce_fusion.4
  81.0 0.0 copy-done
  81.0 0.7 slice.65
  81.8 0.3 copy.9
  82.0 0.0 collective-permute-done
  82.0 0.0 collective-permute-done.1
  82.1 0.2 pad_maximum_fusion
  82.3 0.7 slice.61
  83.0 0.7 slice.63
  83.8 0.9 slice.67
  84.7 2.4 %slice.69 = bf16[1,128,1536]{2,1,0:T(8,128)(2,1)} slice(bf16[1,260,1536]{2,1,0:T(8,128)(2,1)S(1)} %pad_maximum_fusion), slice={[0:1:1], [4:260:2], [0:1536:1]} | slice | bytes 786432 | tf_op jit(solution)/shard_map/slice | solution.py:56
  87.0 5.2 %collective-permute-done.4 = bf16[1,128,1536]{2,1,0:T(8,128)(2,1)} collective-permute-done((bf16[1,128,1536]{2,1,0:T(8,128)(2,1)}, bf16[1,128,1536]{2,1,0:T(8,128)(2,1)}, u32[]{:S(2)}, u32[]{:S(2)}) %collective-permute-start.4) | collective-permute-done | bytes 393248 | tf_op jit(solution)/shard_map/ppermute | solution.py:32
  92.3 4.7 %rev.3 = bf16[1,128,1536]{2,1,0:T(8,128)(2,1)S(1)} reverse(bf16[1,128,1536]{2,1,0:T(8,128)(2,1)} %collective-permute-done.4), dimensions={1} | reverse | bytes 786432 | tf_op jit(solution)/shard_map/rev | solution.py:63
  97.0 1.8 %fusion.19 = (f32[1536]{0:T(1024)S(1)}, f32[1536]{0:T(1024)S(1)}, f32[1536]{0:T(1024)S(1)}, f32[1536]{0:T(1024)S(1)}, f32[1536]{0:T(1024)S(1)}, /*index=5*/bf16[1,128,1536]{2,1,0:T(8,128)(2,1)S(1)}) fusion(bf16[1,128,1536]{2,1,0:T(8,128)(2,1)} %slice.69, bf16[1,128,1536]{2,1,0:T(8,128)(2,1)S(1)} %slice.67, bf16[1,128,1536]{2,1,0:T(8,128)(2,1)S(1)} %slice.65, ...), kind=kLoop, calls=%fused_computation.29 | loop fusion | flops 5497344 | bytes 3600384 | tf_op jit(solution)/shard_map/reduce_sum | solution.py:76
  98.9 0.1 stack.38
  99.0 37.4 %psum.7 = f32[5,1536]{1,0:T(8,128)S(1)} all-reduce(f32[5,1536]{1,0:T(8,128)S(1)} %stack.38), channel_id=1, replica_groups=mesh['dp'=4,'ctx'=8] {'dp','ctx'}, use_global_device_ids=true, to_apply=%region_7.0 | all-reduce | flops 7680 | bytes 61440 | tf_op jit(solution)/shard_map/psum | solution.py:77
  136.4 4.2 %collective-permute-start.5 = (bf16[1,1,1536]{2,1,0:T(2,128)(2,1)S(1)}, bf16[1,1,1536]{2,1,0:T(2,128)(2,1)S(1)}, u32[]{:S(2)}, u32[]{:S(2)}) collective-permute-start(bf16[1,1,1536]{2,1,0:T(2,128)(2,1)S(1)} %get-tuple-element.17), channel_id=1, source_target_pairs={{0,1},{1,2},{2,3},{3,4},{4,5},{5,6},{6,7},{8,9},{9,10},{10,11},{11... | collective-permute-start | bytes 9224 | tf_op jit(solution)/shard_map/ppermute | solution.py:20
  140.5 1.3 collective-permute-start.6
  141.8 0.6 broadcast_multiply_fusion
  142.5 0.0 collective-permute-done.5
  142.5 3.6 %collective-permute-done.6 = bf16[1,1,1536]{2,1,0:T(2,128)(2,1)S(1)} collective-permute-done((bf16[1,1,1536]{2,1,0:T(2,128)(2,1)S(1)}, bf16[1,1,1536]{2,1,0:T(2,128)(2,1)S(1)}, u32[]{:S(2)}, u32[]{:S(2)}) %collective-permute-start.6) | collective-permute-done | bytes 3104 | tf_op jit(solution)/shard_map/ppermute | solution.py:22
  146.1 0.1 maximum_convert_fusion
  146.2 0.3 fusion.23
  146.5 0.1 pad_maximum_fusion.1
  146.6 0.8 copy.10
  147.4 1.2 convert_element_type.56
  (7 shorter events, 0.1 us)
Async XLA Ops:
  0.6 46.8 %copy-start.1 = (bf16[1,128,192]{1,2,0:T(8,128)(2,1)S(1)}, bf16[1,128,192]{1,2,0:T(8,128)(2,1)}, u32[]{:S(2)}) copy-start(bf16[1,128,192]{1,2,0:T(8,128)(2,1)} %param.8) | copy-start | bytes 147460
  1.4 80.6 %collective-permute-start = (bf16[1,2,1536]{2,1,0:T(2,128)(2,1)S(1)}, bf16[1,2,1536]{2,1,0:T(2,128)(2,1)S(1)}, u32[]{:S(2)}, u32[]{:S(2)}) collective-permute-start(bf16[1,2,1536]{2,1,0:T(2,128)(2,1)S(1)} %get-tuple-element.15), channel_id=1, source_target_pairs={{0,1},{1,2},{2,3},{3,4},{4,5},{5,6},{6,7},{8,9},{9,10},{10,11},{11... | collective-permute-start | bytes 18440 | tf_op jit(solution)/shard_map/ppermute | solution.py:20
  6.3 75.7 %collective-permute-start.1 = (bf16[1,2,1536]{2,1,0:T(2,128)(2,1)S(1)}, bf16[1,2,1536]{2,1,0:T(2,128)(2,1)S(1)}, u32[]{:S(2)}, u32[]{:S(2)}) collective-permute-start(bf16[1,2,1536]{2,1,0:T(2,128)(2,1)S(1)} %get-tuple-element.16), channel_id=1, source_target_pairs={{1,0},{2,1},{3,2},{4,3},{5,4},{6,5},{7,6},{9,8},{10,9},{11,10},{12... | collective-permute-start | bytes 18440 | tf_op jit(solution)/shard_map/ppermute | solution.py:22
  7.6 39.7 %collective-permute-start.2 = (bf16[1,128,1536]{2,1,0:T(8,128)(2,1)}, bf16[1,128,1536]{2,1,0:T(8,128)(2,1)S(1)}, u32[]{:S(2)}, u32[]{:S(2)}) collective-permute-start(bf16[1,128,1536]{2,1,0:T(8,128)(2,1)} %param.10), channel_id=1, source_target_pairs={{0,1},{1,0},{2,3},{3,2},{4,5},{5,4},{6,7},{7,6},{8,9},{9,8},{10,11... | collective-permute-start | bytes 1179656 | tf_op jit(solution)/shard_map/ppermute | solution.py:32
  47.3 31.8 %collective-permute-start.3 = (bf16[1,128,1536]{2,1,0:T(8,128)(2,1)S(1)}, bf16[1,128,1536]{2,1,0:T(8,128)(2,1)}, u32[]{:S(2)}, u32[]{:S(2)}) collective-permute-start(bf16[1,128,1536]{2,1,0:T(8,128)(2,1)S(1)} %collective-permute-done.2), channel_id=1, source_target_pairs={{0,2},{1,3},{2,0},{3,1},{4,6},{5,7},{6,4},{7,5},{8,10},{9,11},{10,... | collective-permute-start | bytes 1179656 | tf_op jit(solution)/shard_map/ppermute | solution.py:32
  79.1 1.8 %copy-start.2 = (f32[5,1536]{1,0:T(8,128)S(1)}, f32[5,1536]{1,0:T(8,128)}, u32[]{:S(2)}) copy-start(f32[5,1536]{1,0:T(8,128)} %param.11) | copy-start | bytes 92164
  79.1 1.9 %copy-start = (bf16[1,256,1536]{2,1,0:T(8,128)(2,1)S(1)}, bf16[1,256,1536]{2,1,0:T(8,128)(2,1)}, u32[]{:S(2)}) copy-start(bf16[1,256,1536]{2,1,0:T(8,128)(2,1)} %param.9) | copy-start | bytes 2359300
  79.2 13.1 %collective-permute-start.4 = (bf16[1,128,1536]{2,1,0:T(8,128)(2,1)}, bf16[1,128,1536]{2,1,0:T(8,128)(2,1)}, u32[]{:S(2)}, u32[]{:S(2)}) collective-permute-start(bf16[1,128,1536]{2,1,0:T(8,128)(2,1)} %collective-permute-done.3), channel_id=1, source_target_pairs={{0,4},{1,5},{2,6},{3,7},{4,0},{5,1},{6,2},{7,3},{8,12},{9,13},{10,... | collective-permute-start | bytes 1179656 | tf_op jit(solution)/shard_map/ppermute | solution.py:32
  136.4 6.1 %collective-permute-start.5 = (bf16[1,1,1536]{2,1,0:T(2,128)(2,1)S(1)}, bf16[1,1,1536]{2,1,0:T(2,128)(2,1)S(1)}, u32[]{:S(2)}, u32[]{:S(2)}) collective-permute-start(bf16[1,1,1536]{2,1,0:T(2,128)(2,1)S(1)} %get-tuple-element.17), channel_id=1, source_target_pairs={{0,1},{1,2},{2,3},{3,4},{4,5},{5,6},{6,7},{8,9},{9,10},{10,11},{11... | collective-permute-start | bytes 9224 | tf_op jit(solution)/shard_map/ppermute | solution.py:20
  140.5 5.5 %collective-permute-start.6 = (bf16[1,1,1536]{2,1,0:T(2,128)(2,1)S(1)}, bf16[1,1,1536]{2,1,0:T(2,128)(2,1)S(1)}, u32[]{:S(2)}, u32[]{:S(2)}) collective-permute-start(bf16[1,1,1536]{2,1,0:T(2,128)(2,1)S(1)} %get-tuple-element.18), channel_id=1, source_target_pairs={{1,0},{2,1},{3,2},{4,3},{5,4},{6,5},{7,6},{9,8},{10,9},{11,10},{12... | collective-permute-start | bytes 9224 | tf_op jit(solution)/shard_map/ppermute | solution.py:22
where the time goes:
time: 150 us; the launch traced here: 149 us
  blocking collectives  103 us (69%)
  starting transfers between devices  15.1 us (10%)
  local copies, waits for them, and re-layouts  14.4 us (10%)
  waiting for transfers between devices  8.83 us (6%)
  other arithmetic  4.1 us (3%)
  matrix products  1.88 us (1%)
    psum x1, blocking collectives, body(): summed = lax.psum(partial_grad, ('dp', 'ctx'))  37.4 us
    all_gather x1, blocking collectives, body(): key_piece = lax.all_gather(keys, 'ctx', axis=1, tiled=True)  35.2 us
    all_gather x1, blocking collectives, body(): value_piece = lax.all_gather(values, 'ctx', axis=1, tiled=True)  30.8 us
    ppermute x2, starting transfers between devices, padded_2(): lax.ppermute(tail, axis, [(i, (i + 1) % count) for i in range(ends)])  9.08 us
    slice x5, local copies, waits for them, and re-layouts, body(): padded[:, k:k + 2 * tok_rows:2, :].astype(jnp.float32)  5.48 us
    ppermute x3, waiting for transfers between devices, from_partner(): return lax.ppermute(value, axis, pairs)  5.23 us
    rev x1, local copies, waits for them, and re-layouts, body(): grad = coarse + attended - mirrored[:, ::-1, :].astype(jnp.float32)  4.74 us
    ppermute x2, waiting for transfers between devices, padded_2(): lax.ppermute(head, axis, [((i + 1) % count, i) for i in range(ends)])  3.6 us
  transfers between devices with their start and end apart: 7, of which 2 were waited for; matrix products, arithmetic and copies ran while one was open for 7% of the time, Pallas kernels for 0%

commit v1 on v0

v1 whole, which is shorter than its diff:
```python
import math

import jax
import jax.numpy as jnp
from jax import lax
from jax.experimental import pallas as pl
from jax.experimental.pallas import tpu as pltpu
from jax.sharding import PartitionSpec as P

HEADS = 8
KW = 5
EDGE = 8
LANES = 128


def attend_kernel(edge, q, up, down, f, w, *rest, blocks):
    kv = rest[:blocks]
    base, base_edge, fine, keys, vals_lo, vals_hi, att = rest[blocks:]
    rows = q.shape[0]
    dk = q.shape[1] // HEADS
    per = kv[0].shape[1]
    dv = kv[0].shape[0] - per
    wide = vals_lo.shape[0]
    up_f = up[...].astype(jnp.float32)
    down_f = down[...].astype(jnp.float32)
    for c in range(fine.shape[0]):
        at = slice(c * LANES, (c + 1) * LANES)
        fine[c, 0:EDGE] = up_f[:, at]
        fine[c, EDGE : EDGE + 2 * rows] = f[:, at].astype(jnp.float32)
        fine[c, EDGE + 2 * rows :] = down_f[:, at]
    for j in range(blocks):
        keys[j * per : (j + 1) * per] = kv[j][0:per]
        vals_lo[0:dv, j * per : (j + 1) * per] = kv[j][per:]
        vals_hi[wide - dv :, j * per : (j + 1) * per] = kv[j][per:]
    vals_lo[dv:] = jnp.zeros((wide - dv, blocks * per), vals_lo.dtype)
    vals_hi[0 : wide - dv] = jnp.zeros((wide - dv, blocks * per), vals_hi.dtype)
    q_edge = jnp.concatenate(
        [up_f[1:2, : HEADS * dk], down_f[5:6, : HEADS * dk], jnp.zeros((14, HEADS * dk), jnp.float32)], axis=0
    ).astype(q.dtype)
    scale = dk ** (-0.5)

    def head(h, vals):
        q_h = jnp.concatenate([q[:, h * dk : (h + 1) * dk], q_edge[:, h * dk : (h + 1) * dk]], axis=0)
        s = lax.dot_general(q_h, keys[...], (((1,), (1,)), ((), ())), preferred_element_type=jnp.float32) * scale
        p = jnp.exp(s - jnp.max(s, axis=1, keepdims=True))
        total = jnp.sum(p, axis=1, keepdims=True)
        o = lax.dot_general(
            p.astype(jnp.bfloat16), vals[...], (((1,), (1,)), ((), ())), preferred_element_type=jnp.float32
        )
        return o / total

    for pair in range(HEADS // 2):
        lo = head(2 * pair, vals_lo)
        hi = head(2 * pair + 1, vals_hi)
        at = 2 * dv * pair
        over = 2 * wide - 2 * dv
        att[:, at : at + wide - over] = lo[:, : wide - over]
        att[:, at + wide - over : at + wide] = lo[:, wide - over :] + hi[:, :over]
        att[:, at + wide : at + 2 * dv] = hi[:, over:]
    first = edge[0] == 0
    last = edge[0] == edge[1] - 1
    for c in range(fine.shape[0]):
        at = slice(c * LANES, (c + 1) * LANES)
        acc = att[0:rows, at]
        left = att[rows : rows + 1, at]
        right = att[rows + 1 : rows + 2, at]
        for k in range(KW):
            w_k = w[k : k + 1, at]
            acc = acc + w_k * fine[c, pl.ds(EDGE - 2 + k, rows, stride=2), :]
            left = left + w_k * fine[c, EDGE - 4 + k : EDGE - 3 + k]
            right = right + w_k * fine[c, EDGE + 2 * rows - 2 + k : EDGE + 2 * rows - 1 + k]
        base[:, at] = acc
        base_edge[0:1, at] = jnp.where(first, 0.0, left)
        base_edge[1:2, at] = jnp.where(last, 0.0, right)


def grad_kernel(base, base_edge, fine, rc, rc_edge, partial, grad):
    rows = base.shape[0]
    flip = (
        lax.broadcasted_iota(jnp.int32, (rows, rows), 0) + lax.broadcasted_iota(jnp.int32, (rows, rows), 1) == rows - 1
    ).astype(jnp.bfloat16)
    for c in range(fine.shape[0]):
        at = slice(c * LANES, (c + 1) * LANES)
        g = base[:, at] - jnp.dot(flip, rc[:, at], preferred_element_type=jnp.float32)
        ends = base_edge[0:2, at] - rc_edge[:, at].astype(jnp.float32)
        grad[EDGE : EDGE + rows, at] = g
        grad[EDGE - 1 : EDGE, at] = ends[0:1]
        grad[EDGE + rows : EDGE + rows + 1, at] = ends[1:2]
        for k in range(KW):
            partial[k : k + 1, at] = jnp.sum(
                g * fine[c, pl.ds(EDGE - 2 + k, rows, stride=2), :], axis=0, keepdims=True
            )


def fine_kernel(grad, w, d_fine, wide):
    rows = d_fine.shape[0] // 2
    for c in range(wide.shape[0]):
        at = slice(c * LANES, (c + 1) * LANES)
        here = grad[EDGE : EDGE + rows, at]
        after = grad[EDGE + 1 : EDGE + 1 + rows, at]
        before = grad[EDGE - 1 : EDGE - 1 + rows, at]
        wide[c, pl.ds(0, rows, stride=2), :] = w[0:1, at] * after + w[2:3, at] * here + w[4:5, at] * before
        wide[c, pl.ds(1, rows, stride=2), :] = w[1:2, at] * after + w[3:4, at] * here
        d_fine[:, at] = wide[c].astype(d_fine.dtype)


def swap(value, axis, mask):
    return lax.ppermute(value, axis, [(i, i ^ mask) for i in range(lax.axis_size(axis))])


def body(queries, keys, values, features_fine, rc_state, conv_weight):
    count = lax.axis_size("ctx")
    q, f, rc = queries[0], features_fine[0], rc_state[0]
    rows, chans = rc.shape
    qw = q.shape[1]
    here = lax.axis_index("ctx")
    edge = jnp.stack([here, jnp.full_like(here, count)]).astype(jnp.int32)

    own = jnp.concatenate([keys[0], values[0].T], axis=0)
    if count <= 8:
        got = [own] + [swap(own, "ctx", m) for m in range(2, count, 2)]
        blocks = got + [swap(b, "ctx", 1) for b in got]
    else:
        gathered = lax.all_gather(own, "ctx")
        blocks = [gathered[i] for i in range(count)]

    q_pad = ((0, 0), (0, chans - qw))
    zero = jnp.zeros((2, chans), rc.dtype)
    to_up = jnp.concatenate([rc[-1:], jnp.pad(q[-1:], q_pad), zero, f[-4:]], axis=0)
    to_down = jnp.concatenate([f[:4], rc[:1], jnp.pad(q[:1], q_pad), zero], axis=0)
    up = lax.ppermute(to_up, "ctx", [(i, i + 1) for i in range(count - 1)])
    down = lax.ppermute(to_down, "ctx", [(i + 1, i) for i in range(count - 1)])
    across = [(i, count - 1 - i) for i in range(count)]
    mirrored = lax.ppermute(rc, "ctx", across)
    mirrored_edge = lax.ppermute(jnp.concatenate([down[4:5], up[0:1]], axis=0), "ctx", across)

    n = len(blocks)
    dv = values.shape[2]
    wide = pl.cdiv(dv, 128) * 128
    vmem = pl.BlockSpec(memory_space=pltpu.VMEM)
    base, base_edge, fine = pl.pallas_call(
        lambda *refs: attend_kernel(*refs, blocks=n),
        name="attend",
        out_shape=(
            jax.ShapeDtypeStruct((rows, chans), jnp.float32),
            jax.ShapeDtypeStruct((EDGE, chans), jnp.float32),
            jax.ShapeDtypeStruct((chans // LANES, 2 * rows + 2 * EDGE, LANES), jnp.float32),
        ),
        in_specs=[pl.BlockSpec(memory_space=pltpu.SMEM)] + [vmem] * (5 + n),
        out_specs=(vmem, vmem, vmem),
        scratch_shapes=[
            pltpu.VMEM((n * rows, keys.shape[2]), jnp.bfloat16),
            pltpu.VMEM((wide, n * rows), jnp.bfloat16),
            pltpu.VMEM((wide, n * rows), jnp.bfloat16),
            pltpu.VMEM((rows + 16, chans), jnp.float32),
        ],
    )(edge, q, up, down, f, conv_weight, *blocks)

    partial, grad = pl.pallas_call(
        grad_kernel,
        name="grad",
        out_shape=(
            jax.ShapeDtypeStruct((KW, chans), jnp.float32),
            jax.ShapeDtypeStruct((rows + 2 * EDGE, chans), jnp.float32),
        ),
        in_specs=[vmem] * 5,
        out_specs=(vmem, vmem),
    )(base, base_edge, fine, mirrored, mirrored_edge)

    d_fine = pl.pallas_call(
        fine_kernel,
        name="fine",
        out_shape=jax.ShapeDtypeStruct((2 * rows, chans), jnp.bfloat16),
        in_specs=[vmem] * 2,
        out_specs=vmem,
        scratch_shapes=[pltpu.VMEM((chans // LANES, 2 * rows, LANES), jnp.float32)],
    )(grad, conv_weight)

    total = partial
    for axis in ("dp", "ctx"):
        mask = 1
        while mask < lax.axis_size(axis):
            total = total + swap(total, axis, mask)
            mask *= 2
    scale = 1.0 / math.sqrt(lax.axis_size("dp") * rows * count)
    return (d_fine[None], total * scale)


def solution(mesh):
    placed = (
        P("dp", "ctx", None),
        P("dp", "ctx", None),
        P("dp", "ctx", None),
        P("dp", "ctx", None),
        P("dp", "ctx", None),
        P(),
    )
    return jax.shard_map(
        body, mesh=mesh, in_specs=placed, out_specs=(P("dp", "ctx", None), P()), check_vma=False
    )
```

time: 150 us -> 77.4 us (0.52)
  blocking collectives: 103 us -> 0 us
  waiting for transfers between devices: 8.83 us -> 27.9 us
  starting transfers between devices: 15.1 us -> 29.1 us
  Pallas kernels: 0 us -> 12.5 us
  local copies, waits for them, and re-layouts: 14.4 us -> 3.66 us
  matrix products: 1.88 us -> 0 us
    all_gather x2 -> x0, blocking collectives: 66 us -> none  [the longest x1 35.2 us: body(): key_piece = lax.all_gather(keys, 'ctx', axis=1, tiled=True)]
    psum x1 -> x0, blocking collectives: 37.4 us -> none  [body(): summed = lax.psum(partial_grad, ('dp', 'ctx'))]
    ppermute x7 -> x16, waiting for transfers between devices: 8.83 us -> 27.9 us  [the longest x12 27.9 us: swap(): lax.ppermute(value, axis, [(i, i ^ mask) for i in range(lax.axis_size(axi...]
    ppermute x7 -> x16, starting transfers between devices: 15.1 us -> 29.1 us  [the longest x12 16.5 us: swap(): lax.ppermute(value, axis, [(i, i ^ mask) for i in range(lax.axis_size(axi...]
    pallas_call x0 -> x3, Pallas kernels: none -> 12.5 us  [the longest x1 6.54 us: body(): pl.pallas_call(lambda *refs: attend_kernel(*refs, blocks=n), name='attend...]
    rev x1 -> x0, local copies, waits for them, and re-layouts: 4.74 us -> none  [body(): grad = coarse + attended - mirrored[:, ::-1, :].astype(jnp.float32)]
    slice x8 -> x5, local copies, waits for them, and re-layouts: 6.36 us -> 2.31 us  [the longest x1 0.77 us: body(): rc[:1]]
    reduce_sum x2 -> x0, other arithmetic: 2.74 us -> none  [the longest x1 1.82 us: body(): jnp.sum(grad * taps[k], axis=(0, 1))]
  transfers between devices with their start and end apart: 7 -> 16, of which waited for: 2 -> 9; matrix products, arithmetic and copies ran while one was open for 7% -> 2% of each run, Pallas kernels for 0% -> 12%
where the time goes in v1:
time: 77.4 us; the launch traced here: 76.9 us
  starting transfers between devices  29.1 us (38%)
  waiting for transfers between devices  27.9 us (36%)
  Pallas kernels  12.5 us (16%)
  local copies, waits for them, and re-layouts  3.66 us (5%)
  other arithmetic  2.93 us (4%)
  between operations  0.79 us (1%)
    ppermute x12, waiting for transfers between devices, swap(): lax.ppermute(value, axis, [(i, i ^ mask) for i in range(lax.axis_size(axi...  27.9 us
    ppermute x12, starting transfers between devices, swap(): lax.ppermute(value, axis, [(i, i ^ mask) for i in range(lax.axis_size(axi...  16.5 us
    pallas_call x1, Pallas kernels, body(): pl.pallas_call(lambda *refs: attend_kernel(*refs, blocks=n), name='attend...  6.54 us
    ppermute x1, starting transfers between devices, body(): up = lax.ppermute(to_up, 'ctx', [(i, i + 1) for i in range(count - 1)])  5.53 us
    pallas_call x1, Pallas kernels, body(): pl.pallas_call(grad_kernel, name='grad', out_shape=(jax.ShapeDtypeStruct(...  3.29 us
    ppermute x1, starting transfers between devices, body(): mirrored = lax.ppermute(rc, 'ctx', across)  2.98 us
    ppermute x1, starting transfers between devices, body(): lax.ppermute(jnp.concatenate([down[4:5], up[0:1]], axis=0), 'ctx', across)  2.79 us
    pallas_call x1, Pallas kernels, body(): pl.pallas_call(fine_kernel, name='fine', out_shape=jax.ShapeDtypeStruct((...  2.63 us
  transfers between devices with their start and end apart: 16, of which 9 were waited for; matrix products, arithmetic and copies ran while one was open for 2% of the time, Pallas kernels for 12%

profile of v1, /device:TPU:0, one launch (start us, length us, event | category | flops | bytes accessed | tf_op | source)
XLA Modules:
  0.0 76.9 jit_solution(4882875386147354435)
XLA Ops:
  0.6 0.7 slice_bitcast_fusion.4
  1.4 0.8 %slice_bitcast_fusion.2 = (bf16[1,1536]{1,0:T(2,128)(2,1)S(1)}, bf16[1,1536]{1,0:T(2,128)(2,1)S(1)}) fusion(bf16[1,128,1536]{2,1,0:T(8,128)(2,1)} %param.10), kind=kLoop, calls=%fused_computation.18 | loop fusion | bytes 12288 | tf_op jit(solution)/shard_map/slice | solution.py:130
  2.2 0.8 %slice_bitcast_fusion = (bf16[4,1536]{1,0:T(4,128)(2,1)S(1)}, bf16[4,1536]{1,0:T(4,128)(2,1)S(1)}) fusion(bf16[1,256,1536]{2,1,0:T(8,128)(2,1)} %param.9), kind=kLoop, calls=%fused_computation.15 | loop fusion | bytes 49152 | tf_op jit(solution)/shard_map/slice | solution.py:130
  2.9 0.1 fusion.5
  3.0 1.3 %collective-permute-start.1 = (bf16[8,1536]{1,0:T(8,128)(2,1)S(1)}, bf16[8,1536]{1,0:T(8,128)(2,1)S(1)}, u32[]{:S(2)}, u32[]{:S(2)}) collective-permute-start(bf16[8,1536]{1,0:T(8,128)(2,1)S(1)} %get-tuple-element.18), channel_id=1, source_target_pairs={{1,0},{2,1},{3,2},{4,3},{5,4},{6,5},{7,6},{9,8},{10,9},{11,10},{12... | collective-permute-start | bytes 73736 | tf_op jit(solution)/shard_map/ppermute | solution.py:132
  4.3 5.5 %collective-permute-start = (bf16[8,1536]{1,0:T(8,128)(2,1)S(1)}, bf16[8,1536]{1,0:T(8,128)(2,1)S(1)}, u32[]{:S(2)}, u32[]{:S(2)}) collective-permute-start(bf16[8,1536]{1,0:T(8,128)(2,1)S(1)} %get-tuple-element.19), channel_id=1, source_target_pairs={{0,1},{1,2},{2,3},{3,4},{4,5},{5,6},{6,7},{8,9},{9,10},{10,11},{11... | collective-permute-start | bytes 73736 | tf_op jit(solution)/shard_map/ppermute | solution.py:131
  9.9 3.0 %collective-permute-start.9 = (bf16[128,1536]{1,0:T(8,128)(2,1)}, bf16[128,1536]{1,0:T(8,128)(2,1)S(1)}, u32[]{:S(2)}, u32[]{:S(2)}) collective-permute-start(bf16[128,1536]{1,0:T(8,128)(2,1)} %bitcast.26), channel_id=1, source_target_pairs={{0,7},{1,6},{2,5},{3,4},{4,3},{5,2},{6,1},{7,0},{8,15},{9,14},{10,... | collective-permute-start | bytes 1179656 | tf_op jit(solution)/shard_map/ppermute | solution.py:134
  12.8 0.8 %pad_maximum_fusion.refs_6_ = bf16[320,128]{1,0:T(8,128)(2,1)S(1)} fusion(bf16[192,128]{1,0:T(8,128)(2,1)} %bitcast.24, bf16[128,128]{1,0:T(8,128)(2,1)} %bitcast.25), kind=kLoop, calls=%fused_computation | loop fusion | flops 163840 | bytes 163840 | tf_op jit(solution)/shard_map/concatenate | solution.py:119
  13.6 0.0 copy-start.1
  13.6 2.7 %collective-permute-start.5 = (bf16[320,128]{1,0:T(8,128)(2,1)S(1)}, bf16[320,128]{1,0:T(8,128)(2,1)S(1)}, u32[]{:S(2)}, u32[]{:S(2)}) collective-permute-start(bf16[320,128]{1,0:T(8,128)(2,1)S(1)} %pad_maximum_fusion.refs_6_), channel_id=1, source_target_pairs={{0,1},{1,0},{2,3},{3,2},{4,5},{5,4},{6,7},{7,6},{8,9},{9,8},{10,11... | collective-permute-start | bytes 245768 | tf_op jit(solution)/shard_map/ppermute | solution.py:108
  16.4 0.7 collective-permute-start.4
  17.0 0.0 collective-permute-done.1.refs_3_
  17.1 0.0 copy-start.9
  17.1 0.8 %collective-permute-start.3 = (bf16[320,128]{1,0:T(8,128)(2,1)S(1)}, bf16[320,128]{1,0:T(8,128)(2,1)S(1)}, u32[]{:S(2)}, u32[]{:S(2)}) collective-permute-start(bf16[320,128]{1,0:T(8,128)(2,1)S(1)} %pad_maximum_fusion.refs_6_), channel_id=1, source_target_pairs={{0,4},{1,5},{2,6},{3,7},{4,0},{5,1},{6,2},{7,3},{8,12},{9,13},{10,... | collective-permute-start | bytes 245768 | tf_op jit(solution)/shard_map/ppermute | solution.py:108
  17.9 0.0 collective-permute-done.refs_2_
  17.9 0.0 copy-start.10
  17.9 3.0 %collective-permute-start.2 = (bf16[320,128]{1,0:T(8,128)(2,1)S(1)}, bf16[320,128]{1,0:T(8,128)(2,1)S(1)}, u32[]{:S(2)}, u32[]{:S(2)}) collective-permute-start(bf16[320,128]{1,0:T(8,128)(2,1)S(1)} %pad_maximum_fusion.refs_6_), channel_id=1, source_target_pairs={{0,2},{1,3},{2,0},{3,1},{4,6},{5,7},{6,4},{7,5},{8,10},{9,11},{10,... | collective-permute-start | bytes 245768 | tf_op jit(solution)/shard_map/ppermute | solution.py:108
  20.9 4.4 %collective-permute-done.5.refs_10_ = bf16[320,128]{1,0:T(8,128)(2,1)S(1)} collective-permute-done((bf16[320,128]{1,0:T(8,128)(2,1)S(1)}, bf16[320,128]{1,0:T(8,128)(2,1)S(1)}, u32[]{:S(2)}, u32[]{:S(2)}) %collective-permute-start.5) | collective-permute-done | bytes 81952 | tf_op jit(solution)/shard_map/ppermute | solution.py:108
  25.3 0.0 copy-start.2
  25.3 2.8 %collective-permute-start.10 = (bf16[2,1536]{1,0:T(2,128)(2,1)S(1)}, bf16[2,1536]{1,0:T(2,128)(2,1)S(1)}, u32[]{:S(2)}, u32[]{:S(2)}) collective-permute-start(bf16[2,1536]{1,0:T(2,128)(2,1)S(1)} %pad_maximum_fusion.1), channel_id=1, source_target_pairs={{0,7},{1,6},{2,5},{3,4},{4,3},{5,2},{6,1},{7,0},{8,15},{9,14},{10,... | collective-permute-start | bytes 18440 | tf_op jit(solution)/shard_map/ppermute | solution.py:135
  28.1 0.0 collective-permute-done.4.refs_9_
  28.1 0.0 copy-start.3
  28.1 1.8 %collective-permute-start.8 = (bf16[320,128]{1,0:T(8,128)(2,1)S(1)}, bf16[320,128]{1,0:T(8,128)(2,1)S(1)}, u32[]{:S(2)}, u32[]{:S(2)}) collective-permute-start(bf16[320,128]{1,0:T(8,128)(2,1)S(1)} %collective-permute-done.4.refs_9_), channel_id=1, source_target_pairs={{0,1},{1,0},{2,3},{3,2},{4,5},{5,4},{6,7},{7,6},{8,9},{9,8},{10,11... | collective-permute-start | bytes 245768 | tf_op jit(solution)/shard_map/ppermute | solution.py:108
  29.9 9.5 %collective-permute-done.3.refs_8_ = bf16[320,128]{1,0:T(8,128)(2,1)S(1)} collective-permute-done((bf16[320,128]{1,0:T(8,128)(2,1)S(1)}, bf16[320,128]{1,0:T(8,128)(2,1)S(1)}, u32[]{:S(2)}, u32[]{:S(2)}) %collective-permute-start.3) | collective-permute-done | bytes 81952 | tf_op jit(solution)/shard_map/ppermute | solution.py:108
  39.4 0.0 copy-start.4
  39.4 0.2 collective-permute-start.7
  39.6 0.0 collective-permute-done.2.refs_7_
  39.6 0.0 copy-start.5
  39.6 1.9 %collective-permute-start.6 = (bf16[320,128]{1,0:T(8,128)(2,1)S(1)}, bf16[320,128]{1,0:T(8,128)(2,1)S(1)}, u32[]{:S(2)}, u32[]{:S(2)}) collective-permute-start(bf16[320,128]{1,0:T(8,128)(2,1)S(1)} %collective-permute-done.2.refs_7_), channel_id=1, source_target_pairs={{0,1},{1,0},{2,3},{3,2},{4,5},{5,4},{6,7},{7,6},{8,9},{9,8},{10,11... | collective-permute-start | bytes 245768 | tf_op jit(solution)/shard_map/ppermute | solution.py:108
  41.5 0.6 pad_add_fusion.refs_0_
  42.0 0.0 collective-permute-done.8.refs_13_
  42.0 0.0 copy-start.6
  42.0 1.8 %collective-permute-done.7.refs_12_ = bf16[320,128]{1,0:T(8,128)(2,1)S(1)} collective-permute-done((bf16[320,128]{1,0:T(8,128)(2,1)S(1)}, bf16[320,128]{1,0:T(8,128)(2,1)S(1)}, u32[]{:S(2)}, u32[]{:S(2)}) %collective-permute-start.7) | collective-permute-done | bytes 81952 | tf_op jit(solution)/shard_map/ppermute | solution.py:108
  43.9 0.9 %collective-permute-done.6.refs_11_ = bf16[320,128]{1,0:T(8,128)(2,1)S(1)} collective-permute-done((bf16[320,128]{1,0:T(8,128)(2,1)S(1)}, bf16[320,128]{1,0:T(8,128)(2,1)S(1)}, u32[]{:S(2)}, u32[]{:S(2)}) %collective-permute-start.6) | collective-permute-done | bytes 81952 | tf_op jit(solution)/shard_map/ppermute | solution.py:108
  44.8 0.0 copy-done.1
  44.8 0.0 copy-done.9
  44.8 0.0 copy-done.10
  44.8 0.0 copy-done.2
  44.8 0.0 copy-done.3
  44.8 0.0 copy-done.4
  44.8 0.0 copy-done.5
  44.8 0.0 copy-done.6
  44.8 0.0 copy-done.7
  44.8 0.6 copy-done.8
  45.4 6.5 %attend.1 = (f32[128,1536]{1,0:T(8,128)}, f32[8,1536]{1,0:T(8,128)}, f32[12,272,128]{2,1,0:T(8,128)}) custom-call(s32[2]{0:T(128)} %pad_add_fusion.refs_0_, bf16[128,1024]{1,0:T(8,128)(2,1)} %bitcast.23, bf16[8,1536]{1,0:T(8,128)(2,1)} %copy-done.10, bf16[8,1536]{1,0:T(8,128)(2,1)} %copy-done.9, bf16[256,1536]{1,0:T(8,128)(2,1)} %bitcast.21, f32[5,1536]{1,0:T(8,128)} %w.1, ...), custom_call_target="tpu_custom_call" | custom-call | tf_op jit(solution)/shard_map/attend/pallas_call | solution.py:141
  51.9 0.0 collective-permute-done.10.rc_edge
  51.9 0.0 collective-permute-done.9.rc
  51.9 0.0 copy-start
  51.9 0.6 copy-done.11
  52.5 0.2 copy-done
  52.7 3.3 %grad.1 = (f32[5,1536]{1,0:T(8,128)}, f32[144,1536]{1,0:T(8,128)}) custom-call(f32[128,1536]{1,0:T(8,128)} %get-tuple-element.7.base, f32[8,1536]{1,0:T(8,128)} %get-tuple-element.8.base_edge, f32[12,272,128]{2,1,0:T(8,128)} %get-tuple-element.9.fine, bf16[128,1536]{1,0:T(8,128)(2,1)} %copy-done, bf16[2,1536]{1,0:T(2,128)(2,1)} %copy-done.11), custom_call_target="tpu_custom_call" | custom-call | tf_op jit(solution)/shard_map/grad/pallas_call | solution.py:159
  56.0 0.0 collective-permute-start.11
  56.0 1.4 %collective-permute-done.11 = f32[5,1536]{1,0:T(8,128)S(1)} collective-permute-done((f32[5,1536]{1,0:T(8,128)}, f32[5,1536]{1,0:T(8,128)S(1)}, u32[]{:S(2)}, u32[]{:S(2)}) %collective-permute-start.11) | collective-permute-done | bytes 30752 | tf_op jit(solution)/shard_map/ppermute | solution.py:108
  57.4 0.8 %add.19 = f32[5,1536]{1,0:T(8,128)S(1)} add(f32[5,1536]{1,0:T(8,128)} %get-tuple-element.11, f32[5,1536]{1,0:T(8,128)S(1)} %collective-permute-done.11) | non-fusion elementwise | flops 7680 | bytes 92160 | tf_op jit(solution)/shard_map/add | solution.py:183
  58.2 1.5 %collective-permute-start.12 = (f32[5,1536]{1,0:T(8,128)S(1)}, f32[5,1536]{1,0:T(8,128)S(1)}, u32[]{:S(2)}, u32[]{:S(2)}) collective-permute-start(f32[5,1536]{1,0:T(8,128)S(1)} %add.19), channel_id=1, source_target_pairs={{0,16},{8,24},{16,0},{24,8},{1,17},{9,25},{17,1},{25,9},{2,18},{10... | collective-permute-start | bytes 92168 | tf_op jit(solution)/shard_map/ppermute | solution.py:108
  59.7 2.6 %collective-permute-done.12 = f32[5,1536]{1,0:T(8,128)S(1)} collective-permute-done((f32[5,1536]{1,0:T(8,128)S(1)}, f32[5,1536]{1,0:T(8,128)S(1)}, u32[]{:S(2)}, u32[]{:S(2)}) %collective-permute-start.12) | collective-permute-done | bytes 30752 | tf_op jit(solution)/shard_map/ppermute | solution.py:108
  62.3 1.2 %collective-permute-start.13 = (f32[5,1536]{1,0:T(8,128)S(1)}, f32[5,1536]{1,0:T(8,128)S(1)}, u32[]{:S(2)}, u32[]{:S(2)}) collective-permute-start(f32[5,1536]{1,0:T(8,128)S(1)} %add.20), channel_id=1, source_target_pairs={{0,1},{1,0},{2,3},{3,2},{4,5},{5,4},{6,7},{7,6},{8,9},{9,8},{10,11... | collective-permute-start | bytes 92168 | tf_op jit(solution)/shard_map/ppermute | solution.py:108
  63.5 2.9 %collective-permute-done.13 = f32[5,1536]{1,0:T(8,128)S(1)} collective-permute-done((f32[5,1536]{1,0:T(8,128)S(1)}, f32[5,1536]{1,0:T(8,128)S(1)}, u32[]{:S(2)}, u32[]{:S(2)}) %collective-permute-start.13) | collective-permute-done | bytes 30752 | tf_op jit(solution)/shard_map/ppermute | solution.py:108
  66.5 0.8 %collective-permute-start.14 = (f32[5,1536]{1,0:T(8,128)S(1)}, f32[5,1536]{1,0:T(8,128)S(1)}, u32[]{:S(2)}, u32[]{:S(2)}) collective-permute-start(f32[5,1536]{1,0:T(8,128)S(1)} %add.21), channel_id=1, source_target_pairs={{0,2},{1,3},{2,0},{3,1},{4,6},{5,7},{6,4},{7,5},{8,10},{9,11},{10,... | collective-permute-start | bytes 92168 | tf_op jit(solution)/shard_map/ppermute | solution.py:108
  67.3 3.3 %collective-permute-done.14 = f32[5,1536]{1,0:T(8,128)S(1)} collective-permute-done((f32[5,1536]{1,0:T(8,128)S(1)}, f32[5,1536]{1,0:T(8,128)S(1)}, u32[]{:S(2)}, u32[]{:S(2)}) %collective-permute-start.14) | collective-permute-done | bytes 30752 | tf_op jit(solution)/shard_map/ppermute | solution.py:108
  70.7 1.9 %collective-permute-start.15 = (f32[5,1536]{1,0:T(8,128)S(1)}, f32[5,1536]{1,0:T(8,128)S(1)}, u32[]{:S(2)}, u32[]{:S(2)}) collective-permute-start(f32[5,1536]{1,0:T(8,128)S(1)} %add.22), channel_id=1, source_target_pairs={{0,4},{1,5},{2,6},{3,7},{4,0},{5,1},{6,2},{7,3},{8,12},{9,13},{10,... | collective-permute-start | bytes 92168 | tf_op jit(solution)/shard_map/ppermute | solution.py:108
  72.6 2.6 %fine.1 = bf16[256,1536]{1,0:T(8,128)(2,1)} custom-call(f32[144,1536]{1,0:T(8,128)} %get-tuple-element.10.grad, f32[5,1536]{1,0:T(8,128)} %w.1), custom_call_target="tpu_custom_call" | custom-call | tf_op jit(solution)/shard_map/fine/pallas_call | solution.py:170
  75.2 1.0 %collective-permute-done.15 = f32[5,1536]{1,0:T(8,128)S(1)} collective-permute-done((f32[5,1536]{1,0:T(8,128)S(1)}, f32[5,1536]{1,0:T(8,128)S(1)}, u32[]{:S(2)}, u32[]{:S(2)}) %collective-permute-start.15) | collective-permute-done | bytes 30752 | tf_op jit(solution)/shard_map/ppermute | solution.py:108
  76.2 0.6 add_multiply_fusion
  (10 shorter events, 0.1 us)
Async XLA Ops:
  3.0 14.0 %collective-permute-start.1 = (bf16[8,1536]{1,0:T(8,128)(2,1)S(1)}, bf16[8,1536]{1,0:T(8,128)(2,1)S(1)}, u32[]{:S(2)}, u32[]{:S(2)}) collective-permute-start(bf16[8,1536]{1,0:T(8,128)(2,1)S(1)} %get-tuple-element.18), channel_id=1, source_target_pairs={{1,0},{2,1},{3,2},{4,3},{5,4},{6,5},{7,6},{9,8},{10,9},{11,10},{12... | collective-permute-start | bytes 73736 | tf_op jit(solution)/shard_map/ppermute | solution.py:132
  4.3 13.5 %collective-permute-start = (bf16[8,1536]{1,0:T(8,128)(2,1)S(1)}, bf16[8,1536]{1,0:T(8,128)(2,1)S(1)}, u32[]{:S(2)}, u32[]{:S(2)}) collective-permute-start(bf16[8,1536]{1,0:T(8,128)(2,1)S(1)} %get-tuple-element.19), channel_id=1, source_target_pairs={{0,1},{1,2},{2,3},{3,4},{4,5},{5,6},{6,7},{8,9},{9,10},{10,11},{11... | collective-permute-start | bytes 73736 | tf_op jit(solution)/shard_map/ppermute | solution.py:131
  9.9 42.1 %collective-permute-start.9 = (bf16[128,1536]{1,0:T(8,128)(2,1)}, bf16[128,1536]{1,0:T(8,128)(2,1)S(1)}, u32[]{:S(2)}, u32[]{:S(2)}) collective-permute-start(bf16[128,1536]{1,0:T(8,128)(2,1)} %bitcast.26), channel_id=1, source_target_pairs={{0,7},{1,6},{2,5},{3,4},{4,3},{5,2},{6,1},{7,0},{8,15},{9,14},{10,... | collective-permute-start | bytes 1179656 | tf_op jit(solution)/shard_map/ppermute | solution.py:134
  13.6 31.1 %copy-start.1 = (bf16[320,128]{1,0:T(8,128)(2,1)}, bf16[320,128]{1,0:T(8,128)(2,1)S(1)}, u32[]{:S(2)}) copy-start(bf16[320,128]{1,0:T(8,128)(2,1)S(1)} %pad_maximum_fusion.refs_6_) | copy-start | bytes 245764
  13.6 11.6 %collective-permute-start.5 = (bf16[320,128]{1,0:T(8,128)(2,1)S(1)}, bf16[320,128]{1,0:T(8,128)(2,1)S(1)}, u32[]{:S(2)}, u32[]{:S(2)}) collective-permute-start(bf16[320,128]{1,0:T(8,128)(2,1)S(1)} %pad_maximum_fusion.refs_6_), channel_id=1, source_target_pairs={{0,1},{1,0},{2,3},{3,2},{4,5},{5,4},{6,7},{7,6},{8,9},{9,8},{10,11... | collective-permute-start | bytes 245768 | tf_op jit(solution)/shard_map/ppermute | solution.py:108
  16.4 11.8 %collective-permute-start.4 = (bf16[320,128]{1,0:T(8,128)(2,1)S(1)}, bf16[320,128]{1,0:T(8,128)(2,1)S(1)}, u32[]{:S(2)}, u32[]{:S(2)}) collective-permute-start(bf16[320,128]{1,0:T(8,128)(2,1)S(1)} %pad_maximum_fusion.refs_6_), channel_id=1, source_target_pairs={{0,6},{1,7},{2,4},{3,5},{4,2},{5,3},{6,0},{7,1},{8,14},{9,15},{10,... | collective-permute-start | bytes 245768 | tf_op jit(solution)/shard_map/ppermute | solution.py:108
  17.1 27.7 %copy-start.9 = (bf16[8,1536]{1,0:T(8,128)(2,1)}, bf16[8,1536]{1,0:T(8,128)(2,1)S(1)}, u32[]{:S(2)}) copy-start(bf16[8,1536]{1,0:T(8,128)(2,1)S(1)} %collective-permute-done.1.refs_3_) | copy-start | bytes 73732
  17.1 22.4 %collective-permute-start.3 = (bf16[320,128]{1,0:T(8,128)(2,1)S(1)}, bf16[320,128]{1,0:T(8,128)(2,1)S(1)}, u32[]{:S(2)}, u32[]{:S(2)}) collective-permute-start(bf16[320,128]{1,0:T(8,128)(2,1)S(1)} %pad_maximum_fusion.refs_6_), channel_id=1, source_target_pairs={{0,4},{1,5},{2,6},{3,7},{4,0},{5,1},{6,2},{7,3},{8,12},{9,13},{10,... | collective-permute-start | bytes 245768 | tf_op jit(solution)/shard_map/ppermute | solution.py:108
  17.9 26.9 %copy-start.10 = (bf16[8,1536]{1,0:T(8,128)(2,1)}, bf16[8,1536]{1,0:T(8,128)(2,1)S(1)}, u32[]{:S(2)}) copy-start(bf16[8,1536]{1,0:T(8,128)(2,1)S(1)} %collective-permute-done.refs_2_) | copy-start | bytes 73732
  17.9 21.7 %collective-permute-start.2 = (bf16[320,128]{1,0:T(8,128)(2,1)S(1)}, bf16[320,128]{1,0:T(8,128)(2,1)S(1)}, u32[]{:S(2)}, u32[]{:S(2)}) collective-permute-start(bf16[320,128]{1,0:T(8,128)(2,1)S(1)} %pad_maximum_fusion.refs_6_), channel_id=1, source_target_pairs={{0,2},{1,3},{2,0},{3,1},{4,6},{5,7},{6,4},{7,5},{8,10},{9,11},{10,... | collective-permute-start | bytes 245768 | tf_op jit(solution)/shard_map/ppermute | solution.py:108
  25.3 19.5 %copy-start.2 = (bf16[320,128]{1,0:T(8,128)(2,1)}, bf16[320,128]{1,0:T(8,128)(2,1)S(1)}, u32[]{:S(2)}) copy-start(bf16[320,128]{1,0:T(8,128)(2,1)S(1)} %collective-permute-done.5.refs_10_) | copy-start | bytes 245764
  25.3 26.6 %collective-permute-start.10 = (bf16[2,1536]{1,0:T(2,128)(2,1)S(1)}, bf16[2,1536]{1,0:T(2,128)(2,1)S(1)}, u32[]{:S(2)}, u32[]{:S(2)}) collective-permute-start(bf16[2,1536]{1,0:T(2,128)(2,1)S(1)} %pad_maximum_fusion.1), channel_id=1, source_target_pairs={{0,7},{1,6},{2,5},{3,4},{4,3},{5,2},{6,1},{7,0},{8,15},{9,14},{10,... | collective-permute-start | bytes 18440 | tf_op jit(solution)/shard_map/ppermute | solution.py:135
  28.1 16.7 %copy-start.3 = (bf16[320,128]{1,0:T(8,128)(2,1)}, bf16[320,128]{1,0:T(8,128)(2,1)S(1)}, u32[]{:S(2)}) copy-start(bf16[320,128]{1,0:T(8,128)(2,1)S(1)} %collective-permute-done.4.refs_9_) | copy-start | bytes 245764
  28.1 13.9 %collective-permute-start.8 = (bf16[320,128]{1,0:T(8,128)(2,1)S(1)}, bf16[320,128]{1,0:T(8,128)(2,1)S(1)}, u32[]{:S(2)}, u32[]{:S(2)}) collective-permute-start(bf16[320,128]{1,0:T(8,128)(2,1)S(1)} %collective-permute-done.4.refs_9_), channel_id=1, source_target_pairs={{0,1},{1,0},{2,3},{3,2},{4,5},{5,4},{6,7},{7,6},{8,9},{9,8},{10,11... | collective-permute-start | bytes 245768 | tf_op jit(solution)/shard_map/ppermute | solution.py:108
  39.4 5.4 %copy-start.4 = (bf16[320,128]{1,0:T(8,128)(2,1)}, bf16[320,128]{1,0:T(8,128)(2,1)S(1)}, u32[]{:S(2)}) copy-start(bf16[320,128]{1,0:T(8,128)(2,1)S(1)} %collective-permute-done.3.refs_8_) | copy-start | bytes 245764
  39.4 4.4 %collective-permute-start.7 = (bf16[320,128]{1,0:T(8,128)(2,1)S(1)}, bf16[320,128]{1,0:T(8,128)(2,1)S(1)}, u32[]{:S(2)}, u32[]{:S(2)}) collective-permute-start(bf16[320,128]{1,0:T(8,128)(2,1)S(1)} %collective-permute-done.3.refs_8_), channel_id=1, source_target_pairs={{0,1},{1,0},{2,3},{3,2},{4,5},{5,4},{6,7},{7,6},{8,9},{9,8},{10,11... | collective-permute-start | bytes 245768 | tf_op jit(solution)/shard_map/ppermute | solution.py:108
  39.6 5.2 %copy-start.5 = (bf16[320,128]{1,0:T(8,128)(2,1)}, bf16[320,128]{1,0:T(8,128)(2,1)S(1)}, u32[]{:S(2)}) copy-start(bf16[320,128]{1,0:T(8,128)(2,1)S(1)} %collective-permute-done.2.refs_7_) | copy-start | bytes 245764
  39.6 5.1 %collective-permute-start.6 = (bf16[320,128]{1,0:T(8,128)(2,1)S(1)}, bf16[320,128]{1,0:T(8,128)(2,1)S(1)}, u32[]{:S(2)}, u32[]{:S(2)}) collective-permute-start(bf16[320,128]{1,0:T(8,128)(2,1)S(1)} %collective-permute-done.2.refs_7_), channel_id=1, source_target_pairs={{0,1},{1,0},{2,3},{3,2},{4,5},{5,4},{6,7},{7,6},{8,9},{9,8},{10,11... | collective-permute-start | bytes 245768 | tf_op jit(solution)/shard_map/ppermute | solution.py:108
  42.0 2.8 %copy-start.6 = (bf16[320,128]{1,0:T(8,128)(2,1)}, bf16[320,128]{1,0:T(8,128)(2,1)S(1)}, u32[]{:S(2)}) copy-start(bf16[320,128]{1,0:T(8,128)(2,1)S(1)} %collective-permute-done.8.refs_13_) | copy-start | bytes 245764
  43.9 0.9 %copy-start.7 = (bf16[320,128]{1,0:T(8,128)(2,1)}, bf16[320,128]{1,0:T(8,128)(2,1)S(1)}, u32[]{:S(2)}) copy-start(bf16[320,128]{1,0:T(8,128)(2,1)S(1)} %collective-permute-done.7.refs_12_) | copy-start | bytes 245764
  44.8 0.6 copy-start.8
  51.9 0.6 copy-start.11
  51.9 0.8 copy-start
  56.0 1.4 %collective-permute-start.11 = (f32[5,1536]{1,0:T(8,128)}, f32[5,1536]{1,0:T(8,128)S(1)}, u32[]{:S(2)}, u32[]{:S(2)}) collective-permute-start(f32[5,1536]{1,0:T(8,128)} %get-tuple-element.11), channel_id=1, source_target_pairs={{0,8},{8,0},{16,24},{24,16},{1,9},{9,1},{17,25},{25,17},{2,10},{10... | collective-permute-start | bytes 92168 | tf_op jit(solution)/shard_map/ppermute | solution.py:108
  58.2 4.1 %collective-permute-start.12 = (f32[5,1536]{1,0:T(8,128)S(1)}, f32[5,1536]{1,0:T(8,128)S(1)}, u32[]{:S(2)}, u32[]{:S(2)}) collective-permute-start(f32[5,1536]{1,0:T(8,128)S(1)} %add.19), channel_id=1, source_target_pairs={{0,16},{8,24},{16,0},{24,8},{1,17},{9,25},{17,1},{25,9},{2,18},{10... | collective-permute-start | bytes 92168 | tf_op jit(solution)/shard_map/ppermute | solution.py:108
  62.3 4.2 %collective-permute-start.13 = (f32[5,1536]{1,0:T(8,128)S(1)}, f32[5,1536]{1,0:T(8,128)S(1)}, u32[]{:S(2)}, u32[]{:S(2)}) collective-permute-start(f32[5,1536]{1,0:T(8,128)S(1)} %add.20), channel_id=1, source_target_pairs={{0,1},{1,0},{2,3},{3,2},{4,5},{5,4},{6,7},{7,6},{8,9},{9,8},{10,11... | collective-permute-start | bytes 92168 | tf_op jit(solution)/shard_map/ppermute | solution.py:108
  66.5 4.2 %collective-permute-start.14 = (f32[5,1536]{1,0:T(8,128)S(1)}, f32[5,1536]{1,0:T(8,128)S(1)}, u32[]{:S(2)}, u32[]{:S(2)}) collective-permute-start(f32[5,1536]{1,0:T(8,128)S(1)} %add.21), channel_id=1, source_target_pairs={{0,2},{1,3},{2,0},{3,1},{4,6},{5,7},{6,4},{7,5},{8,10},{9,11},{10,... | collective-permute-start | bytes 92168 | tf_op jit(solution)/shard_map/ppermute | solution.py:108
  70.7 5.6 %collective-permute-start.15 = (f32[5,1536]{1,0:T(8,128)S(1)}, f32[5,1536]{1,0:T(8,128)S(1)}, u32[]{:S(2)}, u32[]{:S(2)}) collective-permute-start(f32[5,1536]{1,0:T(8,128)S(1)} %add.22), channel_id=1, source_target_pairs={{0,4},{1,5},{2,6},{3,7},{4,0},{5,1},{6,2},{7,3},{8,12},{9,13},{10,... | collective-permute-start | bytes 92168 | tf_op jit(solution)/shard_map/ppermute | solution.py:108

commit v2 on v1

--- a/solution.py
+++ b/solution.py
@@ -6,6 +6,7 @@
 from jax.experimental import pallas as pl
 from jax.experimental.pallas import tpu as pltpu
 from jax.sharding import PartitionSpec as P
+
 
 HEADS = 8
 KW = 5
@@ -74,31 +75,37 @@
         base_edge[1:2, at] = jnp.where(last, 0.0, right)
 
 
-def grad_kernel(base, base_edge, fine, rc, rc_edge, partial, grad):
+def grad_kernel(base, fine, rc_a, rc_b, partial, grad):
     rows = base.shape[0]
+    half = rows // 2
     flip = (
-        lax.broadcasted_iota(jnp.int32, (rows, rows), 0) + lax.broadcasted_iota(jnp.int32, (rows, rows), 1) == rows - 1
+        lax.broadcasted_iota(jnp.int32, (half, half), 0) + lax.broadcasted_iota(jnp.int32, (half, half), 1) == half - 1
     ).astype(jnp.bfloat16)
     for c in range(fine.shape[0]):
         at = slice(c * LANES, (c + 1) * LANES)
-        g = base[:, at] - jnp.dot(flip, rc[:, at], preferred_element_type=jnp.float32)
-        ends = base_edge[0:2, at] - rc_edge[:, at].astype(jnp.float32)
-        grad[EDGE : EDGE + rows, at] = g
-        grad[EDGE - 1 : EDGE, at] = ends[0:1]
-        grad[EDGE + rows : EDGE + rows + 1, at] = ends[1:2]
+        sums = [None] * KW
+        for low, rc in ((half, rc_a), (0, rc_b)):
+            g = base[low : low + half, at] - jnp.dot(flip, rc[:, at], preferred_element_type=jnp.float32)
+            grad[low : low + half, at] = g
+            for k in range(KW):
+                tap = fine[c, pl.ds(EDGE - 2 + k + 2 * low, half, stride=2), :]
+                term = jnp.sum((g * tap).reshape(half // 8, 8, LANES), axis=0)
+                sums[k] = term if sums[k] is None else sums[k] + term
         for k in range(KW):
-            partial[k : k + 1, at] = jnp.sum(
-                g * fine[c, pl.ds(EDGE - 2 + k, rows, stride=2), :], axis=0, keepdims=True
-            )
-
-
-def fine_kernel(grad, w, d_fine, wide):
+            partial[k : k + 1, at] = jnp.sum(sums[k], axis=0, keepdims=True)
+
+
+def fine_kernel(grad, base_edge, rc_edge, w, d_fine, wide, padded):
     rows = d_fine.shape[0] // 2
     for c in range(wide.shape[0]):
         at = slice(c * LANES, (c + 1) * LANES)
-        here = grad[EDGE : EDGE + rows, at]
-        after = grad[EDGE + 1 : EDGE + 1 + rows, at]
-        before = grad[EDGE - 1 : EDGE - 1 + rows, at]
+        here = grad[:, at]
+        ends = base_edge[0:2, at] - rc_edge[:, at].astype(jnp.float32)
+        padded[EDGE : EDGE + rows] = here
+        padded[EDGE - 1 : EDGE] = ends[0:1]
+        padded[EDGE + rows : EDGE + rows + 1] = ends[1:2]
+        after = padded[EDGE + 1 : EDGE + 1 + rows]
+        before = padded[EDGE - 1 : EDGE - 1 + rows]
         wide[c, pl.ds(0, rows, stride=2), :] = w[0:1, at] * after + w[2:3, at] * here + w[4:5, at] * before
         wide[c, pl.ds(1, rows, stride=2), :] = w[1:2, at] * after + w[3:4, at] * here
         d_fine[:, at] = wide[c].astype(d_fine.dtype)
@@ -106,6 +113,10 @@
 
 def swap(value, axis, mask):
     return lax.ppermute(value, axis, [(i, i ^ mask) for i in range(lax.axis_size(axis))])
+
+
+def near(value):
+    return pltpu.with_memory_space_constraint(value, pltpu.VMEM)
 
 
 def body(queries, keys, values, features_fine, rc_state, conv_weight):
@@ -117,12 +128,23 @@
     edge = jnp.stack([here, jnp.full_like(here, count)]).astype(jnp.int32)
 
     own = jnp.concatenate([keys[0], values[0].T], axis=0)
-    if count <= 8:
-        got = [own] + [swap(own, "ctx", m) for m in range(2, count, 2)]
-        blocks = got + [swap(b, "ctx", 1) for b in got]
+    half = rows // 2
+    if count == 8:
+        k6 = swap(own, "ctx", 6)
+        k2 = swap(own, "ctx", 2)
+        k1 = swap(own, "ctx", 1)
+        k62 = swap(k6, "ctx", 2)
+        k61 = swap(k6, "ctx", 1)
+        k21 = swap(k2, "ctx", 1)
+        k621 = swap(k62, "ctx", 1)
+        blocks = [own, k6, k2, k1, k62, k61, k21, k621]
+        rc_a = swap(swap(rc[:half], "ctx", 6), "ctx", 1)
+        rc_b = swap(swap(rc[half:], "ctx", 1), "ctx", 6)
     else:
         gathered = lax.all_gather(own, "ctx")
         blocks = [gathered[i] for i in range(count)]
+        rc_a = swap(rc[:half], "ctx", count - 1)
+        rc_b = swap(rc[half:], "ctx", count - 1)
 
     q_pad = ((0, 0), (0, chans - qw))
     zero = jnp.zeros((2, chans), rc.dtype)
@@ -130,9 +152,7 @@
     to_down = jnp.concatenate([f[:4], rc[:1], jnp.pad(q[:1], q_pad), zero], axis=0)
     up = lax.ppermute(to_up, "ctx", [(i, i + 1) for i in range(count - 1)])
     down = lax.ppermute(to_down, "ctx", [(i + 1, i) for i in range(count - 1)])
-    across = [(i, count - 1 - i) for i in range(count)]
-    mirrored = lax.ppermute(rc, "ctx", across)
-    mirrored_edge = lax.ppermute(jnp.concatenate([down[4:5], up[0:1]], axis=0), "ctx", across)
+    rc_edge = swap(jnp.concatenate([down[4:5], up[0:1]], axis=0), "ctx", count - 1)
 
     n = len(blocks)
     dv = values.shape[2]
@@ -142,9 +162,9 @@
         lambda *refs: attend_kernel(*refs, blocks=n),
         name="attend",
         out_shape=(
-            jax.ShapeDtypeStruct((rows, chans), jnp.float32),
-            jax.ShapeDtypeStruct((EDGE, chans), jnp.float32),
-            jax.ShapeDtypeStruct((chans // LANES, 2 * rows + 2 * EDGE, LANES), jnp.float32),
+            pltpu.VMEM((rows, chans), jnp.float32),
+            pltpu.VMEM((EDGE, chans), jnp.float32),
+            pltpu.VMEM((chans // LANES, 2 * rows + 2 * EDGE, LANES), jnp.float32),
         ),
         in_specs=[pl.BlockSpec(memory_space=pltpu.SMEM)] + [vmem] * (5 + n),
         out_specs=(vmem, vmem, vmem),
@@ -154,27 +174,30 @@
             pltpu.VMEM((wide, n * rows), jnp.bfloat16),
             pltpu.VMEM((rows + 16, chans), jnp.float32),
         ],
-    )(edge, q, up, down, f, conv_weight, *blocks)
+        compiler_params=pltpu.CompilerParams(vmem_limit_bytes=24 << 20),
+    )(edge, q, near(up), near(down), f, conv_weight, *[near(b) for b in blocks])
 
     partial, grad = pl.pallas_call(
         grad_kernel,
         name="grad",
-        out_shape=(
-            jax.ShapeDtypeStruct((KW, chans), jnp.float32),
-            jax.ShapeDtypeStruct((rows + 2 * EDGE, chans), jnp.float32),
-        ),
-        in_specs=[vmem] * 5,
+        out_shape=(pltpu.VMEM((KW, chans), jnp.float32), pltpu.VMEM((rows, chans), jnp.float32)),
+        in_specs=[vmem] * 4,
         out_specs=(vmem, vmem),
-    )(base, base_edge, fine, mirrored, mirrored_edge)
+        compiler_params=pltpu.CompilerParams(vmem_limit_bytes=8 << 20),
+    )(near(base), near(fine), near(rc_a), near(rc_b))
 
     d_fine = pl.pallas_call(
         fine_kernel,
         name="fine",
         out_shape=jax.ShapeDtypeStruct((2 * rows, chans), jnp.bfloat16),
-        in_specs=[vmem] * 2,
+        in_specs=[vmem] * 4,
         out_specs=vmem,
-        scratch_shapes=[pltpu.VMEM((chans // LANES, 2 * rows, LANES), jnp.float32)],
-    )(grad, conv_weight)
+        scratch_shapes=[
+            pltpu.VMEM((chans // LANES, 2 * rows, LANES), jnp.float32),
+            pltpu.VMEM((rows + 2 * EDGE, LANES), jnp.float32),
+        ],
+        compiler_params=pltpu.CompilerParams(vmem_limit_bytes=8 << 20),
+    )(near(grad), near(base_edge), near(rc_edge), conv_weight)
 
     total = partial
     for axis in ("dp", "ctx"):
@@ -195,6 +218,5 @@
         P("dp", "ctx", None),
         P(),
     )
-    return jax.shard_map(
-        body, mesh=mesh, in_specs=placed, out_specs=(P("dp", "ctx", None), P()), check_vma=False
-    )
+
+    return jax.shard_map(body, mesh=mesh, in_specs=placed, out_specs=(P("dp", "ctx", None), P()), check_vma=False)

time: 77.4 us -> 65.3 us (0.84)
  Pallas kernels: 12.5 us -> 6.12 us
  waiting for transfers between devices: 27.9 us -> 22.9 us
  local copies, waits for them, and re-layouts: 3.66 us -> 5.12 us
  other arithmetic: 2.93 us -> 1.7 us
  starting transfers between devices: 29.1 us -> 28.3 us
    ppermute x12 -> x17, starting transfers between devices: 16.5 us -> 22.4 us  [swap(): lax.ppermute(value, axis, [(i, i ^ mask) for i in range(lax.axis_size(axi...]
    ppermute x2 -> x0, starting transfers between devices: 5.77 us -> none  [the longest x1 2.98 us: body(): mirrored = lax.ppermute(rc, 'ctx', across)]
    ppermute x12 -> x17, waiting for transfers between devices: 27.9 us -> 22.9 us  [swap(): lax.ppermute(value, axis, [(i, i ^ mask) for i in range(lax.axis_size(axi...]
    pallas_call x1, Pallas kernels: 3.29 us -> 0.51 us  [body(): pl.pallas_call(grad_kernel, name='grad', out_shape=(pltpu.VMEM((KW, chans...]
    pallas_call x1, Pallas kernels: 6.54 us -> 4.22 us  [body(): pl.pallas_call(lambda *refs: attend_kernel(*refs, blocks=n), name='attend...]
    pallas_call x1, Pallas kernels: 2.63 us -> 1.38 us  [body(): pl.pallas_call(fine_kernel, name='fine', out_shape=jax.ShapeDtypeStruct((...]
    slice x0 -> x1, local copies, waits for them, and re-layouts: none -> 1.05 us  [body(): rc_b = swap(swap(rc[half:], 'ctx', 1), 'ctx', 6)]
    ppermute x1, starting transfers between devices: 5.53 us -> 4.55 us  [body(): up = lax.ppermute(to_up, 'ctx', [(i, i + 1) for i in range(count - 1)])]
  transfers between devices with their start and end apart: 16 -> 19, of which waited for: 9 -> 8; matrix products, arithmetic and copies ran while one was open for 2% -> 5% of each run, Pallas kernels for 12% -> 9%
where the time goes in v2:
time: 65.3 us; the launch traced here: 64.9 us
  starting transfers between devices  28.3 us (43%)
  waiting for transfers between devices  22.9 us (35%)
  Pallas kernels  6.12 us (9%)
  local copies, waits for them, and re-layouts  5.12 us (8%)
  other arithmetic  1.7 us (3%)
  between operations  0.78 us (1%)
    ppermute x17, waiting for transfers between devices, swap(): lax.ppermute(value, axis, [(i, i ^ mask) for i in range(lax.axis_size(axi...  22.9 us
    ppermute x17, starting transfers between devices, swap(): lax.ppermute(value, axis, [(i, i ^ mask) for i in range(lax.axis_size(axi...  22.4 us
    ppermute x1, starting transfers between devices, body(): up = lax.ppermute(to_up, 'ctx', [(i, i + 1) for i in range(count - 1)])  4.55 us
    pallas_call x1, Pallas kernels, body(): pl.pallas_call(lambda *refs: attend_kernel(*refs, blocks=n), name='attend...  4.22 us
    unnamed x6, local copies, waits for them, and re-layouts  1.75 us
    pallas_call x1, Pallas kernels, body(): pl.pallas_call(fine_kernel, name='fine', out_shape=jax.ShapeDtypeStruct((...  1.38 us
  transfers between devices with their start and end apart: 19, of which 8 were waited for; matrix products, arithmetic and copies ran while one was open for 5% of the time, Pallas kernels for 9%

profile of v2, /device:TPU:0, one launch (start us, length us, event | category | flops | bytes accessed | tf_op | source)
XLA Modules:
  0.0 64.9 jit_solution(6825572554988529703)
XLA Ops:
  0.6 0.0 copy-start
  0.6 0.9 %pad_maximum_fusion.refs_6_ = bf16[320,128]{1,0:T(8,128)(2,1)S(1)} fusion(bf16[192,128]{1,0:T(8,128)(2,1)} %bitcast.27, bf16[128,128]{1,0:T(8,128)(2,1)} %bitcast.28), kind=kLoop, calls=%fused_computation.2 | loop fusion | flops 163840 | bytes 163840 | tf_op jit(solution)/shard_map/concatenate | solution.py:130
  1.5 5.1 %collective-permute-start.2 = (bf16[320,128]{1,0:T(8,128)(2,1)S(1)}, bf16[320,128]{1,0:T(8,128)(2,1)S(1)}, u32[]{:S(2)}, u32[]{:S(2)}) collective-permute-start(bf16[320,128]{1,0:T(8,128)(2,1)S(1)} %pad_maximum_fusion.refs_6_), channel_id=1, source_target_pairs={{0,6},{1,7},{2,4},{3,5},{4,2},{5,3},{6,0},{7,1},{8,14},{9,15},{10,... | collective-permute-start | bytes 245768 | tf_op jit(solution)/shard_map/ppermute | solution.py:115
  6.6 1.0 %slice_bitcast_fusion = (bf16[64,1536]{1,0:T(8,128)(2,1)S(1)}, bf16[64,1536]{1,0:T(8,128)(2,1)S(1)}) fusion(bf16[1,128,1536]{2,1,0:T(8,128)(2,1)} %param.10), kind=kLoop, calls=%fused_computation | loop fusion | bytes 786432 | tf_op jit(solution)/shard_map/slice | solution.py:142
  7.7 1.6 %collective-permute-start.11 = (bf16[64,1536]{1,0:T(8,128)(2,1)S(1)}, bf16[64,1536]{1,0:T(8,128)(2,1)S(1)}, u32[]{:S(2)}, u32[]{:S(2)}) collective-permute-start(bf16[64,1536]{1,0:T(8,128)(2,1)S(1)} %get-tuple-element.14), channel_id=1, source_target_pairs={{0,1},{1,0},{2,3},{3,2},{4,5},{5,4},{6,7},{7,6},{8,9},{9,8},{10,11... | collective-permute-start | bytes 589832 | tf_op jit(solution)/shard_map/ppermute | solution.py:115
  9.2 0.2 collective-permute-start.9
  9.5 0.8 %slice_bitcast_fusion.4 = (bf16[1,1536]{1,0:T(2,128)(2,1)S(1)}, bf16[1,1536]{1,0:T(2,128)(2,1)S(1)}) fusion(bf16[1,128,1536]{2,1,0:T(8,128)(2,1)} %param.10), kind=kLoop, calls=%fused_computation.20 | loop fusion | bytes 12288 | tf_op jit(solution)/shard_map/slice | solution.py:152
  10.2 0.7 %slice_bitcast_fusion.6 = (bf16[1,1024]{1,0:T(2,128)(2,1)S(1)}, bf16[1,1024]{1,0:T(2,128)(2,1)S(1)}) fusion(bf16[1,128,1024]{2,1,0:T(8,128)(2,1)} %param.6), kind=kLoop, calls=%fused_computation.22 | loop fusion | bytes 8192 | tf_op jit(solution)/shard_map/slice | solution.py:152
  11.0 0.8 %slice_bitcast_fusion.2 = (bf16[4,1536]{1,0:T(4,128)(2,1)S(1)}, bf16[4,1536]{1,0:T(4,128)(2,1)S(1)}) fusion(bf16[1,256,1536]{2,1,0:T(8,128)(2,1)} %param.9), kind=kLoop, calls=%fused_computation.17 | loop fusion | bytes 49152 | tf_op jit(solution)/shard_map/slice | solution.py:152
  11.8 0.1 fusion.5
  11.8 1.3 %collective-permute-start.1 = (bf16[8,1536]{1,0:T(8,128)(2,1)S(1)}, bf16[8,1536]{1,0:T(8,128)(2,1)S(1)}, u32[]{:S(2)}, u32[]{:S(2)}) collective-permute-start(bf16[8,1536]{1,0:T(8,128)(2,1)S(1)} %get-tuple-element.20), channel_id=1, source_target_pairs={{1,0},{2,1},{3,2},{4,3},{5,4},{6,5},{7,6},{9,8},{10,9},{11,10},{12... | collective-permute-start | bytes 73736 | tf_op jit(solution)/shard_map/ppermute | solution.py:154
  13.1 4.5 %collective-permute-start = (bf16[8,1536]{1,0:T(8,128)(2,1)S(1)}, bf16[8,1536]{1,0:T(8,128)(2,1)S(1)}, u32[]{:S(2)}, u32[]{:S(2)}) collective-permute-start(bf16[8,1536]{1,0:T(8,128)(2,1)S(1)} %get-tuple-element.21), channel_id=1, source_target_pairs={{0,1},{1,2},{2,3},{3,4},{4,5},{5,6},{6,7},{8,9},{9,10},{10,11},{11... | collective-permute-start | bytes 73736 | tf_op jit(solution)/shard_map/ppermute | solution.py:153
  17.7 0.0 collective-permute-done.11
  17.7 3.7 %collective-permute-start.12 = (bf16[64,1536]{1,0:T(8,128)(2,1)S(1)}, bf16[64,1536]{1,0:T(8,128)(2,1)S(1)}, u32[]{:S(2)}, u32[]{:S(2)}) collective-permute-start(bf16[64,1536]{1,0:T(8,128)(2,1)S(1)} %collective-permute-done.11), channel_id=1, source_target_pairs={{0,6},{1,7},{2,4},{3,5},{4,2},{5,3},{6,0},{7,1},{8,14},{9,15},{10,... | collective-permute-start | bytes 589832 | tf_op jit(solution)/shard_map/ppermute | solution.py:115
  21.4 0.0 collective-permute-done.9
  21.4 0.0 collective-permute-start.10
  21.4 0.0 collective-permute-done.1.refs_3_
  21.4 2.0 %collective-permute-start.4 = (bf16[320,128]{1,0:T(8,128)(2,1)S(1)}, bf16[320,128]{1,0:T(8,128)(2,1)S(1)}, u32[]{:S(2)}, u32[]{:S(2)}) collective-permute-start(bf16[320,128]{1,0:T(8,128)(2,1)S(1)} %pad_maximum_fusion.refs_6_), channel_id=1, source_target_pairs={{0,1},{1,0},{2,3},{3,2},{4,5},{5,4},{6,7},{7,6},{8,9},{9,8},{10,11... | collective-permute-start | bytes 245768 | tf_op jit(solution)/shard_map/ppermute | solution.py:115
  23.4 0.0 collective-permute-done.refs_2_
  23.4 0.0 collective-permute-start.3
  23.4 0.0 collective-permute-done.2.refs_7_
  23.4 2.0 %collective-permute-start.5 = (bf16[320,128]{1,0:T(8,128)(2,1)S(1)}, bf16[320,128]{1,0:T(8,128)(2,1)S(1)}, u32[]{:S(2)}, u32[]{:S(2)}) collective-permute-start(bf16[320,128]{1,0:T(8,128)(2,1)S(1)} %collective-permute-done.2.refs_7_), channel_id=1, source_target_pairs={{0,2},{1,3},{2,0},{3,1},{4,6},{5,7},{6,4},{7,5},{8,10},{9,11},{10,... | collective-permute-start | bytes 245768 | tf_op jit(solution)/shard_map/ppermute | solution.py:115
  25.4 2.8 %collective-permute-done.4.refs_9_ = bf16[320,128]{1,0:T(8,128)(2,1)S(1)} collective-permute-done((bf16[320,128]{1,0:T(8,128)(2,1)S(1)}, bf16[320,128]{1,0:T(8,128)(2,1)S(1)}, u32[]{:S(2)}, u32[]{:S(2)}) %collective-permute-start.4) | collective-permute-done | bytes 81952 | tf_op jit(solution)/shard_map/ppermute | solution.py:115
  28.2 0.2 collective-permute-start.6
  28.4 0.0 collective-permute-done.3.refs_8_
  28.4 1.9 %collective-permute-start.7 = (bf16[320,128]{1,0:T(8,128)(2,1)S(1)}, bf16[320,128]{1,0:T(8,128)(2,1)S(1)}, u32[]{:S(2)}, u32[]{:S(2)}) collective-permute-start(bf16[320,128]{1,0:T(8,128)(2,1)S(1)} %collective-permute-done.3.refs_8_), channel_id=1, source_target_pairs={{0,1},{1,0},{2,3},{3,2},{4,5},{5,4},{6,7},{7,6},{8,9},{9,8},{10,11... | collective-permute-start | bytes 245768 | tf_op jit(solution)/shard_map/ppermute | solution.py:115
  30.2 0.0 collective-permute-done.5.refs_10_
  30.2 0.2 collective-permute-start.8
  30.4 0.1 pad_add_fusion.refs_0_
  30.5 3.0 %collective-permute-done.7.refs_12_ = bf16[320,128]{1,0:T(8,128)(2,1)S(1)} collective-permute-done((bf16[320,128]{1,0:T(8,128)(2,1)S(1)}, bf16[320,128]{1,0:T(8,128)(2,1)S(1)}, u32[]{:S(2)}, u32[]{:S(2)}) %collective-permute-start.7) | collective-permute-done | bytes 81952 | tf_op jit(solution)/shard_map/ppermute | solution.py:115
  33.5 0.0 collective-permute-done.6.refs_11_
  33.5 1.2 %collective-permute-done.8.refs_13_ = bf16[320,128]{1,0:T(8,128)(2,1)S(1)} collective-permute-done((bf16[320,128]{1,0:T(8,128)(2,1)S(1)}, bf16[320,128]{1,0:T(8,128)(2,1)S(1)}, u32[]{:S(2)}, u32[]{:S(2)}) %collective-permute-start.8) | collective-permute-done | bytes 81952 | tf_op jit(solution)/shard_map/ppermute | solution.py:115
  34.7 0.0 copy-done
  34.7 0.0 copy-start.1
  34.7 0.9 %copy-done.1 = bf16[1,128,1024]{2,1,0:T(8,128)(2,1)S(1)} copy-done((bf16[1,128,1024]{2,1,0:T(8,128)(2,1)S(1)}, bf16[1,128,1024]{2,1,0:T(8,128)(2,1)}, u32[]{:S(2)}) %copy-start.1) | copy-done | bytes 262168
  35.6 0.0 copy-start.2
  35.6 0.8 %copy-done.2 = f32[5,1536]{1,0:T(8,128)S(1)} copy-done((f32[5,1536]{1,0:T(8,128)S(1)}, f32[5,1536]{1,0:T(8,128)}, u32[]{:S(2)}) %copy-start.2) | copy-done | bytes 30744
  36.4 4.2 %attend.1 = (f32[128,1536]{1,0:T(8,128)S(1)}, f32[8,1536]{1,0:T(8,128)S(1)}, f32[12,272,128]{2,1,0:T(8,128)S(1)}) custom-call(s32[2]{0:T(128)S(1)} %pad_add_fusion.refs_0_, bf16[128,1024]{1,0:T(8,128)(2,1)S(1)} %bitcast.25, bf16[8,1536]{1,0:T(8,128)(2,1)S(1)} %collective-permute-done.refs_2_, bf16[8,1536]{1,0:T(8,128)(2,1)S(1)} %collective-permute-done.1.refs_3_, ...), custom_call_target="tpu_custom_call" | custom-call | tf_op jit(solution)/shard_map/attend/pallas_call | solution.py:161
  40.7 0.0 collective-permute-done.12.rc_b
  40.7 0.0 collective-permute-done.10.rc_a
  40.7 0.5 grad.1
  41.2 0.1 collective-permute-start.14
  41.3 1.2 %collective-permute-done.14 = f32[5,1536]{1,0:T(8,128)S(1)} collective-permute-done((f32[5,1536]{1,0:T(8,128)S(1)}, f32[5,1536]{1,0:T(8,128)S(1)}, u32[]{:S(2)}, u32[]{:S(2)}) %collective-permute-start.14) | collective-permute-done | bytes 30752 | tf_op jit(solution)/shard_map/ppermute | solution.py:115
  42.5 1.6 %collective-permute-start.15 = (f32[5,1536]{1,0:T(8,128)S(1)}, f32[5,1536]{1,0:T(8,128)S(1)}, u32[]{:S(2)}, u32[]{:S(2)}) collective-permute-start(f32[5,1536]{1,0:T(8,128)S(1)} %add.19), channel_id=1, source_target_pairs={{0,16},{8,24},{16,0},{24,8},{1,17},{9,25},{17,1},{25,9},{2,18},{10... | collective-permute-start | bytes 92168 | tf_op jit(solution)/shard_map/ppermute | solution.py:115
  44.1 2.6 %collective-permute-done.15 = f32[5,1536]{1,0:T(8,128)S(1)} collective-permute-done((f32[5,1536]{1,0:T(8,128)S(1)}, f32[5,1536]{1,0:T(8,128)S(1)}, u32[]{:S(2)}, u32[]{:S(2)}) %collective-permute-start.15) | collective-permute-done | bytes 30752 | tf_op jit(solution)/shard_map/ppermute | solution.py:115
  46.7 0.9 %collective-permute-start.16 = (f32[5,1536]{1,0:T(8,128)S(1)}, f32[5,1536]{1,0:T(8,128)S(1)}, u32[]{:S(2)}, u32[]{:S(2)}) collective-permute-start(f32[5,1536]{1,0:T(8,128)S(1)} %add.20), channel_id=1, source_target_pairs={{0,1},{1,0},{2,3},{3,2},{4,5},{5,4},{6,7},{7,6},{8,9},{9,8},{10,11... | collective-permute-start | bytes 92168 | tf_op jit(solution)/shard_map/ppermute | solution.py:115
  47.6 3.2 %collective-permute-done.16 = f32[5,1536]{1,0:T(8,128)S(1)} collective-permute-done((f32[5,1536]{1,0:T(8,128)S(1)}, f32[5,1536]{1,0:T(8,128)S(1)}, u32[]{:S(2)}, u32[]{:S(2)}) %collective-permute-start.16) | collective-permute-done | bytes 30752 | tf_op jit(solution)/shard_map/ppermute | solution.py:115
  50.8 0.1 collective-permute-start.17
  50.9 4.0 %collective-permute-done.17 = f32[5,1536]{1,0:T(8,128)S(1)} collective-permute-done((f32[5,1536]{1,0:T(8,128)S(1)}, f32[5,1536]{1,0:T(8,128)S(1)}, u32[]{:S(2)}, u32[]{:S(2)}) %collective-permute-start.17) | collective-permute-done | bytes 30752 | tf_op jit(solution)/shard_map/ppermute | solution.py:115
  55.0 1.5 %collective-permute-start.18 = (f32[5,1536]{1,0:T(8,128)S(1)}, f32[5,1536]{1,0:T(8,128)S(1)}, u32[]{:S(2)}, u32[]{:S(2)}) collective-permute-start(f32[5,1536]{1,0:T(8,128)S(1)} %add.22), channel_id=1, source_target_pairs={{0,4},{1,5},{2,6},{3,7},{4,0},{5,1},{6,2},{7,3},{8,12},{9,13},{10,... | collective-permute-start | bytes 92168 | tf_op jit(solution)/shard_map/ppermute | solution.py:115
  56.5 1.6 %collective-permute-start.13 = (bf16[2,1536]{1,0:T(2,128)(2,1)S(1)}, bf16[2,1536]{1,0:T(2,128)(2,1)S(1)}, u32[]{:S(2)}, u32[]{:S(2)}) collective-permute-start(bf16[2,1536]{1,0:T(2,128)(2,1)S(1)} %pad_maximum_fusion.1), channel_id=1, source_target_pairs={{0,7},{1,6},{2,5},{3,4},{4,3},{5,2},{6,1},{7,0},{8,15},{9,14},{10,... | collective-permute-start | bytes 18440 | tf_op jit(solution)/shard_map/ppermute | solution.py:115
  58.0 4.8 %collective-permute-done.13.rc_edge = bf16[2,1536]{1,0:T(2,128)(2,1)S(1)} collective-permute-done((bf16[2,1536]{1,0:T(2,128)(2,1)S(1)}, bf16[2,1536]{1,0:T(2,128)(2,1)S(1)}, u32[]{:S(2)}, u32[]{:S(2)}) %collective-permute-start.13) | collective-permute-done | bytes 6176 | tf_op jit(solution)/shard_map/ppermute | solution.py:115
  62.9 1.4 %fine.1 = bf16[256,1536]{1,0:T(8,128)(2,1)} custom-call(f32[128,1536]{1,0:T(8,128)S(1)} %get-tuple-element.9.grad, f32[8,1536]{1,0:T(8,128)S(1)} %get-tuple-element.10.base_edge, bf16[2,1536]{1,0:T(2,128)(2,1)S(1)} %collective-permute-done.13.rc_edge, f32[5,1536]{1,0:T(8,128)S(1)} %copy-done.2), custom_call_target="tpu_custom_call" | custom-call | tf_op jit(solution)/shard_map/fine/pallas_call | solution.py:189
  64.2 0.0 collective-permute-done.18
  64.2 0.6 add_multiply_fusion
  (8 shorter events, 0.1 us)
Async XLA Ops:
  0.6 34.1 %copy-start = (bf16[1,256,1536]{2,1,0:T(8,128)(2,1)S(1)}, bf16[1,256,1536]{2,1,0:T(8,128)(2,1)}, u32[]{:S(2)}) copy-start(bf16[1,256,1536]{2,1,0:T(8,128)(2,1)} %param.9) | copy-start | bytes 2359300
  1.5 21.9 %collective-permute-start.2 = (bf16[320,128]{1,0:T(8,128)(2,1)S(1)}, bf16[320,128]{1,0:T(8,128)(2,1)S(1)}, u32[]{:S(2)}, u32[]{:S(2)}) collective-permute-start(bf16[320,128]{1,0:T(8,128)(2,1)S(1)} %pad_maximum_fusion.refs_6_), channel_id=1, source_target_pairs={{0,6},{1,7},{2,4},{3,5},{4,2},{5,3},{6,0},{7,1},{8,14},{9,15},{10,... | collective-permute-start | bytes 245768 | tf_op jit(solution)/shard_map/ppermute | solution.py:115
  7.7 10.0 %collective-permute-start.11 = (bf16[64,1536]{1,0:T(8,128)(2,1)S(1)}, bf16[64,1536]{1,0:T(8,128)(2,1)S(1)}, u32[]{:S(2)}, u32[]{:S(2)}) collective-permute-start(bf16[64,1536]{1,0:T(8,128)(2,1)S(1)} %get-tuple-element.14), channel_id=1, source_target_pairs={{0,1},{1,0},{2,3},{3,2},{4,5},{5,4},{6,7},{7,6},{8,9},{9,8},{10,11... | collective-permute-start | bytes 589832 | tf_op jit(solution)/shard_map/ppermute | solution.py:115
  9.2 12.1 %collective-permute-start.9 = (bf16[64,1536]{1,0:T(8,128)(2,1)S(1)}, bf16[64,1536]{1,0:T(8,128)(2,1)S(1)}, u32[]{:S(2)}, u32[]{:S(2)}) collective-permute-start(bf16[64,1536]{1,0:T(8,128)(2,1)S(1)} %get-tuple-element.15), channel_id=1, source_target_pairs={{0,6},{1,7},{2,4},{3,5},{4,2},{5,3},{6,0},{7,1},{8,14},{9,15},{10,... | collective-permute-start | bytes 589832 | tf_op jit(solution)/shard_map/ppermute | solution.py:115
  11.8 9.5 %collective-permute-start.1 = (bf16[8,1536]{1,0:T(8,128)(2,1)S(1)}, bf16[8,1536]{1,0:T(8,128)(2,1)S(1)}, u32[]{:S(2)}, u32[]{:S(2)}) collective-permute-start(bf16[8,1536]{1,0:T(8,128)(2,1)S(1)} %get-tuple-element.20), channel_id=1, source_target_pairs={{1,0},{2,1},{3,2},{4,3},{5,4},{6,5},{7,6},{9,8},{10,9},{11,10},{12... | collective-permute-start | bytes 73736 | tf_op jit(solution)/shard_map/ppermute | solution.py:154
  13.1 10.3 %collective-permute-start = (bf16[8,1536]{1,0:T(8,128)(2,1)S(1)}, bf16[8,1536]{1,0:T(8,128)(2,1)S(1)}, u32[]{:S(2)}, u32[]{:S(2)}) collective-permute-start(bf16[8,1536]{1,0:T(8,128)(2,1)S(1)} %get-tuple-element.21), channel_id=1, source_target_pairs={{0,1},{1,2},{2,3},{3,4},{4,5},{5,6},{6,7},{8,9},{9,10},{10,11},{11... | collective-permute-start | bytes 73736 | tf_op jit(solution)/shard_map/ppermute | solution.py:153
  17.7 23.0 %collective-permute-start.12 = (bf16[64,1536]{1,0:T(8,128)(2,1)S(1)}, bf16[64,1536]{1,0:T(8,128)(2,1)S(1)}, u32[]{:S(2)}, u32[]{:S(2)}) collective-permute-start(bf16[64,1536]{1,0:T(8,128)(2,1)S(1)} %collective-permute-done.11), channel_id=1, source_target_pairs={{0,6},{1,7},{2,4},{3,5},{4,2},{5,3},{6,0},{7,1},{8,14},{9,15},{10,... | collective-permute-start | bytes 589832 | tf_op jit(solution)/shard_map/ppermute | solution.py:115
  21.4 19.3 %collective-permute-start.10 = (bf16[64,1536]{1,0:T(8,128)(2,1)S(1)}, bf16[64,1536]{1,0:T(8,128)(2,1)S(1)}, u32[]{:S(2)}, u32[]{:S(2)}) collective-permute-start(bf16[64,1536]{1,0:T(8,128)(2,1)S(1)} %collective-permute-done.9), channel_id=1, source_target_pairs={{0,1},{1,0},{2,3},{3,2},{4,5},{5,4},{6,7},{7,6},{8,9},{9,8},{10,11... | collective-permute-start | bytes 589832 | tf_op jit(solution)/shard_map/ppermute | solution.py:115
  21.4 6.8 %collective-permute-start.4 = (bf16[320,128]{1,0:T(8,128)(2,1)S(1)}, bf16[320,128]{1,0:T(8,128)(2,1)S(1)}, u32[]{:S(2)}, u32[]{:S(2)}) collective-permute-start(bf16[320,128]{1,0:T(8,128)(2,1)S(1)} %pad_maximum_fusion.refs_6_), channel_id=1, source_target_pairs={{0,1},{1,0},{2,3},{3,2},{4,5},{5,4},{6,7},{7,6},{8,9},{9,8},{10,11... | collective-permute-start | bytes 245768 | tf_op jit(solution)/shard_map/ppermute | solution.py:115
  23.4 5.0 %collective-permute-start.3 = (bf16[320,128]{1,0:T(8,128)(2,1)S(1)}, bf16[320,128]{1,0:T(8,128)(2,1)S(1)}, u32[]{:S(2)}, u32[]{:S(2)}) collective-permute-start(bf16[320,128]{1,0:T(8,128)(2,1)S(1)} %pad_maximum_fusion.refs_6_), channel_id=1, source_target_pairs={{0,2},{1,3},{2,0},{3,1},{4,6},{5,7},{6,4},{7,5},{8,10},{9,11},{10,... | collective-permute-start | bytes 245768 | tf_op jit(solution)/shard_map/ppermute | solution.py:115
  23.4 6.8 %collective-permute-start.5 = (bf16[320,128]{1,0:T(8,128)(2,1)S(1)}, bf16[320,128]{1,0:T(8,128)(2,1)S(1)}, u32[]{:S(2)}, u32[]{:S(2)}) collective-permute-start(bf16[320,128]{1,0:T(8,128)(2,1)S(1)} %collective-permute-done.2.refs_7_), channel_id=1, source_target_pairs={{0,2},{1,3},{2,0},{3,1},{4,6},{5,7},{6,4},{7,5},{8,10},{9,11},{10,... | collective-permute-start | bytes 245768 | tf_op jit(solution)/shard_map/ppermute | solution.py:115
  28.2 5.3 %collective-permute-start.6 = (bf16[320,128]{1,0:T(8,128)(2,1)S(1)}, bf16[320,128]{1,0:T(8,128)(2,1)S(1)}, u32[]{:S(2)}, u32[]{:S(2)}) collective-permute-start(bf16[320,128]{1,0:T(8,128)(2,1)S(1)} %collective-permute-done.2.refs_7_), channel_id=1, source_target_pairs={{0,1},{1,0},{2,3},{3,2},{4,5},{5,4},{6,7},{7,6},{8,9},{9,8},{10,11... | collective-permute-start | bytes 245768 | tf_op jit(solution)/shard_map/ppermute | solution.py:115
  28.4 5.1 %collective-permute-start.7 = (bf16[320,128]{1,0:T(8,128)(2,1)S(1)}, bf16[320,128]{1,0:T(8,128)(2,1)S(1)}, u32[]{:S(2)}, u32[]{:S(2)}) collective-permute-start(bf16[320,128]{1,0:T(8,128)(2,1)S(1)} %collective-permute-done.3.refs_8_), channel_id=1, source_target_pairs={{0,1},{1,0},{2,3},{3,2},{4,5},{5,4},{6,7},{7,6},{8,9},{9,8},{10,11... | collective-permute-start | bytes 245768 | tf_op jit(solution)/shard_map/ppermute | solution.py:115
  30.2 4.4 %collective-permute-start.8 = (bf16[320,128]{1,0:T(8,128)(2,1)S(1)}, bf16[320,128]{1,0:T(8,128)(2,1)S(1)}, u32[]{:S(2)}, u32[]{:S(2)}) collective-permute-start(bf16[320,128]{1,0:T(8,128)(2,1)S(1)} %collective-permute-done.5.refs_10_), channel_id=1, source_target_pairs={{0,1},{1,0},{2,3},{3,2},{4,5},{5,4},{6,7},{7,6},{8,9},{9,8},{10,11... | collective-permute-start | bytes 245768 | tf_op jit(solution)/shard_map/ppermute | solution.py:115
  34.7 1.0 %copy-start.1 = (bf16[1,128,1024]{2,1,0:T(8,128)(2,1)S(1)}, bf16[1,128,1024]{2,1,0:T(8,128)(2,1)}, u32[]{:S(2)}) copy-start(bf16[1,128,1024]{2,1,0:T(8,128)(2,1)} %param.6) | copy-start | bytes 786436
  35.6 0.8 %copy-start.2 = (f32[5,1536]{1,0:T(8,128)S(1)}, f32[5,1536]{1,0:T(8,128)}, u32[]{:S(2)}) copy-start(f32[5,1536]{1,0:T(8,128)} %w.1) | copy-start | bytes 92164
  41.2 1.3 %collective-permute-start.14 = (f32[5,1536]{1,0:T(8,128)S(1)}, f32[5,1536]{1,0:T(8,128)S(1)}, u32[]{:S(2)}, u32[]{:S(2)}) collective-permute-start(f32[5,1536]{1,0:T(8,128)S(1)} %get-tuple-element.11), channel_id=1, source_target_pairs={{0,8},{8,0},{16,24},{24,16},{1,9},{9,1},{17,25},{25,17},{2,10},{10... | collective-permute-start | bytes 92168 | tf_op jit(solution)/shard_map/ppermute | solution.py:115
  42.5 4.2 %collective-permute-start.15 = (f32[5,1536]{1,0:T(8,128)S(1)}, f32[5,1536]{1,0:T(8,128)S(1)}, u32[]{:S(2)}, u32[]{:S(2)}) collective-permute-start(f32[5,1536]{1,0:T(8,128)S(1)} %add.19), channel_id=1, source_target_pairs={{0,16},{8,24},{16,0},{24,8},{1,17},{9,25},{17,1},{25,9},{2,18},{10... | collective-permute-start | bytes 92168 | tf_op jit(solution)/shard_map/ppermute | solution.py:115
  46.7 4.2 %collective-permute-start.16 = (f32[5,1536]{1,0:T(8,128)S(1)}, f32[5,1536]{1,0:T(8,128)S(1)}, u32[]{:S(2)}, u32[]{:S(2)}) collective-permute-start(f32[5,1536]{1,0:T(8,128)S(1)} %add.20), channel_id=1, source_target_pairs={{0,1},{1,0},{2,3},{3,2},{4,5},{5,4},{6,7},{7,6},{8,9},{9,8},{10,11... | collective-permute-start | bytes 92168 | tf_op jit(solution)/shard_map/ppermute | solution.py:115
  50.8 4.2 %collective-permute-start.17 = (f32[5,1536]{1,0:T(8,128)S(1)}, f32[5,1536]{1,0:T(8,128)S(1)}, u32[]{:S(2)}, u32[]{:S(2)}) collective-permute-start(f32[5,1536]{1,0:T(8,128)S(1)} %add.21), channel_id=1, source_target_pairs={{0,2},{1,3},{2,0},{3,1},{4,6},{5,7},{6,4},{7,5},{8,10},{9,11},{10,... | collective-permute-start | bytes 92168 | tf_op jit(solution)/shard_map/ppermute | solution.py:115
  55.0 9.3 %collective-permute-start.18 = (f32[5,1536]{1,0:T(8,128)S(1)}, f32[5,1536]{1,0:T(8,128)S(1)}, u32[]{:S(2)}, u32[]{:S(2)}) collective-permute-start(f32[5,1536]{1,0:T(8,128)S(1)} %add.22), channel_id=1, source_target_pairs={{0,4},{1,5},{2,6},{3,7},{4,0},{5,1},{6,2},{7,3},{8,12},{9,13},{10,... | collective-permute-start | bytes 92168 | tf_op jit(solution)/shard_map/ppermute | solution.py:115
  56.5 6.4 %collective-permute-start.13 = (bf16[2,1536]{1,0:T(2,128)(2,1)S(1)}, bf16[2,1536]{1,0:T(2,128)(2,1)S(1)}, u32[]{:S(2)}, u32[]{:S(2)}) collective-permute-start(bf16[2,1536]{1,0:T(2,128)(2,1)S(1)} %pad_maximum_fusion.1), channel_id=1, source_target_pairs={{0,7},{1,6},{2,5},{3,4},{4,3},{5,2},{6,1},{7,0},{8,15},{9,14},{10,... | collective-permute-start | bytes 18440 | tf_op jit(solution)/shard_map/ppermute | solution.py:115

commit v3 on v2

v3 whole, which is shorter than its diff:
```python
import math

import jax
import jax.numpy as jnp
from jax import lax
from jax.experimental import pallas as pl
from jax.experimental.pallas import tpu as pltpu
from jax.sharding import PartitionSpec as P


HEADS = 8
KW = 5
EDGE = 8
LANES = 128
TAIL = 4
HEAD = 3
TILE = 16
CUT = 2
VMEM = pl.BlockSpec(memory_space=pltpu.VMEM)
HBM = pl.BlockSpec(memory_space=pltpu.HBM)
SMEM = pl.BlockSpec(memory_space=pltpu.SMEM)


def edge_rows(tiles, heads):
    at = {}
    start = 0
    for name, count in (
        ("f_tail", TAIL * tiles),
        ("f_head", HEAD * tiles),
        ("rc_first", tiles),
        ("rc_last", tiles),
        ("q_first", heads),
        ("q_last", heads),
    ):
        at[name] = start
        start += count
    return at, pl.cdiv(start, TILE) * TILE


def pack_kernel(k, vt, q, f, rc, own, rc_a, rc_b, q_ends, f_ends, rc_ends, edges, sem):
    dk, dv = k.shape[0], vt.shape[0]
    half = rc_a.shape[0]
    q_rows, f_rows, rc_rows = q.shape[0], f.shape[0], rc.shape[0]
    copies = [
        (rc.at[0:TILE], rc_ends.at[0:TILE]),
        (rc.at[rc_rows - TILE :], rc_ends.at[TILE:]),
        (q.at[0:TILE], q_ends.at[0:TILE]),
        (q.at[q_rows - TILE :], q_ends.at[TILE:]),
        (f.at[0:TILE], f_ends.at[0:TILE]),
        (f.at[f_rows - TILE :], f_ends.at[TILE:]),
        (k, own.at[0:dk]),
        (vt, own.at[dk : dk + dv]),
        (rc.at[0:half], rc_a),
        (rc.at[half:], rc_b),
    ]
    started = [pltpu.make_async_copy(src, dst, sem.at[i]) for i, (src, dst) in enumerate(copies)]
    for copy in started:
        copy.start()
    for copy in started[:6]:
        copy.wait()
    tiles = rc.shape[1] // LANES
    heads = q.shape[1] // LANES
    at, _ = edge_rows(tiles, heads)
    rc_f = rc_ends[...].astype(jnp.float32)
    q_f = q_ends[...].astype(jnp.float32)
    f_f = f_ends[...].astype(jnp.float32)
    edges[...] = jnp.zeros(edges.shape, jnp.float32)
    for c in range(tiles):
        to = slice(c * LANES, (c + 1) * LANES)
        for j in range(TAIL):
            edges[at["f_tail"] + j * tiles + c] = f_f[2 * TILE - TAIL + j, to]
        for j in range(HEAD):
            edges[at["f_head"] + j * tiles + c] = f_f[j, to]
        edges[at["rc_first"] + c] = rc_f[0, to]
        edges[at["rc_last"] + c] = rc_f[2 * TILE - 1, to]
    for h in range(heads):
        to = slice(h * LANES, (h + 1) * LANES)
        edges[at["q_first"] + h] = q_f[0, to]
        edges[at["q_last"] + h] = q_f[2 * TILE - 1, to]
    own[dk + dv :] = edges[...].astype(own.dtype)
    for copy in started[6:]:
        copy.wait()


def prep_kernel(q, f, w, q_near, w_near, coarse, fine, f_near, sem):
    started = [
        pltpu.make_async_copy(f, f_near, sem.at[0]),
        pltpu.make_async_copy(w, w_near, sem.at[1]),
        pltpu.make_async_copy(q, q_near, sem.at[2]),
    ]
    for copy in started:
        copy.start()
    for copy in started:
        copy.wait()
    rows = coarse.shape[0]
    for c in range(fine.shape[0]):
        to = slice(c * LANES, (c + 1) * LANES)
        fine[c, 0:EDGE] = jnp.zeros((EDGE, LANES), jnp.float32)
        fine[c, EDGE : EDGE + 2 * rows] = f_near[:, to].astype(jnp.float32)
        fine[c, EDGE + 2 * rows :] = jnp.zeros((EDGE, LANES), jnp.float32)
        acc = w_near[0:1, to] * fine[c, pl.ds(EDGE - 2, rows, stride=2), :]
        for k in range(1, KW):
            acc = acc + w_near[k : k + 1, to] * fine[c, pl.ds(EDGE - 2 + k, rows, stride=2), :]
        coarse[:, to] = acc


def attend_kernel(place, q, w, coarse, fine_in, *rest, parts, per, dv):
    kv = rest[:parts]
    base, ends, fine, keys, vals_lo, vals_hi, edges, att_ends = rest[parts:]
    rows, chans = coarse.shape
    dk = q.shape[1] // HEADS
    wide = vals_lo.shape[0]
    blocks = edges.shape[0]
    tiles = chans // LANES
    at, count = edge_rows(tiles, HEADS)
    j = 0
    for part in kv:
        for low in range(0, part.shape[0], per + dv + count):
            keys[j * per : (j + 1) * per] = part[low : low + per]
            vals_lo[0:dv, j * per : (j + 1) * per] = part[low + per : low + per + dv]
            vals_hi[wide - dv :, j * per : (j + 1) * per] = part[low + per : low + per + dv]
            edges[j] = part[low + per + dv : low + per + dv + count].astype(jnp.float32)
            j += 1
    vals_lo[dv:] = jnp.zeros((wide - dv, blocks * per), vals_lo.dtype)
    vals_hi[0 : wide - dv] = jnp.zeros((wide - dv, blocks * per), vals_hi.dtype)
    has_left = place[0]
    has_right = place[1]
    left_at = place[2]
    right_at = place[3]
    scale = dk ** (-0.5)

    def head(h, vals):
        q_h = jnp.concatenate(
            [
                q[:, h * dk : (h + 1) * dk].astype(jnp.float32),
                edges[left_at, at["q_last"] + h : at["q_last"] + h + 1],
                edges[right_at, at["q_first"] + h : at["q_first"] + h + 1],
                jnp.zeros((TILE - 2, dk), jnp.float32),
            ],
            axis=0,
        ).astype(q.dtype)
        s = lax.dot_general(q_h, keys[...], (((1,), (1,)), ((), ())), preferred_element_type=jnp.float32) * scale
        p = jnp.exp(s - jnp.max(s, axis=1, keepdims=True))
        total = jnp.sum(p, axis=1, keepdims=True)
        o = lax.dot_general(
            p.astype(jnp.bfloat16), vals[...], (((1,), (1,)), ((), ())), preferred_element_type=jnp.float32
        )
        return o / total

    over = 2 * wide - 2 * dv
    for pair in range(HEADS // 2):
        lo = head(2 * pair, vals_lo)
        hi = head(2 * pair + 1, vals_hi)
        first = 2 * dv * pair
        pieces = (
            (first, lo[:, : wide - over]),
            (first + wide - over, lo[:, wide - over :] + hi[:, :over]),
            (first + wide, hi[:, over:]),
        )
        for start, piece in pieces:
            to = slice(start, start + piece.shape[1])
            base[:, to] = coarse[:, to] + piece[:rows]
            att_ends[:, to] = piece[rows : rows + EDGE]
    keep_left = has_left == 1
    keep_right = has_right == 1
    rc_left_at = place[4]
    rc_right_at = place[5]
    last = 2 * rows + EDGE
    for c in range(tiles):
        to = slice(c * LANES, (c + 1) * LANES)
        for i in range(TAIL):
            row = at["f_tail"] + i * tiles + c
            fine[c, EDGE - TAIL + i : EDGE - TAIL + i + 1] = jnp.where(keep_left, edges[left_at, row : row + 1], 0.0)
        for i in range(HEAD):
            row = at["f_head"] + i * tiles + c
            fine[c, last + i : last + i + 1] = jnp.where(keep_right, edges[right_at, row : row + 1], 0.0)
        w_c = [w[k : k + 1, to] for k in range(KW)]
        base[0:1, to] = base[0:1, to] + w_c[0] * fine[c, EDGE - 2 : EDGE - 1] + w_c[1] * fine[c, EDGE - 1 : EDGE]
        base[rows - 1 : rows, to] = base[rows - 1 : rows, to] + w_c[4] * fine[c, last : last + 1]
        row = at["rc_first"] + c
        left = att_ends[0:1, to] - edges[rc_left_at, row : row + 1]
        row = at["rc_last"] + c
        right = att_ends[1:2, to] - edges[rc_right_at, row : row + 1]
        for k in range(KW):
            left = left + w_c[k] * fine[c, EDGE - 4 + k : EDGE - 3 + k]
            right = right + w_c[k] * fine[c, last - 2 + k : last - 1 + k]
        ends[0:1, to] = jnp.where(keep_left, left, 0.0)
        ends[1:2, to] = jnp.where(keep_right, right, 0.0)


def grad_kernel(base, fine, rc_a, rc_b, partial, grad):
    rows = base.shape[0]

    def flip(n):
        i = lax.broadcasted_iota(jnp.int32, (n, n), 0)
        j = lax.broadcasted_iota(jnp.int32, (n, n), 1)
        return (i + j == n - 1).astype(jnp.bfloat16)

    pieces = [(rows - rc_a.shape[0], rc_a, flip(rc_a.shape[0])), (0, rc_b, flip(rc_b.shape[0]))]
    for c in range(fine.shape[0]):
        to = slice(c * LANES, (c + 1) * LANES)
        sums = [None] * KW
        for low, rc, turn in pieces:
            n = rc.shape[0]
            g = base[low : low + n, to] - jnp.dot(turn, rc[:, to], preferred_element_type=jnp.float32)
            grad[low : low + n, to] = g
            for k in range(KW):
                tap = fine[c, pl.ds(EDGE - 2 + k + 2 * low, n, stride=2), :]
                term = jnp.sum((g * tap).reshape(n // 8, 8, LANES), axis=0)
                sums[k] = term if sums[k] is None else sums[k] + term
        for k in range(KW):
            partial[k : k + 1, to] = jnp.sum(sums[k], axis=0, keepdims=True)


def fine_kernel(grad, ends, w, d_fine, wide, padded):
    rows = d_fine.shape[0] // 2
    for c in range(wide.shape[0]):
        to = slice(c * LANES, (c + 1) * LANES)
        here = grad[:, to]
        padded[EDGE : EDGE + rows] = here
        padded[EDGE - 1 : EDGE] = ends[0:1, to]
        padded[EDGE + rows : EDGE + rows + 1] = ends[1:2, to]
        after = padded[EDGE + 1 : EDGE + 1 + rows]
        before = padded[EDGE - 1 : EDGE - 1 + rows]
        wide[c, pl.ds(0, rows, stride=2), :] = w[0:1, to] * after + w[2:3, to] * here + w[4:5, to] * before
        wide[c, pl.ds(1, rows, stride=2), :] = w[1:2, to] * after + w[3:4, to] * here
        d_fine[:, to] = wide[c].astype(d_fine.dtype)


def swap(value, axis, mask):
    return lax.ppermute(value, axis, [(i, i ^ mask) for i in range(lax.axis_size(axis))])


def near(value):
    return pltpu.with_memory_space_constraint(value, pltpu.VMEM)


def far(value):
    return pltpu.with_memory_space_constraint(value, pltpu.HBM)


def limit(mib):
    return pltpu.CompilerParams(vmem_limit_bytes=mib << 20)


def body(queries, keys, values, features_fine, rc_state, conv_weight):
    count = lax.axis_size("ctx")
    q, f, rc = queries[0], features_fine[0], rc_state[0]
    rows, chans = rc.shape
    tiles = chans // LANES
    cut = rows * CUT // 8
    dk, dv = keys.shape[2], values.shape[2]
    _, extra = edge_rows(tiles, HEADS)
    size = rows + dv + extra
    bf16, f32 = jnp.bfloat16, jnp.float32

    own, rc_a, rc_b = pl.pallas_call(
        pack_kernel,
        name="pack",
        out_shape=(pltpu.VMEM((size, LANES), bf16), pltpu.VMEM((cut, chans), bf16), pltpu.VMEM((rows - cut, chans), bf16)),
        in_specs=[HBM] * 5,
        out_specs=(VMEM, VMEM, VMEM),
        scratch_shapes=[
            pltpu.VMEM((2 * TILE, q.shape[1]), bf16),
            pltpu.VMEM((2 * TILE, chans), bf16),
            pltpu.VMEM((2 * TILE, chans), bf16),
            pltpu.VMEM((extra, LANES), f32),
            pltpu.SemaphoreType.DMA((10,)),
        ],
        compiler_params=limit(4),
    )(far(keys[0]), far(values[0].T), far(q), far(f), far(rc))

    here = lax.axis_index("ctx").astype(jnp.int32)
    wanted = jnp.stack([here - 1, here + 1, count - here, count - 2 - here])
    if count == 8:
        k4 = swap(own, "ctx", 4)
        rc_b = swap(rc_b, "ctx", 1)
        pair = jnp.concatenate([own, k4], axis=0)
        k2 = swap(pair, "ctx", 2)
        k1 = swap(pair, "ctx", 1)
        rc_a = swap(rc_a, "ctx", 6)
        rc_b = swap(rc_b, "ctx", 6)
        k21 = swap(k2, "ctx", 1)
        rc_a = swap(rc_a, "ctx", 1)
        parts = [pair, k2, k1, k21]
        mask = here ^ wanted
        wanted = ((mask & 1) * 4) | (mask & 2) | ((mask & 4) // 4)
    else:
        parts = [lax.all_gather(own, "ctx", axis=0, tiled=True)]
        rc_a = swap(rc_a, "ctx", count - 1)
        rc_b = swap(rc_b, "ctx", count - 1)
    wanted = jnp.clip(wanted, 0, count - 1)
    ends_of = jnp.stack([here > 0, here < count - 1]).astype(jnp.int32)
    place = jnp.concatenate([ends_of, wanted])

    q_near, w_near, coarse, fine = pl.pallas_call(
        prep_kernel,
        name="prep",
        out_shape=(
            pltpu.VMEM(q.shape, bf16),
            pltpu.VMEM(conv_weight.shape, f32),
            pltpu.VMEM((rows, chans), f32),
            pltpu.VMEM((tiles, 2 * rows + 2 * EDGE, LANES), f32),
        ),
        in_specs=[HBM] * 3,
        out_specs=(VMEM,) * 4,
        scratch_shapes=[pltpu.VMEM(f.shape, bf16), pltpu.SemaphoreType.DMA((3,))],
        compiler_params=limit(8),
    )(far(q), far(f), far(conv_weight))

    wide = pl.cdiv(dv, LANES) * LANES
    base, ends, fine = pl.pallas_call(
        lambda *refs: attend_kernel(*refs, parts=len(parts), per=rows, dv=dv),
        name="attend",
        out_shape=(
            pltpu.VMEM((rows, chans), f32),
            pltpu.VMEM((EDGE, chans), f32),
            pltpu.VMEM((tiles, 2 * rows + 2 * EDGE, LANES), f32),
        ),
        in_specs=[SMEM] + [VMEM] * (4 + len(parts)),
        out_specs=(VMEM,) * 3,
        scratch_shapes=[
            pltpu.VMEM((count * rows, dk), bf16),
            pltpu.VMEM((wide, count * rows), bf16),
            pltpu.VMEM((wide, count * rows), bf16),
            pltpu.VMEM((count, extra, LANES), f32),
            pltpu.VMEM((EDGE, chans), f32),
        ],
        input_output_aliases={3: 0, 4: 2},
        compiler_params=limit(24),
    )(place, near(q_near), near(w_near), near(coarse), near(fine), *[near(part) for part in parts])

    partial, grad = pl.pallas_call(
        grad_kernel,
        name="grad",
        out_shape=(pltpu.VMEM((KW, chans), f32), pltpu.VMEM((rows, chans), f32)),
        in_specs=[VMEM] * 4,
        out_specs=(VMEM,) * 2,
        compiler_params=limit(8),
    )(near(base), near(fine), near(rc_a), near(rc_b))

    d_fine = pl.pallas_call(
        fine_kernel,
        name="fine",
        out_shape=jax.ShapeDtypeStruct((2 * rows, chans), bf16),
        in_specs=[VMEM] * 3,
        out_specs=VMEM,
        scratch_shapes=[
            pltpu.VMEM((tiles, 2 * rows, LANES), f32),
            pltpu.VMEM((rows + 2 * EDGE, LANES), f32),
        ],
        compiler_params=limit(8),
    )(near(grad), near(ends), near(w_near))

    total = partial
    if count == 8:
        rounds = [("dp", (1 << b,)) for b in range(lax.axis_size("dp").bit_length() - 1)]
        rounds += [("ctx", (1, 2, 3)), ("ctx", (4,))]
    else:
        rounds = [(a, (1 << b,)) for a in ("dp", "ctx") for b in range(lax.axis_size(a).bit_length() - 1)]
    for axis, masks in rounds:
        got = [swap(total, axis, mask) for mask in masks]
        total = sum(got, total)
    scale = 1.0 / math.sqrt(lax.axis_size("dp") * rows * count)
    return (d_fine[None], total * scale)


def solution(mesh):
    placed = (
        P("dp", "ctx", None),
        P("dp", "ctx", None),
        P("dp", "ctx", None),
        P("dp", "ctx", None),
        P("dp", "ctx", None),
        P(),
    )

    return jax.shard_map(body, mesh=mesh, in_specs=placed, out_specs=(P("dp", "ctx", None), P()), check_vma=False)
```

time: 65.3 us -> 55.9 us (0.86)
  local copies, waits for them, and re-layouts: 5.12 us -> 0.02 us
  waiting for transfers between devices: 22.9 us -> 18 us
  Pallas kernels: 6.12 us -> 8.87 us
  starting transfers between devices: 28.3 us -> 27.2 us
  other arithmetic: 1.7 us -> 0.9 us
    ppermute x2 -> x0, starting transfers between devices: 5.84 us -> none  [the longest x1 4.55 us: body(): up = lax.ppermute(to_up, 'ctx', [(i, i + 1) for i in range(count - 1)])]
    ppermute x17 -> x14, waiting for transfers between devices: 22.9 us -> 18 us  [swap(): lax.ppermute(value, axis, [(i, i ^ mask) for i in range(lax.axis_size(axi...]
    ppermute x17 -> x14, starting transfers between devices: 22.4 us -> 27.2 us  [swap(): lax.ppermute(value, axis, [(i, i ^ mask) for i in range(lax.axis_size(axi...]
    slice x6 -> x0, local copies, waits for them, and re-layouts: 3.35 us -> none  [the longest x1 1.05 us: body(): rc_b = swap(swap(rc[half:], 'ctx', 1), 'ctx', 6)]
    pallas_call x1 -> x3, Pallas kernels: 4.22 us -> 7.01 us  [the longest x1 4.06 us: body(): pl.pallas_call(lambda *refs: attend_kernel(*refs, parts=len(parts), per=r...]
    unnamed x6 -> x1, local copies, waits for them, and re-layouts: 1.75 us -> 0.01 us
    concatenate x3 -> x1, other arithmetic: 0.96 us -> 0.07 us  [body(): place = jnp.concatenate([ends_of, wanted])]
  transfers between devices with their start and end apart: 19 -> 14, of which waited for: 8 -> 10; matrix products, arithmetic and copies ran while one was open for 5% -> 0% of each run, Pallas kernels for 9% -> 13%
where the time goes in v3:
time: 55.9 us; the launch traced here: 55.8 us
  starting transfers between devices  27.2 us (49%)
  waiting for transfers between devices  18 us (32%)
  Pallas kernels  8.87 us (16%)
  other arithmetic  0.9 us (2%)
  between operations  0.71 us (1%)
    ppermute x14, starting transfers between devices, swap(): lax.ppermute(value, axis, [(i, i ^ mask) for i in range(lax.axis_size(axi...  27.2 us
    ppermute x14, waiting for transfers between devices, swap(): lax.ppermute(value, axis, [(i, i ^ mask) for i in range(lax.axis_size(axi...  18 us
    pallas_call x1, Pallas kernels, body(): pl.pallas_call(lambda *refs: attend_kernel(*refs, parts=len(parts), per=r...  4.06 us
    pallas_call x1, Pallas kernels, body(): pl.pallas_call(prep_kernel, name='prep', out_shape=(pltpu.VMEM(q.shape, b...  1.66 us
    pallas_call x1, Pallas kernels, body(): pl.pallas_call(fine_kernel, name='fine', out_shape=jax.ShapeDtypeStruct((...  1.37 us
    pallas_call x1, Pallas kernels, body(): pl.pallas_call(pack_kernel, name='pack', out_shape=(pltpu.VMEM((size, LAN...  1.29 us
  transfers between devices with their start and end apart: 14, of which 10 were waited for; matrix products, arithmetic and copies ran while one was open for 0% of the time, Pallas kernels for 13%

profile of v3, /device:TPU:0, one launch (start us, length us, event | category | flops | bytes accessed | tf_op | source)
XLA Modules:
  0.0 55.8 jit_solution(10958939510617777198)
XLA Ops:
  0.6 1.3 %pack.1 = (bf16[448,128]{1,0:T(8,128)(2,1)S(1)}, bf16[32,1536]{1,0:T(8,128)(2,1)S(1)}, bf16[96,1536]{1,0:T(8,128)(2,1)S(1)}) custom-call(bf16[128,128]{1,0:T(8,128)(2,1)} %bitcast.21, bf16[192,128]{1,0:T(8,128)(2,1)} %bitcast.20, bf16[128,1024]{1,0:T(8,128)(2,1)} %bitcast.16, bf16[256,1536]{1,0:T(8,128)(2,1)} %bitcast.14, bf16[128,1536]{1,0:T(8,128)(2,1)} %bitcast.19), custom_call_target="tpu_custom_call" | custom-call | tf_op jit(solution)/shard_map/pack/pallas_call | solution.py:257
  1.9 4.1 %collective-permute-start = (bf16[448,128]{1,0:T(8,128)(2,1)S(1)}, bf16[448,128]{1,0:T(8,128)(2,1)S(1)}, u32[]{:S(2)}, u32[]{:S(2)}) collective-permute-start(bf16[448,128]{1,0:T(8,128)(2,1)S(1)} %get-tuple-element.18), channel_id=1, source_target_pairs={{0,4},{1,5},{2,6},{3,7},{4,0},{5,1},{6,2},{7,3},{8,12},{9,13},{10,... | collective-permute-start | bytes 344072 | tf_op jit(solution)/shard_map/ppermute | solution.py:231
  6.1 1.5 %collective-permute-start.6 = (bf16[96,1536]{1,0:T(8,128)(2,1)S(1)}, bf16[96,1536]{1,0:T(8,128)(2,1)S(1)}, u32[]{:S(2)}, u32[]{:S(2)}) collective-permute-start(bf16[96,1536]{1,0:T(8,128)(2,1)S(1)} %get-tuple-element.22), channel_id=1, source_target_pairs={{0,1},{1,0},{2,3},{3,2},{4,5},{5,4},{6,7},{7,6},{8,9},{9,8},{10,11... | collective-permute-start | bytes 884744 | tf_op jit(solution)/shard_map/ppermute | solution.py:231
  7.6 4.1 %collective-permute-done = bf16[448,128]{1,0:T(8,128)(2,1)S(1)} collective-permute-done((bf16[448,128]{1,0:T(8,128)(2,1)S(1)}, bf16[448,128]{1,0:T(8,128)(2,1)S(1)}, u32[]{:S(2)}, u32[]{:S(2)}) %collective-permute-start) | collective-permute-done | bytes 114720 | tf_op jit(solution)/shard_map/ppermute | solution.py:231
  11.7 0.8 %collective-permute-start.1 = (bf16[896,128]{1,0:T(8,128)(2,1)S(1)}, bf16[896,128]{1,0:T(8,128)(2,1)S(1)}, u32[]{:S(2)}, u32[]{:S(2)}) collective-permute-start(bf16[896,128]{1,0:T(8,128)(2,1)S(1)} %constant_dynamic-update-slice_fusion.refs_5_), channel_id=1, source_target_pairs={{0,2},{1,3},{2,0},{3,1},{4,6},{5,7},{6,4},{7,5},{8,10},{9,11},{10,... | collective-permute-start | bytes 688136 | tf_op jit(solution)/shard_map/ppermute | solution.py:231
  12.5 2.9 %collective-permute-start.4 = (bf16[32,1536]{1,0:T(8,128)(2,1)S(1)}, bf16[32,1536]{1,0:T(8,128)(2,1)S(1)}, u32[]{:S(2)}, u32[]{:S(2)}) collective-permute-start(bf16[32,1536]{1,0:T(8,128)(2,1)S(1)} %get-tuple-element.21), channel_id=1, source_target_pairs={{0,6},{1,7},{2,4},{3,5},{4,2},{5,3},{6,0},{7,1},{8,14},{9,15},{10,... | collective-permute-start | bytes 294920 | tf_op jit(solution)/shard_map/ppermute | solution.py:231
  15.4 1.5 %collective-permute-start.2 = (bf16[896,128]{1,0:T(8,128)(2,1)S(1)}, bf16[896,128]{1,0:T(8,128)(2,1)S(1)}, u32[]{:S(2)}, u32[]{:S(2)}) collective-permute-start(bf16[896,128]{1,0:T(8,128)(2,1)S(1)} %constant_dynamic-update-slice_fusion.refs_5_), channel_id=1, source_target_pairs={{0,1},{1,0},{2,3},{3,2},{4,5},{5,4},{6,7},{7,6},{8,9},{9,8},{10,11... | collective-permute-start | bytes 688136 | tf_op jit(solution)/shard_map/ppermute | solution.py:231
  16.9 0.0 collective-permute-done.6
  16.9 0.9 %collective-permute-start.7 = (bf16[96,1536]{1,0:T(8,128)(2,1)S(1)}, bf16[96,1536]{1,0:T(8,128)(2,1)S(1)}, u32[]{:S(2)}, u32[]{:S(2)}) collective-permute-start(bf16[96,1536]{1,0:T(8,128)(2,1)S(1)} %collective-permute-done.6), channel_id=1, source_target_pairs={{0,6},{1,7},{2,4},{3,5},{4,2},{5,3},{6,0},{7,1},{8,14},{9,15},{10,... | collective-permute-start | bytes 884744 | tf_op jit(solution)/shard_map/ppermute | solution.py:231
  17.8 0.7 %collective-permute-done.1.refs_6_ = bf16[896,128]{1,0:T(8,128)(2,1)S(1)} collective-permute-done((bf16[896,128]{1,0:T(8,128)(2,1)S(1)}, bf16[896,128]{1,0:T(8,128)(2,1)S(1)}, u32[]{:S(2)}, u32[]{:S(2)}) %collective-permute-start.1) | collective-permute-done | bytes 229408 | tf_op jit(solution)/shard_map/ppermute | solution.py:231
  18.5 1.5 %collective-permute-start.3 = (bf16[896,128]{1,0:T(8,128)(2,1)S(1)}, bf16[896,128]{1,0:T(8,128)(2,1)S(1)}, u32[]{:S(2)}, u32[]{:S(2)}) collective-permute-start(bf16[896,128]{1,0:T(8,128)(2,1)S(1)} %collective-permute-done.1.refs_6_), channel_id=1, source_target_pairs={{0,1},{1,0},{2,3},{3,2},{4,5},{5,4},{6,7},{7,6},{8,9},{9,8},{10,11... | collective-permute-start | bytes 688136 | tf_op jit(solution)/shard_map/ppermute | solution.py:231
  20.0 0.1 add_convert_fusion
  20.1 1.7 %prep.1 = (bf16[128,1024]{1,0:T(8,128)(2,1)S(1)}, f32[5,1536]{1,0:T(8,128)S(1)}, f32[128,1536]{1,0:T(8,128)S(1)}, f32[12,272,128]{2,1,0:T(8,128)S(1)}) custom-call(bf16[128,1024]{1,0:T(8,128)(2,1)} %bitcast.17, bf16[256,1536]{1,0:T(8,128)(2,1)} %bitcast.15, f32[5,1536]{1,0:T(8,128)} %w.1), custom_call_target="tpu_custom_call" | custom-call | tf_op jit(solution)/shard_map/prep/pallas_call | solution.py:296
  21.7 0.1 or_clamp_fusion
  21.8 2.1 %collective-permute-done.4 = bf16[32,1536]{1,0:T(8,128)(2,1)S(1)} collective-permute-done((bf16[32,1536]{1,0:T(8,128)(2,1)S(1)}, bf16[32,1536]{1,0:T(8,128)(2,1)S(1)}, u32[]{:S(2)}, u32[]{:S(2)}) %collective-permute-start.4) | collective-permute-done | bytes 98336 | tf_op jit(solution)/shard_map/ppermute | solution.py:231
  24.0 1.5 %collective-permute-start.5 = (bf16[32,1536]{1,0:T(8,128)(2,1)S(1)}, bf16[32,1536]{1,0:T(8,128)(2,1)S(1)}, u32[]{:S(2)}, u32[]{:S(2)}) collective-permute-start(bf16[32,1536]{1,0:T(8,128)(2,1)S(1)} %collective-permute-done.4), channel_id=1, source_target_pairs={{0,1},{1,0},{2,3},{3,2},{4,5},{5,4},{6,7},{7,6},{8,9},{9,8},{10,11... | collective-permute-start | bytes 294920 | tf_op jit(solution)/shard_map/ppermute | solution.py:231
  25.5 0.1 pad_add_fusion.refs_0_
  25.5 0.0 collective-permute-done.2.refs_7_
  25.5 3.0 %collective-permute-done.3.refs_8_ = bf16[896,128]{1,0:T(8,128)(2,1)S(1)} collective-permute-done((bf16[896,128]{1,0:T(8,128)(2,1)S(1)}, bf16[896,128]{1,0:T(8,128)(2,1)S(1)}, u32[]{:S(2)}, u32[]{:S(2)}) %collective-permute-start.3) | collective-permute-done | bytes 229408 | tf_op jit(solution)/shard_map/ppermute | solution.py:231
  28.6 4.1 %attend.1 = (f32[128,1536]{1,0:T(8,128)S(1)}, f32[8,1536]{1,0:T(8,128)S(1)}, f32[12,272,128]{2,1,0:T(8,128)S(1)}) custom-call(s32[6]{0:T(128)S(1)} %pad_add_fusion.refs_0_, bf16[128,1024]{1,0:T(8,128)(2,1)S(1)} %get-tuple-element.14.refs_1_, f32[5,1536]{1,0:T(8,128)S(1)} %get-tuple-element.15.refs_2_.w, ...), custom_call_target="tpu_custom_call", output_to_operand_aliasing={{0}: (3, {}), {2}: (4, {})} | custom-call | tf_op jit(solution)/shard_map/attend/pallas_call | solution.py:312
  32.6 0.0 collective-permute-done.5.rc_a
  32.7 0.0 collective-permute-done.7.rc_b
  32.7 0.5 grad.1
  33.2 0.1 collective-permute-start.8
  33.2 1.2 %collective-permute-done.8 = f32[5,1536]{1,0:T(8,128)S(1)} collective-permute-done((f32[5,1536]{1,0:T(8,128)S(1)}, f32[5,1536]{1,0:T(8,128)S(1)}, u32[]{:S(2)}, u32[]{:S(2)}) %collective-permute-start.8) | collective-permute-done | bytes 30752 | tf_op jit(solution)/shard_map/ppermute | solution.py:231
  34.5 1.5 %collective-permute-start.9 = (f32[5,1536]{1,0:T(8,128)S(1)}, f32[5,1536]{1,0:T(8,128)S(1)}, u32[]{:S(2)}, u32[]{:S(2)}) collective-permute-start(f32[5,1536]{1,0:T(8,128)S(1)} %add.24), channel_id=1, source_target_pairs={{0,16},{8,24},{16,0},{24,8},{1,17},{9,25},{17,1},{25,9},{2,18},{10... | collective-permute-start | bytes 92168 | tf_op jit(solution)/shard_map/ppermute | solution.py:231
  36.0 2.6 %collective-permute-done.9 = f32[5,1536]{1,0:T(8,128)S(1)} collective-permute-done((f32[5,1536]{1,0:T(8,128)S(1)}, f32[5,1536]{1,0:T(8,128)S(1)}, u32[]{:S(2)}, u32[]{:S(2)}) %collective-permute-start.9) | collective-permute-done | bytes 30752 | tf_op jit(solution)/shard_map/ppermute | solution.py:231
  38.6 2.2 %collective-permute-start.12 = (f32[5,1536]{1,0:T(8,128)S(1)}, f32[5,1536]{1,0:T(8,128)S(1)}, u32[]{:S(2)}, u32[]{:S(2)}) collective-permute-start(f32[5,1536]{1,0:T(8,128)S(1)} %add.25), channel_id=1, source_target_pairs={{0,3},{1,2},{2,1},{3,0},{4,7},{5,6},{6,5},{7,4},{8,11},{9,10},{10,... | collective-permute-start | bytes 92168 | tf_op jit(solution)/shard_map/ppermute | solution.py:231
  40.8 0.8 %collective-permute-start.11 = (f32[5,1536]{1,0:T(8,128)S(1)}, f32[5,1536]{1,0:T(8,128)S(1)}, u32[]{:S(2)}, u32[]{:S(2)}) collective-permute-start(f32[5,1536]{1,0:T(8,128)S(1)} %add.25), channel_id=1, source_target_pairs={{0,2},{1,3},{2,0},{3,1},{4,6},{5,7},{6,4},{7,5},{8,10},{9,11},{10,... | collective-permute-start | bytes 92168 | tf_op jit(solution)/shard_map/ppermute | solution.py:231
  41.7 0.5 collective-permute-start.10
  42.2 1.5 %collective-permute-done.12 = f32[5,1536]{1,0:T(8,128)S(1)} collective-permute-done((f32[5,1536]{1,0:T(8,128)S(1)}, f32[5,1536]{1,0:T(8,128)S(1)}, u32[]{:S(2)}, u32[]{:S(2)}) %collective-permute-start.12) | collective-permute-done | bytes 30752 | tf_op jit(solution)/shard_map/ppermute | solution.py:231
  43.7 1.2 %collective-permute-done.11 = f32[5,1536]{1,0:T(8,128)S(1)} collective-permute-done((f32[5,1536]{1,0:T(8,128)S(1)}, f32[5,1536]{1,0:T(8,128)S(1)}, u32[]{:S(2)}, u32[]{:S(2)}) %collective-permute-start.11) | collective-permute-done | bytes 30752 | tf_op jit(solution)/shard_map/ppermute | solution.py:231
  44.9 0.8 %collective-permute-done.10 = f32[5,1536]{1,0:T(8,128)S(1)} collective-permute-done((f32[5,1536]{1,0:T(8,128)S(1)}, f32[5,1536]{1,0:T(8,128)S(1)}, u32[]{:S(2)}, u32[]{:S(2)}) %collective-permute-start.10) | collective-permute-done | bytes 30752 | tf_op jit(solution)/shard_map/ppermute | solution.py:231
  45.8 7.3 %collective-permute-start.13 = (f32[5,1536]{1,0:T(8,128)S(1)}, f32[5,1536]{1,0:T(8,128)S(1)}, u32[]{:S(2)}, u32[]{:S(2)}) collective-permute-start(f32[5,1536]{1,0:T(8,128)S(1)} %add_add_fusion), channel_id=1, source_target_pairs={{0,4},{1,5},{2,6},{3,7},{4,0},{5,1},{6,2},{7,3},{8,12},{9,13},{10,... | collective-permute-start | bytes 92168 | tf_op jit(solution)/shard_map/ppermute | solution.py:231
  53.1 1.4 %fine.1 = bf16[256,1536]{1,0:T(8,128)(2,1)} custom-call(f32[128,1536]{1,0:T(8,128)S(1)} %get-tuple-element.23.grad, f32[8,1536]{1,0:T(8,128)S(1)} %get-tuple-element.24.ends, f32[5,1536]{1,0:T(8,128)S(1)} %get-tuple-element.15.refs_2_.w), custom_call_target="tpu_custom_call" | custom-call | tf_op jit(solution)/shard_map/fine/pallas_call | solution.py:342
  54.4 0.7 %collective-permute-done.13 = f32[5,1536]{1,0:T(8,128)S(1)} collective-permute-done((f32[5,1536]{1,0:T(8,128)S(1)}, f32[5,1536]{1,0:T(8,128)S(1)}, u32[]{:S(2)}, u32[]{:S(2)}) %collective-permute-start.13) | collective-permute-done | bytes 30752 | tf_op jit(solution)/shard_map/ppermute | solution.py:231
  55.1 0.6 %add_multiply_fusion = f32[5,1536]{1,0:T(8,128)} fusion(f32[5,1536]{1,0:T(8,128)S(1)} %add_add_fusion, f32[5,1536]{1,0:T(8,128)S(1)} %collective-permute-done.13), kind=kLoop, calls=%fused_computation | loop fusion | flops 15360 | bytes 92160 | tf_op jit(solution)/shard_map/mul | solution.py:365
  (5 shorter events, 0.1 us)
Async XLA Ops:
  1.9 9.7 %collective-permute-start = (bf16[448,128]{1,0:T(8,128)(2,1)S(1)}, bf16[448,128]{1,0:T(8,128)(2,1)S(1)}, u32[]{:S(2)}, u32[]{:S(2)}) collective-permute-start(bf16[448,128]{1,0:T(8,128)(2,1)S(1)} %get-tuple-element.18), channel_id=1, source_target_pairs={{0,4},{1,5},{2,6},{3,7},{4,0},{5,1},{6,2},{7,3},{8,12},{9,13},{10,... | collective-permute-start | bytes 344072 | tf_op jit(solution)/shard_map/ppermute | solution.py:231
  6.1 10.8 %collective-permute-start.6 = (bf16[96,1536]{1,0:T(8,128)(2,1)S(1)}, bf16[96,1536]{1,0:T(8,128)(2,1)S(1)}, u32[]{:S(2)}, u32[]{:S(2)}) collective-permute-start(bf16[96,1536]{1,0:T(8,128)(2,1)S(1)} %get-tuple-element.22), channel_id=1, source_target_pairs={{0,1},{1,0},{2,3},{3,2},{4,5},{5,4},{6,7},{7,6},{8,9},{9,8},{10,11... | collective-permute-start | bytes 884744 | tf_op jit(solution)/shard_map/ppermute | solution.py:231
  11.7 6.8 %collective-permute-start.1 = (bf16[896,128]{1,0:T(8,128)(2,1)S(1)}, bf16[896,128]{1,0:T(8,128)(2,1)S(1)}, u32[]{:S(2)}, u32[]{:S(2)}) collective-permute-start(bf16[896,128]{1,0:T(8,128)(2,1)S(1)} %constant_dynamic-update-slice_fusion.refs_5_), channel_id=1, source_target_pairs={{0,2},{1,3},{2,0},{3,1},{4,6},{5,7},{6,4},{7,5},{8,10},{9,11},{10,... | collective-permute-start | bytes 688136 | tf_op jit(solution)/shard_map/ppermute | solution.py:231
  12.5 11.5 %collective-permute-start.4 = (bf16[32,1536]{1,0:T(8,128)(2,1)S(1)}, bf16[32,1536]{1,0:T(8,128)(2,1)S(1)}, u32[]{:S(2)}, u32[]{:S(2)}) collective-permute-start(bf16[32,1536]{1,0:T(8,128)(2,1)S(1)} %get-tuple-element.21), channel_id=1, source_target_pairs={{0,6},{1,7},{2,4},{3,5},{4,2},{5,3},{6,0},{7,1},{8,14},{9,15},{10,... | collective-permute-start | bytes 294920 | tf_op jit(solution)/shard_map/ppermute | solution.py:231
  15.4 10.2 %collective-permute-start.2 = (bf16[896,128]{1,0:T(8,128)(2,1)S(1)}, bf16[896,128]{1,0:T(8,128)(2,1)S(1)}, u32[]{:S(2)}, u32[]{:S(2)}) collective-permute-start(bf16[896,128]{1,0:T(8,128)(2,1)S(1)} %constant_dynamic-update-slice_fusion.refs_5_), channel_id=1, source_target_pairs={{0,1},{1,0},{2,3},{3,2},{4,5},{5,4},{6,7},{7,6},{8,9},{9,8},{10,11... | collective-permute-start | bytes 688136 | tf_op jit(solution)/shard_map/ppermute | solution.py:231
  16.9 15.8 %collective-permute-start.7 = (bf16[96,1536]{1,0:T(8,128)(2,1)S(1)}, bf16[96,1536]{1,0:T(8,128)(2,1)S(1)}, u32[]{:S(2)}, u32[]{:S(2)}) collective-permute-start(bf16[96,1536]{1,0:T(8,128)(2,1)S(1)} %collective-permute-done.6), channel_id=1, source_target_pairs={{0,6},{1,7},{2,4},{3,5},{4,2},{5,3},{6,0},{7,1},{8,14},{9,15},{10,... | collective-permute-start | bytes 884744 | tf_op jit(solution)/shard_map/ppermute | solution.py:231
  18.5 10.1 %collective-permute-start.3 = (bf16[896,128]{1,0:T(8,128)(2,1)S(1)}, bf16[896,128]{1,0:T(8,128)(2,1)S(1)}, u32[]{:S(2)}, u32[]{:S(2)}) collective-permute-start(bf16[896,128]{1,0:T(8,128)(2,1)S(1)} %collective-permute-done.1.refs_6_), channel_id=1, source_target_pairs={{0,1},{1,0},{2,3},{3,2},{4,5},{5,4},{6,7},{7,6},{8,9},{9,8},{10,11... | collective-permute-start | bytes 688136 | tf_op jit(solution)/shard_map/ppermute | solution.py:231
  24.0 8.7 %collective-permute-start.5 = (bf16[32,1536]{1,0:T(8,128)(2,1)S(1)}, bf16[32,1536]{1,0:T(8,128)(2,1)S(1)}, u32[]{:S(2)}, u32[]{:S(2)}) collective-permute-start(bf16[32,1536]{1,0:T(8,128)(2,1)S(1)} %collective-permute-done.4), channel_id=1, source_target_pairs={{0,1},{1,0},{2,3},{3,2},{4,5},{5,4},{6,7},{7,6},{8,9},{9,8},{10,11... | collective-permute-start | bytes 294920 | tf_op jit(solution)/shard_map/ppermute | solution.py:231
  33.2 1.3 %collective-permute-start.8 = (f32[5,1536]{1,0:T(8,128)S(1)}, f32[5,1536]{1,0:T(8,128)S(1)}, u32[]{:S(2)}, u32[]{:S(2)}) collective-permute-start(f32[5,1536]{1,0:T(8,128)S(1)} %get-tuple-element.25), channel_id=1, source_target_pairs={{0,8},{8,0},{16,24},{24,16},{1,9},{9,1},{17,25},{25,17},{2,10},{10... | collective-permute-start | bytes 92168 | tf_op jit(solution)/shard_map/ppermute | solution.py:231
  34.5 4.2 %collective-permute-start.9 = (f32[5,1536]{1,0:T(8,128)S(1)}, f32[5,1536]{1,0:T(8,128)S(1)}, u32[]{:S(2)}, u32[]{:S(2)}) collective-permute-start(f32[5,1536]{1,0:T(8,128)S(1)} %add.24), channel_id=1, source_target_pairs={{0,16},{8,24},{16,0},{24,8},{1,17},{9,25},{17,1},{25,9},{2,18},{10... | collective-permute-start | bytes 92168 | tf_op jit(solution)/shard_map/ppermute | solution.py:231
  38.6 5.1 %collective-permute-start.12 = (f32[5,1536]{1,0:T(8,128)S(1)}, f32[5,1536]{1,0:T(8,128)S(1)}, u32[]{:S(2)}, u32[]{:S(2)}) collective-permute-start(f32[5,1536]{1,0:T(8,128)S(1)} %add.25), channel_id=1, source_target_pairs={{0,3},{1,2},{2,1},{3,0},{4,7},{5,6},{6,5},{7,4},{8,11},{9,10},{10,... | collective-permute-start | bytes 92168 | tf_op jit(solution)/shard_map/ppermute | solution.py:231
  40.8 4.1 %collective-permute-start.11 = (f32[5,1536]{1,0:T(8,128)S(1)}, f32[5,1536]{1,0:T(8,128)S(1)}, u32[]{:S(2)}, u32[]{:S(2)}) collective-permute-start(f32[5,1536]{1,0:T(8,128)S(1)} %add.25), channel_id=1, source_target_pairs={{0,2},{1,3},{2,0},{3,1},{4,6},{5,7},{6,4},{7,5},{8,10},{9,11},{10,... | collective-permute-start | bytes 92168 | tf_op jit(solution)/shard_map/ppermute | solution.py:231
  41.7 4.1 %collective-permute-start.10 = (f32[5,1536]{1,0:T(8,128)S(1)}, f32[5,1536]{1,0:T(8,128)S(1)}, u32[]{:S(2)}, u32[]{:S(2)}) collective-permute-start(f32[5,1536]{1,0:T(8,128)S(1)} %add.25), channel_id=1, source_target_pairs={{0,1},{1,0},{2,3},{3,2},{4,5},{5,4},{6,7},{7,6},{8,9},{9,8},{10,11... | collective-permute-start | bytes 92168 | tf_op jit(solution)/shard_map/ppermute | solution.py:231
  45.8 9.4 %collective-permute-start.13 = (f32[5,1536]{1,0:T(8,128)S(1)}, f32[5,1536]{1,0:T(8,128)S(1)}, u32[]{:S(2)}, u32[]{:S(2)}) collective-permute-start(f32[5,1536]{1,0:T(8,128)S(1)} %add_add_fusion), channel_id=1, source_target_pairs={{0,4},{1,5},{2,6},{3,7},{4,0},{5,1},{6,2},{7,3},{8,12},{9,13},{10,... | collective-permute-start | bytes 92168 | tf_op jit(solution)/shard_map/ppermute | solution.py:231

commit v4 on v3

--- a/solution.py
+++ b/solution.py
@@ -15,7 +15,7 @@
 TAIL = 4
 HEAD = 3
 TILE = 16
-CUT = 2
+CUT = 3
 VMEM = pl.BlockSpec(memory_space=pltpu.VMEM)
 HBM = pl.BlockSpec(memory_space=pltpu.HBM)
 SMEM = pl.BlockSpec(memory_space=pltpu.SMEM)
@@ -104,67 +104,115 @@
         coarse[:, to] = acc
 
 
-def attend_kernel(place, q, w, coarse, fine_in, *rest, parts, per, dv):
-    kv = rest[:parts]
+def load_blocks(blocks, per, dv, keys, vals_lo, vals_hi):
+    wide = vals_lo.shape[0]
+    for j, (ref, low) in enumerate(blocks):
+        to = slice(j * per, (j + 1) * per)
+        keys[to] = ref[low : low + per]
+        vals_lo[0:dv, to] = ref[low + per : low + per + dv]
+        vals_hi[wide - dv :, to] = ref[low + per : low + per + dv]
+    span = len(blocks) * per
+    vals_lo[dv:] = jnp.zeros((wide - dv, span), vals_lo.dtype)
+    vals_hi[0 : wide - dv] = jnp.zeros((wide - dv, span), vals_hi.dtype)
+
+
+def times(a, b):
+    return lax.dot_general(a, b, (((1,), (1,)), ((), ())), preferred_element_type=jnp.float32)
+
+
+def first_kernel(q, *rest, parts, per, dv, count):
+    refs = rest[:parts]
+    keys, vals_lo, vals_hi, tops, totals, sums = rest[parts:]
+    dk = q.shape[1] // HEADS
+    blocks = block_list(refs, per + dv + count)
+    load_blocks(blocks[: keys.shape[0] // per], per, dv, keys, vals_lo, vals_hi)
+    scale = dk ** (-0.5)
+    for h in range(HEADS):
+        vals = vals_hi if h % 2 else vals_lo
+        s = times(q[:, h * dk : (h + 1) * dk], keys[...]) * scale
+        top = jnp.max(s, axis=1, keepdims=True)
+        p = jnp.exp(s - top)
+        tops[h] = jnp.broadcast_to(top, tops.shape[1:])
+        totals[h] = jnp.broadcast_to(jnp.sum(p, axis=1, keepdims=True), totals.shape[1:])
+        sums[h] = times(p.astype(jnp.bfloat16), vals[...])
+
+
+def block_list(refs, size):
+    return [(ref, low) for ref in refs for low in range(0, ref.shape[0], size)]
+
+
+def attend_kernel(q, w, coarse, fine_in, keys_a, lo_a, hi_a, tops, totals, sums, *rest, parts, per, dv, ring):
+    refs = rest[:parts]
     base, ends, fine, keys, vals_lo, vals_hi, edges, att_ends = rest[parts:]
     rows, chans = coarse.shape
     dk = q.shape[1] // HEADS
     wide = vals_lo.shape[0]
-    blocks = edges.shape[0]
     tiles = chans // LANES
     at, count = edge_rows(tiles, HEADS)
-    j = 0
-    for part in kv:
-        for low in range(0, part.shape[0], per + dv + count):
-            keys[j * per : (j + 1) * per] = part[low : low + per]
-            vals_lo[0:dv, j * per : (j + 1) * per] = part[low + per : low + per + dv]
-            vals_hi[wide - dv :, j * per : (j + 1) * per] = part[low + per : low + per + dv]
-            edges[j] = part[low + per + dv : low + per + dv + count].astype(jnp.float32)
-            j += 1
-    vals_lo[dv:] = jnp.zeros((wide - dv, blocks * per), vals_lo.dtype)
-    vals_hi[0 : wide - dv] = jnp.zeros((wide - dv, blocks * per), vals_hi.dtype)
-    has_left = place[0]
-    has_right = place[1]
-    left_at = place[2]
-    right_at = place[3]
+    blocks = block_list(refs, per + dv + count)
+    total_blocks = len(blocks)
+    load_blocks(blocks[total_blocks // 2 :], per, dv, keys, vals_lo, vals_hi)
+    for j, (ref, low) in enumerate(blocks):
+        edges[j] = ref[low + per + dv : low + per + dv + count].astype(jnp.float32)
+    here = lax.axis_index("ctx").astype(jnp.int32)
+
+    def spot(other):
+        if not ring:
+            return jnp.clip(other, 0, total_blocks - 1)
+        mask = (here ^ other) & (total_blocks - 1)
+        return ((mask & 1) * 4) | (mask & 2) | ((mask & 4) // 4)
+
+    keep_left = here > 0
+    keep_right = here < total_blocks - 1
+    left_at, right_at = spot(here - 1), spot(here + 1)
+    rc_left_at, rc_right_at = spot(total_blocks - here), spot(total_blocks - 2 - here)
     scale = dk ** (-0.5)
-
-    def head(h, vals):
-        q_h = jnp.concatenate(
-            [
-                q[:, h * dk : (h + 1) * dk].astype(jnp.float32),
-                edges[left_at, at["q_last"] + h : at["q_last"] + h + 1],
-                edges[right_at, at["q_first"] + h : at["q_first"] + h + 1],
-                jnp.zeros((TILE - 2, dk), jnp.float32),
-            ],
-            axis=0,
-        ).astype(q.dtype)
-        s = lax.dot_general(q_h, keys[...], (((1,), (1,)), ((), ())), preferred_element_type=jnp.float32) * scale
-        p = jnp.exp(s - jnp.max(s, axis=1, keepdims=True))
-        total = jnp.sum(p, axis=1, keepdims=True)
-        o = lax.dot_general(
-            p.astype(jnp.bfloat16), vals[...], (((1,), (1,)), ((), ())), preferred_element_type=jnp.float32
+    over = 2 * wide - 2 * dv
+
+    def head(h):
+        vals = vals_hi if h % 2 else vals_lo
+        s = times(q[:, h * dk : (h + 1) * dk], keys[...]) * scale
+        old = tops[h, :, 0:1]
+        top = jnp.maximum(old, jnp.max(s, axis=1, keepdims=True))
+        fade = jnp.exp(old - top)
+        p = jnp.exp(s - top)
+        total = totals[h, :, 0:1] * fade + jnp.sum(p, axis=1, keepdims=True)
+        return (sums[h] * fade + times(p.astype(jnp.bfloat16), vals[...])) / total
+
+    def spread(h, lo, hi):
+        start = dv * h
+        return (
+            (start, lo[:, : wide - over]),
+            (start + wide - over, lo[:, wide - over :] + hi[:, :over]),
+            (start + wide, hi[:, over:]),
         )
-        return o / total
-
-    over = 2 * wide - 2 * dv
-    for pair in range(HEADS // 2):
-        lo = head(2 * pair, vals_lo)
-        hi = head(2 * pair + 1, vals_hi)
-        first = 2 * dv * pair
-        pieces = (
-            (first, lo[:, : wide - over]),
-            (first + wide - over, lo[:, wide - over :] + hi[:, :over]),
-            (first + wide, hi[:, over:]),
-        )
-        for start, piece in pieces:
+
+    for h in range(0, HEADS, 2):
+        for start, piece in spread(h, head(h), head(h + 1)):
             to = slice(start, start + piece.shape[1])
-            base[:, to] = coarse[:, to] + piece[:rows]
-            att_ends[:, to] = piece[rows : rows + EDGE]
-    keep_left = has_left == 1
-    keep_right = has_right == 1
-    rc_left_at = place[4]
-    rc_right_at = place[5]
+            base[:, to] = coarse[:, to] + piece
+
+    q_edge = jnp.concatenate(
+        [
+            edges[left_at, at["q_last"] : at["q_last"] + HEADS],
+            edges[right_at, at["q_first"] : at["q_first"] + HEADS],
+        ],
+        axis=0,
+    ).astype(q.dtype)
+    s_a = times(q_edge, keys_a[...]) * scale
+    s_b = times(q_edge, keys[...]) * scale
+    top = jnp.maximum(jnp.max(s_a, axis=1, keepdims=True), jnp.max(s_b, axis=1, keepdims=True))
+    p_a, p_b = jnp.exp(s_a - top), jnp.exp(s_b - top)
+    total = jnp.sum(p_a, axis=1, keepdims=True) + jnp.sum(p_b, axis=1, keepdims=True)
+    p_a, p_b = p_a.astype(jnp.bfloat16), p_b.astype(jnp.bfloat16)
+    edge_lo = (times(p_a, lo_a[...]) + times(p_b, vals_lo[...])) / total
+    edge_hi = (times(p_a, hi_a[...]) + times(p_b, vals_hi[...])) / total
+    for side in range(2):
+        for h in range(0, HEADS, 2):
+            i = side * HEADS + h
+            for start, piece in spread(h, edge_lo[i : i + 1], edge_hi[i + 1 : i + 2]):
+                att_ends[side : side + 1, start : start + piece.shape[1]] = piece
+
     last = 2 * rows + EDGE
     for c in range(tiles):
         to = slice(c * LANES, (c + 1) * LANES)
@@ -270,28 +318,24 @@
         compiler_params=limit(4),
     )(far(keys[0]), far(values[0].T), far(q), far(f), far(rc))
 
-    here = lax.axis_index("ctx").astype(jnp.int32)
-    wanted = jnp.stack([here - 1, here + 1, count - here, count - 2 - here])
     if count == 8:
         k4 = swap(own, "ctx", 4)
+        k2a = swap(own, "ctx", 2)
+        k1a = swap(own, "ctx", 1)
         rc_b = swap(rc_b, "ctx", 1)
-        pair = jnp.concatenate([own, k4], axis=0)
-        k2 = swap(pair, "ctx", 2)
-        k1 = swap(pair, "ctx", 1)
         rc_a = swap(rc_a, "ctx", 6)
+        k2b = swap(k4, "ctx", 2)
+        k21a = swap(k2a, "ctx", 1)
+        k1b = swap(k4, "ctx", 1)
         rc_b = swap(rc_b, "ctx", 6)
-        k21 = swap(k2, "ctx", 1)
+        k21b = swap(k2b, "ctx", 1)
         rc_a = swap(rc_a, "ctx", 1)
-        parts = [pair, k2, k1, k21]
-        mask = here ^ wanted
-        wanted = ((mask & 1) * 4) | (mask & 2) | ((mask & 4) // 4)
+        early = [own, k4, k2a, k2b]
+        parts = early + [k1a, k1b, k21a, k21b]
     else:
-        parts = [lax.all_gather(own, "ctx", axis=0, tiled=True)]
+        early = parts = [lax.all_gather(own, "ctx", axis=0, tiled=True)]
         rc_a = swap(rc_a, "ctx", count - 1)
         rc_b = swap(rc_b, "ctx", count - 1)
-    wanted = jnp.clip(wanted, 0, count - 1)
-    ends_of = jnp.stack([here > 0, here < count - 1]).astype(jnp.int32)
-    place = jnp.concatenate([ends_of, wanted])
 
     q_near, w_near, coarse, fine = pl.pallas_call(
         prep_kernel,
@@ -309,26 +353,51 @@
     )(far(q), far(f), far(conv_weight))
 
     wide = pl.cdiv(dv, LANES) * LANES
+    some = count // 2 * rows
+    first = [near(part) for part in early]
+    keys_a, lo_a, hi_a, tops, totals, sums = pl.pallas_call(
+        lambda *refs: first_kernel(*refs, parts=len(early), per=rows, dv=dv, count=extra),
+        name="first",
+        out_shape=(
+            pltpu.VMEM((some, dk), bf16),
+            pltpu.VMEM((wide, some), bf16),
+            pltpu.VMEM((wide, some), bf16),
+            pltpu.VMEM((HEADS, rows, LANES), f32),
+            pltpu.VMEM((HEADS, rows, LANES), f32),
+            pltpu.VMEM((HEADS, rows, wide), f32),
+        ),
+        in_specs=[VMEM] * (1 + len(early)),
+        out_specs=(VMEM,) * 6,
+        compiler_params=limit(16),
+    )(near(q_near), *first)
+
     base, ends, fine = pl.pallas_call(
-        lambda *refs: attend_kernel(*refs, parts=len(parts), per=rows, dv=dv),
+        lambda *refs: attend_kernel(*refs, parts=len(parts), per=rows, dv=dv, ring=count == 8),
         name="attend",
         out_shape=(
             pltpu.VMEM((rows, chans), f32),
             pltpu.VMEM((EDGE, chans), f32),
             pltpu.VMEM((tiles, 2 * rows + 2 * EDGE, LANES), f32),
         ),
-        in_specs=[SMEM] + [VMEM] * (4 + len(parts)),
+        in_specs=[VMEM] * (10 + len(parts)),
         out_specs=(VMEM,) * 3,
         scratch_shapes=[
-            pltpu.VMEM((count * rows, dk), bf16),
-            pltpu.VMEM((wide, count * rows), bf16),
-            pltpu.VMEM((wide, count * rows), bf16),
+            pltpu.VMEM((some, dk), bf16),
+            pltpu.VMEM((wide, some), bf16),
+            pltpu.VMEM((wide, some), bf16),
             pltpu.VMEM((count, extra, LANES), f32),
             pltpu.VMEM((EDGE, chans), f32),
         ],
-        input_output_aliases={3: 0, 4: 2},
-        compiler_params=limit(24),
-    )(place, near(q_near), near(w_near), near(coarse), near(fine), *[near(part) for part in parts])
+        input_output_aliases={2: 0, 3: 2},
+        compiler_params=limit(16),
+    )(
+        near(q_near),
+        near(w_near),
+        near(coarse),
+        near(fine),
+        *[near(x) for x in (keys_a, lo_a, hi_a, tops, totals, sums)],
+        *[near(part) for part in parts],
+    )
 
     partial, grad = pl.pallas_call(
         grad_kernel,

time: 55.9 us -> 58.3 us (1.043)
  waiting for transfers between devices: 18 us -> 20.4 us
    ppermute x14 -> x17, waiting for transfers between devices: 18 us -> 20.4 us  [swap(): lax.ppermute(value, axis, [(i, i ^ mask) for i in range(lax.axis_size(axi...]
    pallas_call x0 -> x1, Pallas kernels: none -> 1.69 us  [body(): pl.pallas_call(lambda *refs: first_kernel(*refs, parts=len(early), per=ro...]
    pallas_call x1, Pallas kernels: 4.06 us -> 2.93 us  [body(): pl.pallas_call(lambda *refs: attend_kernel(*refs, parts=len(parts), per=r...]
    ppermute x14 -> x17, starting transfers between devices: 27.2 us -> 26.9 us  [swap(): lax.ppermute(value, axis, [(i, i ^ mask) for i in range(lax.axis_size(axi...]
  transfers between devices with their start and end apart: 14 -> 17, of which waited for: 10 -> 11; matrix products, arithmetic and copies ran while one was open for 0% -> 0% of each run, Pallas kernels for 13% -> 13%
where the time goes in v4:
time: 58.3 us; the launch traced here: 58.1 us
  starting transfers between devices  26.9 us (46%)
  waiting for transfers between devices  20.4 us (35%)
  Pallas kernels  9.43 us (16%)
  between operations  0.71 us (1%)
  other arithmetic  0.66 us (1%)
    ppermute x17, starting transfers between devices, swap(): lax.ppermute(value, axis, [(i, i ^ mask) for i in range(lax.axis_size(axi...  26.9 us
    ppermute x17, waiting for transfers between devices, swap(): lax.ppermute(value, axis, [(i, i ^ mask) for i in range(lax.axis_size(axi...  20.4 us
    pallas_call x1, Pallas kernels, body(): pl.pallas_call(lambda *refs: attend_kernel(*refs, parts=len(parts), per=r...  2.93 us
    pallas_call x1, Pallas kernels, body(): pl.pallas_call(lambda *refs: first_kernel(*refs, parts=len(early), per=ro...  1.69 us
    pallas_call x1, Pallas kernels, body(): pl.pallas_call(prep_kernel, name='prep', out_shape=(pltpu.VMEM(q.shape, b...  1.66 us
    pallas_call x1, Pallas kernels, body(): pl.pallas_call(fine_kernel, name='fine', out_shape=jax.ShapeDtypeStruct((...  1.37 us
    pallas_call x1, Pallas kernels, body(): pl.pallas_call(pack_kernel, name='pack', out_shape=(pltpu.VMEM((size, LAN...  1.29 us
  transfers between devices with their start and end apart: 17, of which 11 were waited for; matrix products, arithmetic and copies ran while one was open for 0% of the time, Pallas kernels for 13%

profile of v4, /device:TPU:0, one launch (start us, length us, event | category | flops | bytes accessed | tf_op | source)
XLA Modules:
  0.0 58.1 jit_solution(15062667842277112071)
XLA Ops:
  0.6 1.3 %pack.1 = (bf16[448,128]{1,0:T(8,128)(2,1)S(1)}, bf16[48,1536]{1,0:T(8,128)(2,1)S(1)}, bf16[80,1536]{1,0:T(8,128)(2,1)S(1)}) custom-call(bf16[128,128]{1,0:T(8,128)(2,1)} %bitcast.15, bf16[192,128]{1,0:T(8,128)(2,1)} %bitcast.14, bf16[128,1024]{1,0:T(8,128)(2,1)} %bitcast.10, bf16[256,1536]{1,0:T(8,128)(2,1)} %bitcast.8, bf16[128,1536]{1,0:T(8,128)(2,1)} %bitcast.13), custom_call_target="tpu_custom_call" | custom-call | tf_op jit(solution)/shard_map/pack/pallas_call | solution.py:305
  1.9 3.1 %collective-permute-start.9 = (bf16[80,1536]{1,0:T(8,128)(2,1)S(1)}, bf16[80,1536]{1,0:T(8,128)(2,1)S(1)}, u32[]{:S(2)}, u32[]{:S(2)}) collective-permute-start(bf16[80,1536]{1,0:T(8,128)(2,1)S(1)} %get-tuple-element.34), channel_id=1, source_target_pairs={{0,1},{1,0},{2,3},{3,2},{4,5},{5,4},{6,7},{7,6},{8,9},{9,8},{10,11... | collective-permute-start | bytes 737288 | tf_op jit(solution)/shard_map/ppermute | solution.py:279
  5.0 2.6 %collective-permute-start = (bf16[448,128]{1,0:T(8,128)(2,1)S(1)}, bf16[448,128]{1,0:T(8,128)(2,1)S(1)}, u32[]{:S(2)}, u32[]{:S(2)}) collective-permute-start(bf16[448,128]{1,0:T(8,128)(2,1)S(1)} %get-tuple-element.24.refs_1_.refs_10_), channel_id=1, source_target_pairs={{0,4},{1,5},{2,6},{3,7},{4,0},{5,1},{6,2},{7,3},{8,12},{9,13},{10,... | collective-permute-start | bytes 344072 | tf_op jit(solution)/shard_map/ppermute | solution.py:279
  7.6 1.3 %collective-permute-start.7 = (bf16[48,1536]{1,0:T(8,128)(2,1)S(1)}, bf16[48,1536]{1,0:T(8,128)(2,1)S(1)}, u32[]{:S(2)}, u32[]{:S(2)}) collective-permute-start(bf16[48,1536]{1,0:T(8,128)(2,1)S(1)} %get-tuple-element.33), channel_id=1, source_target_pairs={{0,6},{1,7},{2,4},{3,5},{4,2},{5,3},{6,0},{7,1},{8,14},{9,15},{10,... | collective-permute-start | bytes 442376 | tf_op jit(solution)/shard_map/ppermute | solution.py:279
  8.9 2.0 %collective-permute-done.9 = bf16[80,1536]{1,0:T(8,128)(2,1)S(1)} collective-permute-done((bf16[80,1536]{1,0:T(8,128)(2,1)S(1)}, bf16[80,1536]{1,0:T(8,128)(2,1)S(1)}, u32[]{:S(2)}, u32[]{:S(2)}) %collective-permute-start.9) | collective-permute-done | bytes 245792 | tf_op jit(solution)/shard_map/ppermute | solution.py:279
  10.9 3.8 %collective-permute-start.10 = (bf16[80,1536]{1,0:T(8,128)(2,1)S(1)}, bf16[80,1536]{1,0:T(8,128)(2,1)S(1)}, u32[]{:S(2)}, u32[]{:S(2)}) collective-permute-start(bf16[80,1536]{1,0:T(8,128)(2,1)S(1)} %collective-permute-done.9), channel_id=1, source_target_pairs={{0,6},{1,7},{2,4},{3,5},{4,2},{5,3},{6,0},{7,1},{8,14},{9,15},{10,... | collective-permute-start | bytes 737288 | tf_op jit(solution)/shard_map/ppermute | solution.py:279
  14.8 1.5 %collective-permute-start.3 = (bf16[448,128]{1,0:T(8,128)(2,1)S(1)}, bf16[448,128]{1,0:T(8,128)(2,1)S(1)}, u32[]{:S(2)}, u32[]{:S(2)}) collective-permute-start(bf16[448,128]{1,0:T(8,128)(2,1)S(1)} %get-tuple-element.24.refs_1_.refs_10_), channel_id=1, source_target_pairs={{0,1},{1,0},{2,3},{3,2},{4,5},{5,4},{6,7},{7,6},{8,9},{9,8},{10,11... | collective-permute-start | bytes 344072 | tf_op jit(solution)/shard_map/ppermute | solution.py:279
  16.3 0.0 collective-permute-start.1
  16.3 6.2 %collective-permute-done.refs_2_.refs_11_ = bf16[448,128]{1,0:T(8,128)(2,1)S(1)} collective-permute-done((bf16[448,128]{1,0:T(8,128)(2,1)S(1)}, bf16[448,128]{1,0:T(8,128)(2,1)S(1)}, u32[]{:S(2)}, u32[]{:S(2)}) %collective-permute-start) | collective-permute-done | bytes 114720 | tf_op jit(solution)/shard_map/ppermute | solution.py:279
  22.5 0.0 collective-permute-start.2
  22.5 0.0 collective-permute-done.7
  22.5 0.5 collective-permute-start.8
  23.0 0.0 collective-permute-done.3.refs_14_
  23.0 1.5 %collective-permute-start.4 = (bf16[448,128]{1,0:T(8,128)(2,1)S(1)}, bf16[448,128]{1,0:T(8,128)(2,1)S(1)}, u32[]{:S(2)}, u32[]{:S(2)}) collective-permute-start(bf16[448,128]{1,0:T(8,128)(2,1)S(1)} %collective-permute-done.refs_2_.refs_11_), channel_id=1, source_target_pairs={{0,1},{1,0},{2,3},{3,2},{4,5},{5,4},{6,7},{7,6},{8,9},{9,8},{10,11... | collective-permute-start | bytes 344072 | tf_op jit(solution)/shard_map/ppermute | solution.py:279
  24.5 0.0 collective-permute-done.1.refs_3_.refs_12_
  24.5 0.5 collective-permute-start.5
  25.0 2.3 %collective-permute-done.2.refs_4_.refs_13_ = bf16[448,128]{1,0:T(8,128)(2,1)S(1)} collective-permute-done((bf16[448,128]{1,0:T(8,128)(2,1)S(1)}, bf16[448,128]{1,0:T(8,128)(2,1)S(1)}, u32[]{:S(2)}, u32[]{:S(2)}) %collective-permute-start.2) | collective-permute-done | bytes 114720 | tf_op jit(solution)/shard_map/ppermute | solution.py:279
  27.3 0.5 collective-permute-start.6
  27.8 1.7 %prep.1 = (bf16[128,1024]{1,0:T(8,128)(2,1)S(1)}, f32[5,1536]{1,0:T(8,128)S(1)}, f32[128,1536]{1,0:T(8,128)S(1)}, f32[12,272,128]{2,1,0:T(8,128)S(1)}) custom-call(bf16[128,1024]{1,0:T(8,128)(2,1)} %bitcast.11, bf16[256,1536]{1,0:T(8,128)(2,1)} %bitcast.9, f32[5,1536]{1,0:T(8,128)} %w.1), custom_call_target="tpu_custom_call" | custom-call | tf_op jit(solution)/shard_map/prep/pallas_call | solution.py:340
  29.5 1.7 %first.1 = (bf16[512,128]{1,0:T(8,128)(2,1)S(1)}, bf16[256,512]{1,0:T(8,128)(2,1)S(1)}, bf16[256,512]{1,0:T(8,128)(2,1)S(1)}, f32[8,128,128]{2,1,0:T(8,128)S(1)}...) custom-call(bf16[128,1024]{1,0:T(8,128)(2,1)S(1)} %get-tuple-element.20.refs_0_, ...), custom_call_target="tpu_custom_call" | custom-call | tf_op jit(solution)/shard_map/first/pallas_call | solution.py:358
  31.2 1.5 %collective-permute-done.5.refs_16_ = bf16[448,128]{1,0:T(8,128)(2,1)S(1)} collective-permute-done((bf16[448,128]{1,0:T(8,128)(2,1)S(1)}, bf16[448,128]{1,0:T(8,128)(2,1)S(1)}, u32[]{:S(2)}, u32[]{:S(2)}) %collective-permute-start.5) | collective-permute-done | bytes 114720 | tf_op jit(solution)/shard_map/ppermute | solution.py:279
  32.6 0.0 collective-permute-done.4.refs_15_
  32.6 1.2 %collective-permute-done.6.refs_17_ = bf16[448,128]{1,0:T(8,128)(2,1)S(1)} collective-permute-done((bf16[448,128]{1,0:T(8,128)(2,1)S(1)}, bf16[448,128]{1,0:T(8,128)(2,1)S(1)}, u32[]{:S(2)}, u32[]{:S(2)}) %collective-permute-start.6) | collective-permute-done | bytes 114720 | tf_op jit(solution)/shard_map/ppermute | solution.py:279
  33.9 2.9 %attend.1 = (f32[128,1536]{1,0:T(8,128)S(1)}, f32[8,1536]{1,0:T(8,128)S(1)}, f32[12,272,128]{2,1,0:T(8,128)S(1)}) custom-call(bf16[128,1024]{1,0:T(8,128)(2,1)S(1)} %get-tuple-element.20.refs_0_, f32[5,1536]{1,0:T(8,128)S(1)} %get-tuple-element.21.refs_1_.w, ...), custom_call_target="tpu_custom_call", output_to_operand_aliasing={{0}: (2, {}), {2}: (3, {})} | custom-call | tf_op jit(solution)/shard_map/attend/pallas_call | solution.py:374
  36.8 0.0 collective-permute-done.8.rc_a
  36.8 0.0 collective-permute-done.10.rc_b
  36.8 0.5 grad.1
  37.3 0.1 collective-permute-start.11
  37.4 1.2 %collective-permute-done.11 = f32[5,1536]{1,0:T(8,128)S(1)} collective-permute-done((f32[5,1536]{1,0:T(8,128)S(1)}, f32[5,1536]{1,0:T(8,128)S(1)}, u32[]{:S(2)}, u32[]{:S(2)}) %collective-permute-start.11) | collective-permute-done | bytes 30752 | tf_op jit(solution)/shard_map/ppermute | solution.py:279
  38.6 1.5 %collective-permute-start.12 = (f32[5,1536]{1,0:T(8,128)S(1)}, f32[5,1536]{1,0:T(8,128)S(1)}, u32[]{:S(2)}, u32[]{:S(2)}) collective-permute-start(f32[5,1536]{1,0:T(8,128)S(1)} %add.18), channel_id=1, source_target_pairs={{0,16},{8,24},{16,0},{24,8},{1,17},{9,25},{17,1},{25,9},{2,18},{10... | collective-permute-start | bytes 92168 | tf_op jit(solution)/shard_map/ppermute | solution.py:279
  40.2 2.6 %collective-permute-done.12 = f32[5,1536]{1,0:T(8,128)S(1)} collective-permute-done((f32[5,1536]{1,0:T(8,128)S(1)}, f32[5,1536]{1,0:T(8,128)S(1)}, u32[]{:S(2)}, u32[]{:S(2)}) %collective-permute-start.12) | collective-permute-done | bytes 30752 | tf_op jit(solution)/shard_map/ppermute | solution.py:279
  42.8 4.5 %collective-permute-start.15 = (f32[5,1536]{1,0:T(8,128)S(1)}, f32[5,1536]{1,0:T(8,128)S(1)}, u32[]{:S(2)}, u32[]{:S(2)}) collective-permute-start(f32[5,1536]{1,0:T(8,128)S(1)} %add.19), channel_id=1, source_target_pairs={{0,3},{1,2},{2,1},{3,0},{4,7},{5,6},{6,5},{7,4},{8,11},{9,10},{10,... | collective-permute-start | bytes 92168 | tf_op jit(solution)/shard_map/ppermute | solution.py:279
  47.3 0.1 collective-permute-start.14
  47.4 1.4 %collective-permute-start.13 = (f32[5,1536]{1,0:T(8,128)S(1)}, f32[5,1536]{1,0:T(8,128)S(1)}, u32[]{:S(2)}, u32[]{:S(2)}) collective-permute-start(f32[5,1536]{1,0:T(8,128)S(1)} %add.19), channel_id=1, source_target_pairs={{0,1},{1,0},{2,3},{3,2},{4,5},{5,4},{6,7},{7,6},{8,9},{9,8},{10,11... | collective-permute-start | bytes 92168 | tf_op jit(solution)/shard_map/ppermute | solution.py:279
  48.8 0.7 %collective-permute-done.15 = f32[5,1536]{1,0:T(8,128)S(1)} collective-permute-done((f32[5,1536]{1,0:T(8,128)S(1)}, f32[5,1536]{1,0:T(8,128)S(1)}, u32[]{:S(2)}, u32[]{:S(2)}) %collective-permute-start.15) | collective-permute-done | bytes 30752 | tf_op jit(solution)/shard_map/ppermute | solution.py:279
  49.5 1.9 %collective-permute-done.14 = f32[5,1536]{1,0:T(8,128)S(1)} collective-permute-done((f32[5,1536]{1,0:T(8,128)S(1)}, f32[5,1536]{1,0:T(8,128)S(1)}, u32[]{:S(2)}, u32[]{:S(2)}) %collective-permute-start.14) | collective-permute-done | bytes 30752 | tf_op jit(solution)/shard_map/ppermute | solution.py:279
  51.4 0.1 collective-permute-done.13
  51.6 3.9 %collective-permute-start.16 = (f32[5,1536]{1,0:T(8,128)S(1)}, f32[5,1536]{1,0:T(8,128)S(1)}, u32[]{:S(2)}, u32[]{:S(2)}) collective-permute-start(f32[5,1536]{1,0:T(8,128)S(1)} %add_add_fusion), channel_id=1, source_target_pairs={{0,4},{1,5},{2,6},{3,7},{4,0},{5,1},{6,2},{7,3},{8,12},{9,13},{10,... | collective-permute-start | bytes 92168 | tf_op jit(solution)/shard_map/ppermute | solution.py:279
  55.4 1.4 %fine.1 = bf16[256,1536]{1,0:T(8,128)(2,1)} custom-call(f32[128,1536]{1,0:T(8,128)S(1)} %get-tuple-element.35.grad, f32[8,1536]{1,0:T(8,128)S(1)} %get-tuple-element.36.ends, f32[5,1536]{1,0:T(8,128)S(1)} %get-tuple-element.21.refs_1_.w), custom_call_target="tpu_custom_call" | custom-call | tf_op jit(solution)/shard_map/fine/pallas_call | solution.py:411
  56.8 0.7 %collective-permute-done.16 = f32[5,1536]{1,0:T(8,128)S(1)} collective-permute-done((f32[5,1536]{1,0:T(8,128)S(1)}, f32[5,1536]{1,0:T(8,128)S(1)}, u32[]{:S(2)}, u32[]{:S(2)}) %collective-permute-start.16) | collective-permute-done | bytes 30752 | tf_op jit(solution)/shard_map/ppermute | solution.py:279
  57.5 0.6 %add_multiply_fusion = f32[5,1536]{1,0:T(8,128)} fusion(f32[5,1536]{1,0:T(8,128)S(1)} %add_add_fusion, f32[5,1536]{1,0:T(8,128)S(1)} %collective-permute-done.16), kind=kLoop, calls=%fused_computation | loop fusion | flops 15360 | bytes 92160 | tf_op jit(solution)/shard_map/mul | solution.py:434
  (3 shorter events, 0.0 us)
Async XLA Ops:
  1.9 9.0 %collective-permute-start.9 = (bf16[80,1536]{1,0:T(8,128)(2,1)S(1)}, bf16[80,1536]{1,0:T(8,128)(2,1)S(1)}, u32[]{:S(2)}, u32[]{:S(2)}) collective-permute-start(bf16[80,1536]{1,0:T(8,128)(2,1)S(1)} %get-tuple-element.34), channel_id=1, source_target_pairs={{0,1},{1,0},{2,3},{3,2},{4,5},{5,4},{6,7},{7,6},{8,9},{9,8},{10,11... | collective-permute-start | bytes 737288 | tf_op jit(solution)/shard_map/ppermute | solution.py:279
  5.0 17.5 %collective-permute-start = (bf16[448,128]{1,0:T(8,128)(2,1)S(1)}, bf16[448,128]{1,0:T(8,128)(2,1)S(1)}, u32[]{:S(2)}, u32[]{:S(2)}) collective-permute-start(bf16[448,128]{1,0:T(8,128)(2,1)S(1)} %get-tuple-element.24.refs_1_.refs_10_), channel_id=1, source_target_pairs={{0,4},{1,5},{2,6},{3,7},{4,0},{5,1},{6,2},{7,3},{8,12},{9,13},{10,... | collective-permute-start | bytes 344072 | tf_op jit(solution)/shard_map/ppermute | solution.py:279
  7.6 14.9 %collective-permute-start.7 = (bf16[48,1536]{1,0:T(8,128)(2,1)S(1)}, bf16[48,1536]{1,0:T(8,128)(2,1)S(1)}, u32[]{:S(2)}, u32[]{:S(2)}) collective-permute-start(bf16[48,1536]{1,0:T(8,128)(2,1)S(1)} %get-tuple-element.33), channel_id=1, source_target_pairs={{0,6},{1,7},{2,4},{3,5},{4,2},{5,3},{6,0},{7,1},{8,14},{9,15},{10,... | collective-permute-start | bytes 442376 | tf_op jit(solution)/shard_map/ppermute | solution.py:279
  10.9 25.9 %collective-permute-start.10 = (bf16[80,1536]{1,0:T(8,128)(2,1)S(1)}, bf16[80,1536]{1,0:T(8,128)(2,1)S(1)}, u32[]{:S(2)}, u32[]{:S(2)}) collective-permute-start(bf16[80,1536]{1,0:T(8,128)(2,1)S(1)} %collective-permute-done.9), channel_id=1, source_target_pairs={{0,6},{1,7},{2,4},{3,5},{4,2},{5,3},{6,0},{7,1},{8,14},{9,15},{10,... | collective-permute-start | bytes 737288 | tf_op jit(solution)/shard_map/ppermute | solution.py:279
  14.8 8.2 %collective-permute-start.3 = (bf16[448,128]{1,0:T(8,128)(2,1)S(1)}, bf16[448,128]{1,0:T(8,128)(2,1)S(1)}, u32[]{:S(2)}, u32[]{:S(2)}) collective-permute-start(bf16[448,128]{1,0:T(8,128)(2,1)S(1)} %get-tuple-element.24.refs_1_.refs_10_), channel_id=1, source_target_pairs={{0,1},{1,0},{2,3},{3,2},{4,5},{5,4},{6,7},{7,6},{8,9},{9,8},{10,11... | collective-permute-start | bytes 344072 | tf_op jit(solution)/shard_map/ppermute | solution.py:279
  16.3 8.3 %collective-permute-start.1 = (bf16[448,128]{1,0:T(8,128)(2,1)S(1)}, bf16[448,128]{1,0:T(8,128)(2,1)S(1)}, u32[]{:S(2)}, u32[]{:S(2)}) collective-permute-start(bf16[448,128]{1,0:T(8,128)(2,1)S(1)} %get-tuple-element.24.refs_1_.refs_10_), channel_id=1, source_target_pairs={{0,2},{1,3},{2,0},{3,1},{4,6},{5,7},{6,4},{7,5},{8,10},{9,11},{10,... | collective-permute-start | bytes 344072 | tf_op jit(solution)/shard_map/ppermute | solution.py:279
  22.5 4.8 %collective-permute-start.2 = (bf16[448,128]{1,0:T(8,128)(2,1)S(1)}, bf16[448,128]{1,0:T(8,128)(2,1)S(1)}, u32[]{:S(2)}, u32[]{:S(2)}) collective-permute-start(bf16[448,128]{1,0:T(8,128)(2,1)S(1)} %collective-permute-done.refs_2_.refs_11_), channel_id=1, source_target_pairs={{0,2},{1,3},{2,0},{3,1},{4,6},{5,7},{6,4},{7,5},{8,10},{9,11},{10,... | collective-permute-start | bytes 344072 | tf_op jit(solution)/shard_map/ppermute | solution.py:279
  22.5 14.3 %collective-permute-start.8 = (bf16[48,1536]{1,0:T(8,128)(2,1)S(1)}, bf16[48,1536]{1,0:T(8,128)(2,1)S(1)}, u32[]{:S(2)}, u32[]{:S(2)}) collective-permute-start(bf16[48,1536]{1,0:T(8,128)(2,1)S(1)} %collective-permute-done.7), channel_id=1, source_target_pairs={{0,1},{1,0},{2,3},{3,2},{4,5},{5,4},{6,7},{7,6},{8,9},{9,8},{10,11... | collective-permute-start | bytes 442376 | tf_op jit(solution)/shard_map/ppermute | solution.py:279
  23.0 9.6 %collective-permute-start.4 = (bf16[448,128]{1,0:T(8,128)(2,1)S(1)}, bf16[448,128]{1,0:T(8,128)(2,1)S(1)}, u32[]{:S(2)}, u32[]{:S(2)}) collective-permute-start(bf16[448,128]{1,0:T(8,128)(2,1)S(1)} %collective-permute-done.refs_2_.refs_11_), channel_id=1, source_target_pairs={{0,1},{1,0},{2,3},{3,2},{4,5},{5,4},{6,7},{7,6},{8,9},{9,8},{10,11... | collective-permute-start | bytes 344072 | tf_op jit(solution)/shard_map/ppermute | solution.py:279
  24.5 8.1 %collective-permute-start.5 = (bf16[448,128]{1,0:T(8,128)(2,1)S(1)}, bf16[448,128]{1,0:T(8,128)(2,1)S(1)}, u32[]{:S(2)}, u32[]{:S(2)}) collective-permute-start(bf16[448,128]{1,0:T(8,128)(2,1)S(1)} %collective-permute-done.1.refs_3_.refs_12_), channel_id=1, source_target_pairs={{0,1},{1,0},{2,3},{3,2},{4,5},{5,4},{6,7},{7,6},{8,9},{9,8},{10,11... | collective-permute-start | bytes 344072 | tf_op jit(solution)/shard_map/ppermute | solution.py:279
  27.3 6.6 %collective-permute-start.6 = (bf16[448,128]{1,0:T(8,128)(2,1)S(1)}, bf16[448,128]{1,0:T(8,128)(2,1)S(1)}, u32[]{:S(2)}, u32[]{:S(2)}) collective-permute-start(bf16[448,128]{1,0:T(8,128)(2,1)S(1)} %collective-permute-done.2.refs_4_.refs_13_), channel_id=1, source_target_pairs={{0,1},{1,0},{2,3},{3,2},{4,5},{5,4},{6,7},{7,6},{8,9},{9,8},{10,11... | collective-permute-start | bytes 344072 | tf_op jit(solution)/shard_map/ppermute | solution.py:279
  37.3 1.3 %collective-permute-start.11 = (f32[5,1536]{1,0:T(8,128)S(1)}, f32[5,1536]{1,0:T(8,128)S(1)}, u32[]{:S(2)}, u32[]{:S(2)}) collective-permute-start(f32[5,1536]{1,0:T(8,128)S(1)} %get-tuple-element.37), channel_id=1, source_target_pairs={{0,8},{8,0},{16,24},{24,16},{1,9},{9,1},{17,25},{25,17},{2,10},{10... | collective-permute-start | bytes 92168 | tf_op jit(solution)/shard_map/ppermute | solution.py:279
  38.6 4.2 %collective-permute-start.12 = (f32[5,1536]{1,0:T(8,128)S(1)}, f32[5,1536]{1,0:T(8,128)S(1)}, u32[]{:S(2)}, u32[]{:S(2)}) collective-permute-start(f32[5,1536]{1,0:T(8,128)S(1)} %add.18), channel_id=1, source_target_pairs={{0,16},{8,24},{16,0},{24,8},{1,17},{9,25},{17,1},{25,9},{2,18},{10... | collective-permute-start | bytes 92168 | tf_op jit(solution)/shard_map/ppermute | solution.py:279
  42.8 6.7 %collective-permute-start.15 = (f32[5,1536]{1,0:T(8,128)S(1)}, f32[5,1536]{1,0:T(8,128)S(1)}, u32[]{:S(2)}, u32[]{:S(2)}) collective-permute-start(f32[5,1536]{1,0:T(8,128)S(1)} %add.19), channel_id=1, source_target_pairs={{0,3},{1,2},{2,1},{3,0},{4,7},{5,6},{6,5},{7,4},{8,11},{9,10},{10,... | collective-permute-start | bytes 92168 | tf_op jit(solution)/shard_map/ppermute | solution.py:279
  47.3 4.1 %collective-permute-start.14 = (f32[5,1536]{1,0:T(8,128)S(1)}, f32[5,1536]{1,0:T(8,128)S(1)}, u32[]{:S(2)}, u32[]{:S(2)}) collective-permute-start(f32[5,1536]{1,0:T(8,128)S(1)} %add.19), channel_id=1, source_target_pairs={{0,2},{1,3},{2,0},{3,1},{4,6},{5,7},{6,4},{7,5},{8,10},{9,11},{10,... | collective-permute-start | bytes 92168 | tf_op jit(solution)/shard_map/ppermute | solution.py:279
  47.4 4.1 %collective-permute-start.13 = (f32[5,1536]{1,0:T(8,128)S(1)}, f32[5,1536]{1,0:T(8,128)S(1)}, u32[]{:S(2)}, u32[]{:S(2)}) collective-permute-start(f32[5,1536]{1,0:T(8,128)S(1)} %add.19), channel_id=1, source_target_pairs={{0,1},{1,0},{2,3},{3,2},{4,5},{5,4},{6,7},{7,6},{8,9},{9,8},{10,11... | collective-permute-start | bytes 92168 | tf_op jit(solution)/shard_map/ppermute | solution.py:279
  51.6 6.0 %collective-permute-start.16 = (f32[5,1536]{1,0:T(8,128)S(1)}, f32[5,1536]{1,0:T(8,128)S(1)}, u32[]{:S(2)}, u32[]{:S(2)}) collective-permute-start(f32[5,1536]{1,0:T(8,128)S(1)} %add_add_fusion), channel_id=1, source_target_pairs={{0,4},{1,5},{2,6},{3,7},{4,0},{5,1},{6,2},{7,3},{8,12},{9,13},{10,... | collective-permute-start | bytes 92168 | tf_op jit(solution)/shard_map/ppermute | solution.py:279

commit v5 on v4

--- a/solution.py
+++ b/solution.py
@@ -15,7 +15,7 @@
 TAIL = 4
 HEAD = 3
 TILE = 16
-CUT = 3
+CUT = 7
 VMEM = pl.BlockSpec(memory_space=pltpu.VMEM)
 HBM = pl.BlockSpec(memory_space=pltpu.HBM)
 SMEM = pl.BlockSpec(memory_space=pltpu.SMEM)
@@ -160,7 +160,10 @@
         if not ring:
             return jnp.clip(other, 0, total_blocks - 1)
         mask = (here ^ other) & (total_blocks - 1)
-        return ((mask & 1) * 4) | (mask & 2) | ((mask & 4) // 4)
+        found = jnp.int32(0)
+        for i, of in enumerate((0, 4, 2, 1, 6, 3, 5, 7)):
+            found = jnp.where(mask == of, jnp.int32(i), found)
+        return found
 
     keep_left = here > 0
     keep_right = here < total_blocks - 1
@@ -296,7 +299,7 @@
     q, f, rc = queries[0], features_fine[0], rc_state[0]
     rows, chans = rc.shape
     tiles = chans // LANES
-    cut = rows * CUT // 8
+    cut = rows * CUT // 16
     dk, dv = keys.shape[2], values.shape[2]
     _, extra = edge_rows(tiles, HEADS)
     size = rows + dv + extra
@@ -330,8 +333,8 @@
         rc_b = swap(rc_b, "ctx", 6)
         k21b = swap(k2b, "ctx", 1)
         rc_a = swap(rc_a, "ctx", 1)
-        early = [own, k4, k2a, k2b]
-        parts = early + [k1a, k1b, k21a, k21b]
+        early = [own, k4, k2a, k1a]
+        parts = early + [k2b, k21a, k1b, k21b]
     else:
         early = parts = [lax.all_gather(own, "ctx", axis=0, tiled=True)]
         rc_a = swap(rc_a, "ctx", count - 1)
@@ -422,13 +425,12 @@
     )(near(grad), near(ends), near(w_near))
 
     total = partial
-    if count == 8:
-        rounds = [("dp", (1 << b,)) for b in range(lax.axis_size("dp").bit_length() - 1)]
-        rounds += [("ctx", (1, 2, 3)), ("ctx", (4,))]
+    if count == 8 and lax.axis_size("dp") == 4:
+        rounds = ((8,), (16, 1, 17), (2, 4, 6))
     else:
-        rounds = [(a, (1 << b,)) for a in ("dp", "ctx") for b in range(lax.axis_size(a).bit_length() - 1)]
-    for axis, masks in rounds:
-        got = [swap(total, axis, mask) for mask in masks]
+        rounds = [(1 << b,) for b in range((lax.axis_size("dp") * count).bit_length() - 1)]
+    for masks in rounds:
+        got = [swap(total, ("dp", "ctx"), mask) for mask in masks]
         total = sum(got, total)
     scale = 1.0 / math.sqrt(lax.axis_size("dp") * rows * count)
     return (d_fine[None], total * scale)
@@ -444,4 +446,6 @@
         P(),
     )
 
-    return jax.shard_map(body, mesh=mesh, in_specs=placed, out_specs=(P("dp", "ctx", None), P()), check_vma=False)
+    return jax.shard_map(
+        body, mesh=mesh, in_specs=placed, out_specs=(P("dp", "ctx", None), P()), check_vma=False
+    )

time: 58.3 us -> 53.6 us (0.919)
  starting transfers between devices: 26.9 us -> 22.3 us
    ppermute x17 -> x18, starting transfers between devices: 26.9 us -> 22.3 us  [swap(): lax.ppermute(value, axis, [(i, i ^ mask) for i in range(lax.axis_size(axi...]
    ppermute x17 -> x18, waiting for transfers between devices: 20.4 us -> 20.2 us  [swap(): lax.ppermute(value, axis, [(i, i ^ mask) for i in range(lax.axis_size(axi...]
  transfers between devices with their start and end apart: 17 -> 18, of which waited for: 11 -> 10; matrix products, arithmetic and copies ran while one was open for 0% -> 0% of each run, Pallas kernels for 13% -> 14%
where the time goes in v5:
time: 53.6 us; the launch traced here: 53.4 us
  starting transfers between devices  22.3 us (42%)
  waiting for transfers between devices  20.2 us (38%)
  Pallas kernels  9.46 us (18%)
  between operations  0.71 us (1%)
  other arithmetic  0.66 us (1%)
    ppermute x18, starting transfers between devices, swap(): lax.ppermute(value, axis, [(i, i ^ mask) for i in range(lax.axis_size(axi...  22.3 us
    ppermute x18, waiting for transfers between devices, swap(): lax.ppermute(value, axis, [(i, i ^ mask) for i in range(lax.axis_size(axi...  20.2 us
    pallas_call x1, Pallas kernels, body(): pl.pallas_call(lambda *refs: attend_kernel(*refs, parts=len(parts), per=r...  2.92 us
    pallas_call x1, Pallas kernels, body(): pl.pallas_call(lambda *refs: first_kernel(*refs, parts=len(early), per=ro...  1.7 us
    pallas_call x1, Pallas kernels, body(): pl.pallas_call(prep_kernel, name='prep', out_shape=(pltpu.VMEM(q.shape, b...  1.66 us
    pallas_call x1, Pallas kernels, body(): pl.pallas_call(fine_kernel, name='fine', out_shape=jax.ShapeDtypeStruct((...  1.37 us
    pallas_call x1, Pallas kernels, body(): pl.pallas_call(pack_kernel, name='pack', out_shape=(pltpu.VMEM((size, LAN...  1.29 us
  transfers between devices with their start and end apart: 18, of which 10 were waited for; matrix products, arithmetic and copies ran while one was open for 0% of the time, Pallas kernels for 14%

profile of v5, /device:TPU:0, one launch (start us, length us, event | category | flops | bytes accessed | tf_op | source)
XLA Modules:
  0.0 53.4 jit_solution(17340968981728997032)
XLA Ops:
  0.6 1.3 %pack.1 = (bf16[448,128]{1,0:T(8,128)(2,1)S(1)}, bf16[56,1536]{1,0:T(8,128)(2,1)S(1)}, bf16[72,1536]{1,0:T(8,128)(2,1)S(1)}) custom-call(bf16[128,128]{1,0:T(8,128)(2,1)} %bitcast.15, bf16[192,128]{1,0:T(8,128)(2,1)} %bitcast.14, bf16[128,1024]{1,0:T(8,128)(2,1)} %bitcast.10, bf16[256,1536]{1,0:T(8,128)(2,1)} %bitcast.8, bf16[128,1536]{1,0:T(8,128)(2,1)} %bitcast.13), custom_call_target="tpu_custom_call" | custom-call | tf_op jit(solution)/shard_map/pack/pallas_call | solution.py:308
  1.9 3.1 %collective-permute-start.9 = (bf16[72,1536]{1,0:T(8,128)(2,1)S(1)}, bf16[72,1536]{1,0:T(8,128)(2,1)S(1)}, u32[]{:S(2)}, u32[]{:S(2)}) collective-permute-start(bf16[72,1536]{1,0:T(8,128)(2,1)S(1)} %get-tuple-element.34), channel_id=1, source_target_pairs={{0,1},{1,0},{2,3},{3,2},{4,5},{5,4},{6,7},{7,6},{8,9},{9,8},{10,11... | collective-permute-start | bytes 663560 | tf_op jit(solution)/shard_map/ppermute | solution.py:282
  5.0 2.6 %collective-permute-start = (bf16[448,128]{1,0:T(8,128)(2,1)S(1)}, bf16[448,128]{1,0:T(8,128)(2,1)S(1)}, u32[]{:S(2)}, u32[]{:S(2)}) collective-permute-start(bf16[448,128]{1,0:T(8,128)(2,1)S(1)} %get-tuple-element.24.refs_1_.refs_10_), channel_id=1, source_target_pairs={{0,4},{1,5},{2,6},{3,7},{4,0},{5,1},{6,2},{7,3},{8,12},{9,13},{10,... | collective-permute-start | bytes 344072 | tf_op jit(solution)/shard_map/ppermute | solution.py:282
  7.6 1.3 %collective-permute-start.7 = (bf16[56,1536]{1,0:T(8,128)(2,1)S(1)}, bf16[56,1536]{1,0:T(8,128)(2,1)S(1)}, u32[]{:S(2)}, u32[]{:S(2)}) collective-permute-start(bf16[56,1536]{1,0:T(8,128)(2,1)S(1)} %get-tuple-element.33), channel_id=1, source_target_pairs={{0,6},{1,7},{2,4},{3,5},{4,2},{5,3},{6,0},{7,1},{8,14},{9,15},{10,... | collective-permute-start | bytes 516104 | tf_op jit(solution)/shard_map/ppermute | solution.py:282
  8.9 0.5 collective-permute-start.2
  9.4 0.2 collective-permute-start.1
  9.7 8.1 %collective-permute-done.refs_2_.refs_11_ = bf16[448,128]{1,0:T(8,128)(2,1)S(1)} collective-permute-done((bf16[448,128]{1,0:T(8,128)(2,1)S(1)}, bf16[448,128]{1,0:T(8,128)(2,1)S(1)}, u32[]{:S(2)}, u32[]{:S(2)}) %collective-permute-start) | collective-permute-done | bytes 114720 | tf_op jit(solution)/shard_map/ppermute | solution.py:282
  17.8 0.0 collective-permute-start.3
  17.8 0.0 collective-permute-done.9
  17.8 2.5 %collective-permute-start.10 = (bf16[72,1536]{1,0:T(8,128)(2,1)S(1)}, bf16[72,1536]{1,0:T(8,128)(2,1)S(1)}, u32[]{:S(2)}, u32[]{:S(2)}) collective-permute-start(bf16[72,1536]{1,0:T(8,128)(2,1)S(1)} %collective-permute-done.9), channel_id=1, source_target_pairs={{0,6},{1,7},{2,4},{3,5},{4,2},{5,3},{6,0},{7,1},{8,14},{9,15},{10,... | collective-permute-start | bytes 663560 | tf_op jit(solution)/shard_map/ppermute | solution.py:282
  20.3 0.0 collective-permute-done.7
  20.3 0.5 collective-permute-start.8
  20.8 0.0 collective-permute-done.2.refs_4_.refs_13_
  20.8 1.5 %collective-permute-start.5 = (bf16[448,128]{1,0:T(8,128)(2,1)S(1)}, bf16[448,128]{1,0:T(8,128)(2,1)S(1)}, u32[]{:S(2)}, u32[]{:S(2)}) collective-permute-start(bf16[448,128]{1,0:T(8,128)(2,1)S(1)} %collective-permute-done.refs_2_.refs_11_), channel_id=1, source_target_pairs={{0,1},{1,0},{2,3},{3,2},{4,5},{5,4},{6,7},{7,6},{8,9},{9,8},{10,11... | collective-permute-start | bytes 344072 | tf_op jit(solution)/shard_map/ppermute | solution.py:282
  22.3 0.0 collective-permute-done.1.refs_3_.refs_12_
  22.3 0.5 collective-permute-start.4
  22.8 0.0 collective-permute-done.3.refs_14_
  22.8 1.5 %collective-permute-start.6 = (bf16[448,128]{1,0:T(8,128)(2,1)S(1)}, bf16[448,128]{1,0:T(8,128)(2,1)S(1)}, u32[]{:S(2)}, u32[]{:S(2)}) collective-permute-start(bf16[448,128]{1,0:T(8,128)(2,1)S(1)} %collective-permute-done.3.refs_14_), channel_id=1, source_target_pairs={{0,1},{1,0},{2,3},{3,2},{4,5},{5,4},{6,7},{7,6},{8,9},{9,8},{10,11... | collective-permute-start | bytes 344072 | tf_op jit(solution)/shard_map/ppermute | solution.py:282
  24.3 1.7 %prep.1 = (bf16[128,1024]{1,0:T(8,128)(2,1)S(1)}, f32[5,1536]{1,0:T(8,128)S(1)}, f32[128,1536]{1,0:T(8,128)S(1)}, f32[12,272,128]{2,1,0:T(8,128)S(1)}) custom-call(bf16[128,1024]{1,0:T(8,128)(2,1)} %bitcast.11, bf16[256,1536]{1,0:T(8,128)(2,1)} %bitcast.9, f32[5,1536]{1,0:T(8,128)} %w.1), custom_call_target="tpu_custom_call" | custom-call | tf_op jit(solution)/shard_map/prep/pallas_call | solution.py:343
  26.0 1.7 %first.1 = (bf16[512,128]{1,0:T(8,128)(2,1)S(1)}, bf16[256,512]{1,0:T(8,128)(2,1)S(1)}, bf16[256,512]{1,0:T(8,128)(2,1)S(1)}, f32[8,128,128]{2,1,0:T(8,128)S(1)}...) custom-call(bf16[128,1024]{1,0:T(8,128)(2,1)S(1)} %get-tuple-element.20.refs_0_, ...), custom_call_target="tpu_custom_call" | custom-call | tf_op jit(solution)/shard_map/first/pallas_call | solution.py:361
  27.7 4.6 %collective-permute-done.4.refs_15_ = bf16[448,128]{1,0:T(8,128)(2,1)S(1)} collective-permute-done((bf16[448,128]{1,0:T(8,128)(2,1)S(1)}, bf16[448,128]{1,0:T(8,128)(2,1)S(1)}, u32[]{:S(2)}, u32[]{:S(2)}) %collective-permute-start.4) | collective-permute-done | bytes 114720 | tf_op jit(solution)/shard_map/ppermute | solution.py:282
  32.3 0.0 collective-permute-done.5.refs_16_
  32.4 1.2 %collective-permute-done.6.refs_17_ = bf16[448,128]{1,0:T(8,128)(2,1)S(1)} collective-permute-done((bf16[448,128]{1,0:T(8,128)(2,1)S(1)}, bf16[448,128]{1,0:T(8,128)(2,1)S(1)}, u32[]{:S(2)}, u32[]{:S(2)}) %collective-permute-start.6) | collective-permute-done | bytes 114720 | tf_op jit(solution)/shard_map/ppermute | solution.py:282
  33.6 2.9 %attend.1 = (f32[128,1536]{1,0:T(8,128)S(1)}, f32[8,1536]{1,0:T(8,128)S(1)}, f32[12,272,128]{2,1,0:T(8,128)S(1)}) custom-call(bf16[128,1024]{1,0:T(8,128)(2,1)S(1)} %get-tuple-element.20.refs_0_, f32[5,1536]{1,0:T(8,128)S(1)} %get-tuple-element.21.refs_1_.w, ...), custom_call_target="tpu_custom_call", output_to_operand_aliasing={{0}: (2, {}), {2}: (3, {})} | custom-call | tf_op jit(solution)/shard_map/attend/pallas_call | solution.py:377
  36.5 0.0 collective-permute-done.8.rc_a
  36.5 0.0 collective-permute-done.10.rc_b
  36.5 0.5 grad.1
  37.1 0.1 collective-permute-start.11
  37.1 1.2 %collective-permute-done.11 = f32[5,1536]{1,0:T(8,128)S(1)} collective-permute-done((f32[5,1536]{1,0:T(8,128)S(1)}, f32[5,1536]{1,0:T(8,128)S(1)}, u32[]{:S(2)}, u32[]{:S(2)}) %collective-permute-start.11) | collective-permute-done | bytes 30752 | tf_op jit(solution)/shard_map/ppermute | solution.py:282
  38.4 1.5 %collective-permute-start.14 = (f32[5,1536]{1,0:T(8,128)S(1)}, f32[5,1536]{1,0:T(8,128)S(1)}, u32[]{:S(2)}, u32[]{:S(2)}) collective-permute-start(f32[5,1536]{1,0:T(8,128)S(1)} %add.21), channel_id=1, source_target_pairs={{0,17},{1,16},{2,19},{3,18},{4,21},{5,20},{6,23},{7,22},{8,25},{9,... | collective-permute-start | bytes 92168 | tf_op jit(solution)/shard_map/ppermute | solution.py:282
  39.9 1.5 %collective-permute-start.13 = (f32[5,1536]{1,0:T(8,128)S(1)}, f32[5,1536]{1,0:T(8,128)S(1)}, u32[]{:S(2)}, u32[]{:S(2)}) collective-permute-start(f32[5,1536]{1,0:T(8,128)S(1)} %add.21), channel_id=1, source_target_pairs={{0,1},{1,0},{2,3},{3,2},{4,5},{5,4},{6,7},{7,6},{8,9},{9,8},{10,11... | collective-permute-start | bytes 92168 | tf_op jit(solution)/shard_map/ppermute | solution.py:282
  41.4 0.5 %collective-permute-start.12 = (f32[5,1536]{1,0:T(8,128)S(1)}, f32[5,1536]{1,0:T(8,128)S(1)}, u32[]{:S(2)}, u32[]{:S(2)}) collective-permute-start(f32[5,1536]{1,0:T(8,128)S(1)} %add.21), channel_id=1, source_target_pairs={{0,16},{1,17},{2,18},{3,19},{4,20},{5,21},{6,22},{7,23},{8,24},{9,... | collective-permute-start | bytes 92168 | tf_op jit(solution)/shard_map/ppermute | solution.py:282
  41.9 1.5 %collective-permute-done.14 = f32[5,1536]{1,0:T(8,128)S(1)} collective-permute-done((f32[5,1536]{1,0:T(8,128)S(1)}, f32[5,1536]{1,0:T(8,128)S(1)}, u32[]{:S(2)}, u32[]{:S(2)}) %collective-permute-start.14) | collective-permute-done | bytes 30752 | tf_op jit(solution)/shard_map/ppermute | solution.py:282
  43.4 0.7 %collective-permute-done.13 = f32[5,1536]{1,0:T(8,128)S(1)} collective-permute-done((f32[5,1536]{1,0:T(8,128)S(1)}, f32[5,1536]{1,0:T(8,128)S(1)}, u32[]{:S(2)}, u32[]{:S(2)}) %collective-permute-start.13) | collective-permute-done | bytes 30752 | tf_op jit(solution)/shard_map/ppermute | solution.py:282
  44.1 1.3 %collective-permute-done.12 = f32[5,1536]{1,0:T(8,128)S(1)} collective-permute-done((f32[5,1536]{1,0:T(8,128)S(1)}, f32[5,1536]{1,0:T(8,128)S(1)}, u32[]{:S(2)}, u32[]{:S(2)}) %collective-permute-start.12) | collective-permute-done | bytes 30752 | tf_op jit(solution)/shard_map/ppermute | solution.py:282
  45.5 1.3 %collective-permute-start.17 = (f32[5,1536]{1,0:T(8,128)S(1)}, f32[5,1536]{1,0:T(8,128)S(1)}, u32[]{:S(2)}, u32[]{:S(2)}) collective-permute-start(f32[5,1536]{1,0:T(8,128)S(1)} %add_add_fusion), channel_id=1, source_target_pairs={{0,6},{1,7},{2,4},{3,5},{4,2},{5,3},{6,0},{7,1},{8,14},{9,15},{10,... | collective-permute-start | bytes 92168 | tf_op jit(solution)/shard_map/ppermute | solution.py:282
  46.7 1.9 %collective-permute-start.16 = (f32[5,1536]{1,0:T(8,128)S(1)}, f32[5,1536]{1,0:T(8,128)S(1)}, u32[]{:S(2)}, u32[]{:S(2)}) collective-permute-start(f32[5,1536]{1,0:T(8,128)S(1)} %add_add_fusion), channel_id=1, source_target_pairs={{0,4},{1,5},{2,6},{3,7},{4,0},{5,1},{6,2},{7,3},{8,12},{9,13},{10,... | collective-permute-start | bytes 92168 | tf_op jit(solution)/shard_map/ppermute | solution.py:282
  48.7 1.2 %collective-permute-start.15 = (f32[5,1536]{1,0:T(8,128)S(1)}, f32[5,1536]{1,0:T(8,128)S(1)}, u32[]{:S(2)}, u32[]{:S(2)}) collective-permute-start(f32[5,1536]{1,0:T(8,128)S(1)} %add_add_fusion), channel_id=1, source_target_pairs={{0,2},{1,3},{2,0},{3,1},{4,6},{5,7},{6,4},{7,5},{8,10},{9,11},{10,... | collective-permute-start | bytes 92168 | tf_op jit(solution)/shard_map/ppermute | solution.py:282
  49.9 1.4 %fine.1 = bf16[256,1536]{1,0:T(8,128)(2,1)} custom-call(f32[128,1536]{1,0:T(8,128)S(1)} %get-tuple-element.35.grad, f32[8,1536]{1,0:T(8,128)S(1)} %get-tuple-element.36.ends, f32[5,1536]{1,0:T(8,128)S(1)} %get-tuple-element.21.refs_1_.w), custom_call_target="tpu_custom_call" | custom-call | tf_op jit(solution)/shard_map/fine/pallas_call | solution.py:414
  51.3 0.7 %collective-permute-done.17 = f32[5,1536]{1,0:T(8,128)S(1)} collective-permute-done((f32[5,1536]{1,0:T(8,128)S(1)}, f32[5,1536]{1,0:T(8,128)S(1)}, u32[]{:S(2)}, u32[]{:S(2)}) %collective-permute-start.17) | collective-permute-done | bytes 30752 | tf_op jit(solution)/shard_map/ppermute | solution.py:282
  52.0 0.3 collective-permute-done.16
  52.3 0.5 collective-permute-done.15
  52.8 0.6 %add_multiply_fusion = f32[5,1536]{1,0:T(8,128)} fusion(f32[5,1536]{1,0:T(8,128)S(1)} %collective-permute-done.17, f32[5,1536]{1,0:T(8,128)S(1)} %collective-permute-done.16, f32[5,1536]{1,0:T(8,128)S(1)} %add_add_fusion, f32[5,1536]{1,0:T(8,128)S(1)} %collective-permute-done.15), kind=kLoop, calls=%fused_computation | loop fusion | flops 30720 | bytes 153600 | tf_op jit(solution)/shard_map/mul | solution.py:436
  (2 shorter events, 0.0 us)
Async XLA Ops:
  1.9 15.9 %collective-permute-start.9 = (bf16[72,1536]{1,0:T(8,128)(2,1)S(1)}, bf16[72,1536]{1,0:T(8,128)(2,1)S(1)}, u32[]{:S(2)}, u32[]{:S(2)}) collective-permute-start(bf16[72,1536]{1,0:T(8,128)(2,1)S(1)} %get-tuple-element.34), channel_id=1, source_target_pairs={{0,1},{1,0},{2,3},{3,2},{4,5},{5,4},{6,7},{7,6},{8,9},{9,8},{10,11... | collective-permute-start | bytes 663560 | tf_op jit(solution)/shard_map/ppermute | solution.py:282
  5.0 12.8 %collective-permute-start = (bf16[448,128]{1,0:T(8,128)(2,1)S(1)}, bf16[448,128]{1,0:T(8,128)(2,1)S(1)}, u32[]{:S(2)}, u32[]{:S(2)}) collective-permute-start(bf16[448,128]{1,0:T(8,128)(2,1)S(1)} %get-tuple-element.24.refs_1_.refs_10_), channel_id=1, source_target_pairs={{0,4},{1,5},{2,6},{3,7},{4,0},{5,1},{6,2},{7,3},{8,12},{9,13},{10,... | collective-permute-start | bytes 344072 | tf_op jit(solution)/shard_map/ppermute | solution.py:282
  7.6 12.7 %collective-permute-start.7 = (bf16[56,1536]{1,0:T(8,128)(2,1)S(1)}, bf16[56,1536]{1,0:T(8,128)(2,1)S(1)}, u32[]{:S(2)}, u32[]{:S(2)}) collective-permute-start(bf16[56,1536]{1,0:T(8,128)(2,1)S(1)} %get-tuple-element.33), channel_id=1, source_target_pairs={{0,6},{1,7},{2,4},{3,5},{4,2},{5,3},{6,0},{7,1},{8,14},{9,15},{10,... | collective-permute-start | bytes 516104 | tf_op jit(solution)/shard_map/ppermute | solution.py:282
  8.9 11.9 %collective-permute-start.2 = (bf16[448,128]{1,0:T(8,128)(2,1)S(1)}, bf16[448,128]{1,0:T(8,128)(2,1)S(1)}, u32[]{:S(2)}, u32[]{:S(2)}) collective-permute-start(bf16[448,128]{1,0:T(8,128)(2,1)S(1)} %get-tuple-element.24.refs_1_.refs_10_), channel_id=1, source_target_pairs={{0,1},{1,0},{2,3},{3,2},{4,5},{5,4},{6,7},{7,6},{8,9},{9,8},{10,11... | collective-permute-start | bytes 344072 | tf_op jit(solution)/shard_map/ppermute | solution.py:282
  9.4 12.9 %collective-permute-start.1 = (bf16[448,128]{1,0:T(8,128)(2,1)S(1)}, bf16[448,128]{1,0:T(8,128)(2,1)S(1)}, u32[]{:S(2)}, u32[]{:S(2)}) collective-permute-start(bf16[448,128]{1,0:T(8,128)(2,1)S(1)} %get-tuple-element.24.refs_1_.refs_10_), channel_id=1, source_target_pairs={{0,2},{1,3},{2,0},{3,1},{4,6},{5,7},{6,4},{7,5},{8,10},{9,11},{10,... | collective-permute-start | bytes 344072 | tf_op jit(solution)/shard_map/ppermute | solution.py:282
  17.8 5.0 %collective-permute-start.3 = (bf16[448,128]{1,0:T(8,128)(2,1)S(1)}, bf16[448,128]{1,0:T(8,128)(2,1)S(1)}, u32[]{:S(2)}, u32[]{:S(2)}) collective-permute-start(bf16[448,128]{1,0:T(8,128)(2,1)S(1)} %collective-permute-done.refs_2_.refs_11_), channel_id=1, source_target_pairs={{0,2},{1,3},{2,0},{3,1},{4,6},{5,7},{6,4},{7,5},{8,10},{9,11},{10,... | collective-permute-start | bytes 344072 | tf_op jit(solution)/shard_map/ppermute | solution.py:282
  17.8 18.7 %collective-permute-start.10 = (bf16[72,1536]{1,0:T(8,128)(2,1)S(1)}, bf16[72,1536]{1,0:T(8,128)(2,1)S(1)}, u32[]{:S(2)}, u32[]{:S(2)}) collective-permute-start(bf16[72,1536]{1,0:T(8,128)(2,1)S(1)} %collective-permute-done.9), channel_id=1, source_target_pairs={{0,6},{1,7},{2,4},{3,5},{4,2},{5,3},{6,0},{7,1},{8,14},{9,15},{10,... | collective-permute-start | bytes 663560 | tf_op jit(solution)/shard_map/ppermute | solution.py:282
  20.3 16.2 %collective-permute-start.8 = (bf16[56,1536]{1,0:T(8,128)(2,1)S(1)}, bf16[56,1536]{1,0:T(8,128)(2,1)S(1)}, u32[]{:S(2)}, u32[]{:S(2)}) collective-permute-start(bf16[56,1536]{1,0:T(8,128)(2,1)S(1)} %collective-permute-done.7), channel_id=1, source_target_pairs={{0,1},{1,0},{2,3},{3,2},{4,5},{5,4},{6,7},{7,6},{8,9},{9,8},{10,11... | collective-permute-start | bytes 516104 | tf_op jit(solution)/shard_map/ppermute | solution.py:282
  20.8 11.6 %collective-permute-start.5 = (bf16[448,128]{1,0:T(8,128)(2,1)S(1)}, bf16[448,128]{1,0:T(8,128)(2,1)S(1)}, u32[]{:S(2)}, u32[]{:S(2)}) collective-permute-start(bf16[448,128]{1,0:T(8,128)(2,1)S(1)} %collective-permute-done.refs_2_.refs_11_), channel_id=1, source_target_pairs={{0,1},{1,0},{2,3},{3,2},{4,5},{5,4},{6,7},{7,6},{8,9},{9,8},{10,11... | collective-permute-start | bytes 344072 | tf_op jit(solution)/shard_map/ppermute | solution.py:282
  22.3 10.0 %collective-permute-start.4 = (bf16[448,128]{1,0:T(8,128)(2,1)S(1)}, bf16[448,128]{1,0:T(8,128)(2,1)S(1)}, u32[]{:S(2)}, u32[]{:S(2)}) collective-permute-start(bf16[448,128]{1,0:T(8,128)(2,1)S(1)} %collective-permute-done.1.refs_3_.refs_12_), channel_id=1, source_target_pairs={{0,1},{1,0},{2,3},{3,2},{4,5},{5,4},{6,7},{7,6},{8,9},{9,8},{10,11... | collective-permute-start | bytes 344072 | tf_op jit(solution)/shard_map/ppermute | solution.py:282
  22.8 10.8 %collective-permute-start.6 = (bf16[448,128]{1,0:T(8,128)(2,1)S(1)}, bf16[448,128]{1,0:T(8,128)(2,1)S(1)}, u32[]{:S(2)}, u32[]{:S(2)}) collective-permute-start(bf16[448,128]{1,0:T(8,128)(2,1)S(1)} %collective-permute-done.3.refs_14_), channel_id=1, source_target_pairs={{0,1},{1,0},{2,3},{3,2},{4,5},{5,4},{6,7},{7,6},{8,9},{9,8},{10,11... | collective-permute-start | bytes 344072 | tf_op jit(solution)/shard_map/ppermute | solution.py:282
  37.1 1.3 %collective-permute-start.11 = (f32[5,1536]{1,0:T(8,128)S(1)}, f32[5,1536]{1,0:T(8,128)S(1)}, u32[]{:S(2)}, u32[]{:S(2)}) collective-permute-start(f32[5,1536]{1,0:T(8,128)S(1)} %get-tuple-element.37), channel_id=1, source_target_pairs={{0,8},{1,9},{2,10},{3,11},{4,12},{5,13},{6,14},{7,15},{8,0},{9,1},... | collective-permute-start | bytes 92168 | tf_op jit(solution)/shard_map/ppermute | solution.py:282
  38.4 5.1 %collective-permute-start.14 = (f32[5,1536]{1,0:T(8,128)S(1)}, f32[5,1536]{1,0:T(8,128)S(1)}, u32[]{:S(2)}, u32[]{:S(2)}) collective-permute-start(f32[5,1536]{1,0:T(8,128)S(1)} %add.21), channel_id=1, source_target_pairs={{0,17},{1,16},{2,19},{3,18},{4,21},{5,20},{6,23},{7,22},{8,25},{9,... | collective-permute-start | bytes 92168 | tf_op jit(solution)/shard_map/ppermute | solution.py:282
  39.9 4.3 %collective-permute-start.13 = (f32[5,1536]{1,0:T(8,128)S(1)}, f32[5,1536]{1,0:T(8,128)S(1)}, u32[]{:S(2)}, u32[]{:S(2)}) collective-permute-start(f32[5,1536]{1,0:T(8,128)S(1)} %add.21), channel_id=1, source_target_pairs={{0,1},{1,0},{2,3},{3,2},{4,5},{5,4},{6,7},{7,6},{8,9},{9,8},{10,11... | collective-permute-start | bytes 92168 | tf_op jit(solution)/shard_map/ppermute | solution.py:282
  41.4 4.1 %collective-permute-start.12 = (f32[5,1536]{1,0:T(8,128)S(1)}, f32[5,1536]{1,0:T(8,128)S(1)}, u32[]{:S(2)}, u32[]{:S(2)}) collective-permute-start(f32[5,1536]{1,0:T(8,128)S(1)} %add.21), channel_id=1, source_target_pairs={{0,16},{1,17},{2,18},{3,19},{4,20},{5,21},{6,22},{7,23},{8,24},{9,... | collective-permute-start | bytes 92168 | tf_op jit(solution)/shard_map/ppermute | solution.py:282
  45.5 6.5 %collective-permute-start.17 = (f32[5,1536]{1,0:T(8,128)S(1)}, f32[5,1536]{1,0:T(8,128)S(1)}, u32[]{:S(2)}, u32[]{:S(2)}) collective-permute-start(f32[5,1536]{1,0:T(8,128)S(1)} %add_add_fusion), channel_id=1, source_target_pairs={{0,6},{1,7},{2,4},{3,5},{4,2},{5,3},{6,0},{7,1},{8,14},{9,15},{10,... | collective-permute-start | bytes 92168 | tf_op jit(solution)/shard_map/ppermute | solution.py:282
  46.7 5.5 %collective-permute-start.16 = (f32[5,1536]{1,0:T(8,128)S(1)}, f32[5,1536]{1,0:T(8,128)S(1)}, u32[]{:S(2)}, u32[]{:S(2)}) collective-permute-start(f32[5,1536]{1,0:T(8,128)S(1)} %add_add_fusion), channel_id=1, source_target_pairs={{0,4},{1,5},{2,6},{3,7},{4,0},{5,1},{6,2},{7,3},{8,12},{9,13},{10,... | collective-permute-start | bytes 92168 | tf_op jit(solution)/shard_map/ppermute | solution.py:282
  48.7 4.1 %collective-permute-start.15 = (f32[5,1536]{1,0:T(8,128)S(1)}, f32[5,1536]{1,0:T(8,128)S(1)}, u32[]{:S(2)}, u32[]{:S(2)}) collective-permute-start(f32[5,1536]{1,0:T(8,128)S(1)} %add_add_fusion), channel_id=1, source_target_pairs={{0,2},{1,3},{2,0},{3,1},{4,6},{5,7},{6,4},{7,5},{8,10},{9,11},{10,... | collective-permute-start | bytes 92168 | tf_op jit(solution)/shard_map/ppermute | solution.py:282

commit v6 on v5

--- a/solution.py
+++ b/solution.py
@@ -15,7 +15,7 @@
 TAIL = 4
 HEAD = 3
 TILE = 16
-CUT = 7
+CUT = 8
 VMEM = pl.BlockSpec(memory_space=pltpu.VMEM)
 HBM = pl.BlockSpec(memory_space=pltpu.HBM)
 SMEM = pl.BlockSpec(memory_space=pltpu.SMEM)
@@ -446,6 +446,4 @@
         P(),
     )
 
-    return jax.shard_map(
-        body, mesh=mesh, in_specs=placed, out_specs=(P("dp", "ctx", None), P()), check_vma=False
-    )
+    return jax.shard_map(body, mesh=mesh, in_specs=placed, out_specs=(P("dp", "ctx", None), P()), check_vma=False)

time: 53.6 us -> 54.4 us (1.015)
  starting transfers between devices: 22.3 us -> 23.4 us
    ppermute x18, starting transfers between devices: 22.3 us -> 23.4 us  [swap(): lax.ppermute(value, axis, [(i, i ^ mask) for i in range(lax.axis_size(axi...]
  transfers between devices with their start and end apart: 18 -> 18, of which waited for: 10 -> 9; matrix products, arithmetic and copies ran while one was open for 0% -> 0% of each run, Pallas kernels for 14% -> 14%
where the time goes in v6:
time: 54.4 us; the launch traced here: 54.3 us
  starting transfers between devices  23.4 us (43%)
  waiting for transfers between devices  20.1 us (37%)
  Pallas kernels  9.44 us (17%)
  between operations  0.71 us (1%)
  other arithmetic  0.66 us (1%)
    ppermute x18, starting transfers between devices, swap(): lax.ppermute(value, axis, [(i, i ^ mask) for i in range(lax.axis_size(axi...  23.4 us
    ppermute x18, waiting for transfers between devices, swap(): lax.ppermute(value, axis, [(i, i ^ mask) for i in range(lax.axis_size(axi...  20.1 us
    pallas_call x1, Pallas kernels, body(): pl.pallas_call(lambda *refs: attend_kernel(*refs, parts=len(parts), per=r...  2.92 us
    pallas_call x1, Pallas kernels, body(): pl.pallas_call(lambda *refs: first_kernel(*refs, parts=len(early), per=ro...  1.69 us
    pallas_call x1, Pallas kernels, body(): pl.pallas_call(prep_kernel, name='prep', out_shape=(pltpu.VMEM(q.shape, b...  1.66 us
    pallas_call x1, Pallas kernels, body(): pl.pallas_call(fine_kernel, name='fine', out_shape=jax.ShapeDtypeStruct((...  1.37 us
    pallas_call x1, Pallas kernels, body(): pl.pallas_call(pack_kernel, name='pack', out_shape=(pltpu.VMEM((size, LAN...  1.3 us
  transfers between devices with their start and end apart: 18, of which 9 were waited for; matrix products, arithmetic and copies ran while one was open for 0% of the time, Pallas kernels for 14%

profile of v6, /device:TPU:0, one launch (start us, length us, event | category | flops | bytes accessed | tf_op | source)
XLA Modules:
  0.0 54.3 jit_solution(119308718581772919)
XLA Ops:
  0.6 1.3 %pack.1 = (bf16[448,128]{1,0:T(8,128)(2,1)S(1)}, bf16[64,1536]{1,0:T(8,128)(2,1)S(1)}, bf16[64,1536]{1,0:T(8,128)(2,1)S(1)}) custom-call(bf16[128,128]{1,0:T(8,128)(2,1)} %bitcast.15, bf16[192,128]{1,0:T(8,128)(2,1)} %bitcast.14, bf16[128,1024]{1,0:T(8,128)(2,1)} %bitcast.10, bf16[256,1536]{1,0:T(8,128)(2,1)} %bitcast.8, bf16[128,1536]{1,0:T(8,128)(2,1)} %bitcast.13), custom_call_target="tpu_custom_call" | custom-call | tf_op jit(solution)/shard_map/pack/pallas_call | solution.py:308
  1.9 5.1 %collective-permute-start.7 = (bf16[64,1536]{1,0:T(8,128)(2,1)S(1)}, bf16[64,1536]{1,0:T(8,128)(2,1)S(1)}, u32[]{:S(2)}, u32[]{:S(2)}) collective-permute-start(bf16[64,1536]{1,0:T(8,128)(2,1)S(1)} %get-tuple-element.33), channel_id=1, source_target_pairs={{0,6},{1,7},{2,4},{3,5},{4,2},{5,3},{6,0},{7,1},{8,14},{9,15},{10,... | collective-permute-start | bytes 589832 | tf_op jit(solution)/shard_map/ppermute | solution.py:282
  7.1 1.5 %collective-permute-start.9 = (bf16[64,1536]{1,0:T(8,128)(2,1)S(1)}, bf16[64,1536]{1,0:T(8,128)(2,1)S(1)}, u32[]{:S(2)}, u32[]{:S(2)}) collective-permute-start(bf16[64,1536]{1,0:T(8,128)(2,1)S(1)} %get-tuple-element.34), channel_id=1, source_target_pairs={{0,1},{1,0},{2,3},{3,2},{4,5},{5,4},{6,7},{7,6},{8,9},{9,8},{10,11... | collective-permute-start | bytes 589832 | tf_op jit(solution)/shard_map/ppermute | solution.py:282
  8.6 0.0 collective-permute-start
  8.6 0.5 collective-permute-start.2
  9.1 0.6 %collective-permute-start.1 = (bf16[448,128]{1,0:T(8,128)(2,1)S(1)}, bf16[448,128]{1,0:T(8,128)(2,1)S(1)}, u32[]{:S(2)}, u32[]{:S(2)}) collective-permute-start(bf16[448,128]{1,0:T(8,128)(2,1)S(1)} %get-tuple-element.24.refs_1_.refs_10_), channel_id=1, source_target_pairs={{0,2},{1,3},{2,0},{3,1},{4,6},{5,7},{6,4},{7,5},{8,10},{9,11},{10,... | collective-permute-start | bytes 344072 | tf_op jit(solution)/shard_map/ppermute | solution.py:282
  9.8 10.5 %collective-permute-done.refs_2_.refs_11_ = bf16[448,128]{1,0:T(8,128)(2,1)S(1)} collective-permute-done((bf16[448,128]{1,0:T(8,128)(2,1)S(1)}, bf16[448,128]{1,0:T(8,128)(2,1)S(1)}, u32[]{:S(2)}, u32[]{:S(2)}) %collective-permute-start) | collective-permute-done | bytes 114720 | tf_op jit(solution)/shard_map/ppermute | solution.py:282
  20.3 0.0 collective-permute-start.3
  20.3 0.0 collective-permute-done.7
  20.3 1.5 %collective-permute-start.8 = (bf16[64,1536]{1,0:T(8,128)(2,1)S(1)}, bf16[64,1536]{1,0:T(8,128)(2,1)S(1)}, u32[]{:S(2)}, u32[]{:S(2)}) collective-permute-start(bf16[64,1536]{1,0:T(8,128)(2,1)S(1)} %collective-permute-done.7), channel_id=1, source_target_pairs={{0,1},{1,0},{2,3},{3,2},{4,5},{5,4},{6,7},{7,6},{8,9},{9,8},{10,11... | collective-permute-start | bytes 589832 | tf_op jit(solution)/shard_map/ppermute | solution.py:282
  21.8 0.0 collective-permute-done.9
  21.8 2.5 %collective-permute-start.10 = (bf16[64,1536]{1,0:T(8,128)(2,1)S(1)}, bf16[64,1536]{1,0:T(8,128)(2,1)S(1)}, u32[]{:S(2)}, u32[]{:S(2)}) collective-permute-start(bf16[64,1536]{1,0:T(8,128)(2,1)S(1)} %collective-permute-done.9), channel_id=1, source_target_pairs={{0,6},{1,7},{2,4},{3,5},{4,2},{5,3},{6,0},{7,1},{8,14},{9,15},{10,... | collective-permute-start | bytes 589832 | tf_op jit(solution)/shard_map/ppermute | solution.py:282
  24.3 0.0 collective-permute-done.2.refs_4_.refs_13_
  24.3 0.5 collective-permute-start.5
  24.8 0.0 collective-permute-done.1.refs_3_.refs_12_
  24.8 1.5 %collective-permute-start.4 = (bf16[448,128]{1,0:T(8,128)(2,1)S(1)}, bf16[448,128]{1,0:T(8,128)(2,1)S(1)}, u32[]{:S(2)}, u32[]{:S(2)}) collective-permute-start(bf16[448,128]{1,0:T(8,128)(2,1)S(1)} %collective-permute-done.1.refs_3_.refs_12_), channel_id=1, source_target_pairs={{0,1},{1,0},{2,3},{3,2},{4,5},{5,4},{6,7},{7,6},{8,9},{9,8},{10,11... | collective-permute-start | bytes 344072 | tf_op jit(solution)/shard_map/ppermute | solution.py:282
  26.3 0.0 collective-permute-done.3.refs_14_
  26.3 1.5 %collective-permute-start.6 = (bf16[448,128]{1,0:T(8,128)(2,1)S(1)}, bf16[448,128]{1,0:T(8,128)(2,1)S(1)}, u32[]{:S(2)}, u32[]{:S(2)}) collective-permute-start(bf16[448,128]{1,0:T(8,128)(2,1)S(1)} %collective-permute-done.3.refs_14_), channel_id=1, source_target_pairs={{0,1},{1,0},{2,3},{3,2},{4,5},{5,4},{6,7},{7,6},{8,9},{9,8},{10,11... | collective-permute-start | bytes 344072 | tf_op jit(solution)/shard_map/ppermute | solution.py:282
  27.8 1.7 %prep.1 = (bf16[128,1024]{1,0:T(8,128)(2,1)S(1)}, f32[5,1536]{1,0:T(8,128)S(1)}, f32[128,1536]{1,0:T(8,128)S(1)}, f32[12,272,128]{2,1,0:T(8,128)S(1)}) custom-call(bf16[128,1024]{1,0:T(8,128)(2,1)} %bitcast.11, bf16[256,1536]{1,0:T(8,128)(2,1)} %bitcast.9, f32[5,1536]{1,0:T(8,128)} %w.1), custom_call_target="tpu_custom_call" | custom-call | tf_op jit(solution)/shard_map/prep/pallas_call | solution.py:343
  29.5 1.7 %first.1 = (bf16[512,128]{1,0:T(8,128)(2,1)S(1)}, bf16[256,512]{1,0:T(8,128)(2,1)S(1)}, bf16[256,512]{1,0:T(8,128)(2,1)S(1)}, f32[8,128,128]{2,1,0:T(8,128)S(1)}...) custom-call(bf16[128,1024]{1,0:T(8,128)(2,1)S(1)} %get-tuple-element.20.refs_0_, ...), custom_call_target="tpu_custom_call" | custom-call | tf_op jit(solution)/shard_map/first/pallas_call | solution.py:361
  31.2 1.2 %collective-permute-done.4.refs_15_ = bf16[448,128]{1,0:T(8,128)(2,1)S(1)} collective-permute-done((bf16[448,128]{1,0:T(8,128)(2,1)S(1)}, bf16[448,128]{1,0:T(8,128)(2,1)S(1)}, u32[]{:S(2)}, u32[]{:S(2)}) %collective-permute-start.4) | collective-permute-done | bytes 114720 | tf_op jit(solution)/shard_map/ppermute | solution.py:282
  32.4 0.0 collective-permute-done.5.refs_16_
  32.4 1.2 %collective-permute-done.6.refs_17_ = bf16[448,128]{1,0:T(8,128)(2,1)S(1)} collective-permute-done((bf16[448,128]{1,0:T(8,128)(2,1)S(1)}, bf16[448,128]{1,0:T(8,128)(2,1)S(1)}, u32[]{:S(2)}, u32[]{:S(2)}) %collective-permute-start.6) | collective-permute-done | bytes 114720 | tf_op jit(solution)/shard_map/ppermute | solution.py:282
  33.6 2.9 %attend.1 = (f32[128,1536]{1,0:T(8,128)S(1)}, f32[8,1536]{1,0:T(8,128)S(1)}, f32[12,272,128]{2,1,0:T(8,128)S(1)}) custom-call(bf16[128,1024]{1,0:T(8,128)(2,1)S(1)} %get-tuple-element.20.refs_0_, f32[5,1536]{1,0:T(8,128)S(1)} %get-tuple-element.21.refs_1_.w, ...), custom_call_target="tpu_custom_call", output_to_operand_aliasing={{0}: (2, {}), {2}: (3, {})} | custom-call | tf_op jit(solution)/shard_map/attend/pallas_call | solution.py:377
  36.5 0.0 collective-permute-done.8.rc_a
  36.6 0.0 collective-permute-done.10.rc_b
  36.6 0.5 grad.1
  37.1 0.1 collective-permute-start.11
  37.1 1.2 %collective-permute-done.11 = f32[5,1536]{1,0:T(8,128)S(1)} collective-permute-done((f32[5,1536]{1,0:T(8,128)S(1)}, f32[5,1536]{1,0:T(8,128)S(1)}, u32[]{:S(2)}, u32[]{:S(2)}) %collective-permute-start.11) | collective-permute-done | bytes 30752 | tf_op jit(solution)/shard_map/ppermute | solution.py:282
  38.4 2.5 %collective-permute-start.14 = (f32[5,1536]{1,0:T(8,128)S(1)}, f32[5,1536]{1,0:T(8,128)S(1)}, u32[]{:S(2)}, u32[]{:S(2)}) collective-permute-start(f32[5,1536]{1,0:T(8,128)S(1)} %add.21), channel_id=1, source_target_pairs={{0,17},{1,16},{2,19},{3,18},{4,21},{5,20},{6,23},{7,22},{8,25},{9,... | collective-permute-start | bytes 92168 | tf_op jit(solution)/shard_map/ppermute | solution.py:282
  40.9 0.5 collective-permute-start.13
  41.4 0.5 collective-permute-start.12
  41.9 1.5 %collective-permute-done.14 = f32[5,1536]{1,0:T(8,128)S(1)} collective-permute-done((f32[5,1536]{1,0:T(8,128)S(1)}, f32[5,1536]{1,0:T(8,128)S(1)}, u32[]{:S(2)}, u32[]{:S(2)}) %collective-permute-start.14) | collective-permute-done | bytes 30752 | tf_op jit(solution)/shard_map/ppermute | solution.py:282
  43.4 1.5 %collective-permute-done.13 = f32[5,1536]{1,0:T(8,128)S(1)} collective-permute-done((f32[5,1536]{1,0:T(8,128)S(1)}, f32[5,1536]{1,0:T(8,128)S(1)}, u32[]{:S(2)}, u32[]{:S(2)}) %collective-permute-start.13) | collective-permute-done | bytes 30752 | tf_op jit(solution)/shard_map/ppermute | solution.py:282
  45.0 0.5 collective-permute-done.12
  45.5 3.1 %collective-permute-start.17 = (f32[5,1536]{1,0:T(8,128)S(1)}, f32[5,1536]{1,0:T(8,128)S(1)}, u32[]{:S(2)}, u32[]{:S(2)}) collective-permute-start(f32[5,1536]{1,0:T(8,128)S(1)} %add_add_fusion), channel_id=1, source_target_pairs={{0,6},{1,7},{2,4},{3,5},{4,2},{5,3},{6,0},{7,1},{8,14},{9,15},{10,... | collective-permute-start | bytes 92168 | tf_op jit(solution)/shard_map/ppermute | solution.py:282
  48.6 0.1 collective-permute-start.16
  48.8 1.2 %collective-permute-start.15 = (f32[5,1536]{1,0:T(8,128)S(1)}, f32[5,1536]{1,0:T(8,128)S(1)}, u32[]{:S(2)}, u32[]{:S(2)}) collective-permute-start(f32[5,1536]{1,0:T(8,128)S(1)} %add_add_fusion), channel_id=1, source_target_pairs={{0,2},{1,3},{2,0},{3,1},{4,6},{5,7},{6,4},{7,5},{8,10},{9,11},{10,... | collective-permute-start | bytes 92168 | tf_op jit(solution)/shard_map/ppermute | solution.py:282
  49.9 1.4 %fine.1 = bf16[256,1536]{1,0:T(8,128)(2,1)} custom-call(f32[128,1536]{1,0:T(8,128)S(1)} %get-tuple-element.35.grad, f32[8,1536]{1,0:T(8,128)S(1)} %get-tuple-element.36.ends, f32[5,1536]{1,0:T(8,128)S(1)} %get-tuple-element.21.refs_1_.w), custom_call_target="tpu_custom_call" | custom-call | tf_op jit(solution)/shard_map/fine/pallas_call | solution.py:414
  51.3 0.2 collective-permute-done.17
  51.5 2.1 %collective-permute-done.16 = f32[5,1536]{1,0:T(8,128)S(1)} collective-permute-done((f32[5,1536]{1,0:T(8,128)S(1)}, f32[5,1536]{1,0:T(8,128)S(1)}, u32[]{:S(2)}, u32[]{:S(2)}) %collective-permute-start.16) | collective-permute-done | bytes 30752 | tf_op jit(solution)/shard_map/ppermute | solution.py:282
  53.6 0.0 collective-permute-done.15
  53.6 0.6 %add_multiply_fusion = f32[5,1536]{1,0:T(8,128)} fusion(f32[5,1536]{1,0:T(8,128)S(1)} %collective-permute-done.17, f32[5,1536]{1,0:T(8,128)S(1)} %collective-permute-done.16, f32[5,1536]{1,0:T(8,128)S(1)} %add_add_fusion, f32[5,1536]{1,0:T(8,128)S(1)} %collective-permute-done.15), kind=kLoop, calls=%fused_computation | loop fusion | flops 30720 | bytes 153600 | tf_op jit(solution)/shard_map/mul | solution.py:436
  (2 shorter events, 0.0 us)
Async XLA Ops:
  1.9 18.3 %collective-permute-start.7 = (bf16[64,1536]{1,0:T(8,128)(2,1)S(1)}, bf16[64,1536]{1,0:T(8,128)(2,1)S(1)}, u32[]{:S(2)}, u32[]{:S(2)}) collective-permute-start(bf16[64,1536]{1,0:T(8,128)(2,1)S(1)} %get-tuple-element.33), channel_id=1, source_target_pairs={{0,6},{1,7},{2,4},{3,5},{4,2},{5,3},{6,0},{7,1},{8,14},{9,15},{10,... | collective-permute-start | bytes 589832 | tf_op jit(solution)/shard_map/ppermute | solution.py:282
  7.1 14.7 %collective-permute-start.9 = (bf16[64,1536]{1,0:T(8,128)(2,1)S(1)}, bf16[64,1536]{1,0:T(8,128)(2,1)S(1)}, u32[]{:S(2)}, u32[]{:S(2)}) collective-permute-start(bf16[64,1536]{1,0:T(8,128)(2,1)S(1)} %get-tuple-element.34), channel_id=1, source_target_pairs={{0,1},{1,0},{2,3},{3,2},{4,5},{5,4},{6,7},{7,6},{8,9},{9,8},{10,11... | collective-permute-start | bytes 589832 | tf_op jit(solution)/shard_map/ppermute | solution.py:282
  8.6 11.7 %collective-permute-start = (bf16[448,128]{1,0:T(8,128)(2,1)S(1)}, bf16[448,128]{1,0:T(8,128)(2,1)S(1)}, u32[]{:S(2)}, u32[]{:S(2)}) collective-permute-start(bf16[448,128]{1,0:T(8,128)(2,1)S(1)} %get-tuple-element.24.refs_1_.refs_10_), channel_id=1, source_target_pairs={{0,4},{1,5},{2,6},{3,7},{4,0},{5,1},{6,2},{7,3},{8,12},{9,13},{10,... | collective-permute-start | bytes 344072 | tf_op jit(solution)/shard_map/ppermute | solution.py:282
  8.6 15.7 %collective-permute-start.2 = (bf16[448,128]{1,0:T(8,128)(2,1)S(1)}, bf16[448,128]{1,0:T(8,128)(2,1)S(1)}, u32[]{:S(2)}, u32[]{:S(2)}) collective-permute-start(bf16[448,128]{1,0:T(8,128)(2,1)S(1)} %get-tuple-element.24.refs_1_.refs_10_), channel_id=1, source_target_pairs={{0,1},{1,0},{2,3},{3,2},{4,5},{5,4},{6,7},{7,6},{8,9},{9,8},{10,11... | collective-permute-start | bytes 344072 | tf_op jit(solution)/shard_map/ppermute | solution.py:282
  9.1 15.7 %collective-permute-start.1 = (bf16[448,128]{1,0:T(8,128)(2,1)S(1)}, bf16[448,128]{1,0:T(8,128)(2,1)S(1)}, u32[]{:S(2)}, u32[]{:S(2)}) collective-permute-start(bf16[448,128]{1,0:T(8,128)(2,1)S(1)} %get-tuple-element.24.refs_1_.refs_10_), channel_id=1, source_target_pairs={{0,2},{1,3},{2,0},{3,1},{4,6},{5,7},{6,4},{7,5},{8,10},{9,11},{10,... | collective-permute-start | bytes 344072 | tf_op jit(solution)/shard_map/ppermute | solution.py:282
  20.3 6.0 %collective-permute-start.3 = (bf16[448,128]{1,0:T(8,128)(2,1)S(1)}, bf16[448,128]{1,0:T(8,128)(2,1)S(1)}, u32[]{:S(2)}, u32[]{:S(2)}) collective-permute-start(bf16[448,128]{1,0:T(8,128)(2,1)S(1)} %collective-permute-done.refs_2_.refs_11_), channel_id=1, source_target_pairs={{0,2},{1,3},{2,0},{3,1},{4,6},{5,7},{6,4},{7,5},{8,10},{9,11},{10,... | collective-permute-start | bytes 344072 | tf_op jit(solution)/shard_map/ppermute | solution.py:282
  20.3 16.3 %collective-permute-start.8 = (bf16[64,1536]{1,0:T(8,128)(2,1)S(1)}, bf16[64,1536]{1,0:T(8,128)(2,1)S(1)}, u32[]{:S(2)}, u32[]{:S(2)}) collective-permute-start(bf16[64,1536]{1,0:T(8,128)(2,1)S(1)} %collective-permute-done.7), channel_id=1, source_target_pairs={{0,1},{1,0},{2,3},{3,2},{4,5},{5,4},{6,7},{7,6},{8,9},{9,8},{10,11... | collective-permute-start | bytes 589832 | tf_op jit(solution)/shard_map/ppermute | solution.py:282
  21.8 14.8 %collective-permute-start.10 = (bf16[64,1536]{1,0:T(8,128)(2,1)S(1)}, bf16[64,1536]{1,0:T(8,128)(2,1)S(1)}, u32[]{:S(2)}, u32[]{:S(2)}) collective-permute-start(bf16[64,1536]{1,0:T(8,128)(2,1)S(1)} %collective-permute-done.9), channel_id=1, source_target_pairs={{0,6},{1,7},{2,4},{3,5},{4,2},{5,3},{6,0},{7,1},{8,14},{9,15},{10,... | collective-permute-start | bytes 589832 | tf_op jit(solution)/shard_map/ppermute | solution.py:282
  24.3 8.1 %collective-permute-start.5 = (bf16[448,128]{1,0:T(8,128)(2,1)S(1)}, bf16[448,128]{1,0:T(8,128)(2,1)S(1)}, u32[]{:S(2)}, u32[]{:S(2)}) collective-permute-start(bf16[448,128]{1,0:T(8,128)(2,1)S(1)} %collective-permute-done.refs_2_.refs_11_), channel_id=1, source_target_pairs={{0,1},{1,0},{2,3},{3,2},{4,5},{5,4},{6,7},{7,6},{8,9},{9,8},{10,11... | collective-permute-start | bytes 344072 | tf_op jit(solution)/shard_map/ppermute | solution.py:282
  24.8 7.6 %collective-permute-start.4 = (bf16[448,128]{1,0:T(8,128)(2,1)S(1)}, bf16[448,128]{1,0:T(8,128)(2,1)S(1)}, u32[]{:S(2)}, u32[]{:S(2)}) collective-permute-start(bf16[448,128]{1,0:T(8,128)(2,1)S(1)} %collective-permute-done.1.refs_3_.refs_12_), channel_id=1, source_target_pairs={{0,1},{1,0},{2,3},{3,2},{4,5},{5,4},{6,7},{7,6},{8,9},{9,8},{10,11... | collective-permute-start | bytes 344072 | tf_op jit(solution)/shard_map/ppermute | solution.py:282
  26.3 7.3 %collective-permute-start.6 = (bf16[448,128]{1,0:T(8,128)(2,1)S(1)}, bf16[448,128]{1,0:T(8,128)(2,1)S(1)}, u32[]{:S(2)}, u32[]{:S(2)}) collective-permute-start(bf16[448,128]{1,0:T(8,128)(2,1)S(1)} %collective-permute-done.3.refs_14_), channel_id=1, source_target_pairs={{0,1},{1,0},{2,3},{3,2},{4,5},{5,4},{6,7},{7,6},{8,9},{9,8},{10,11... | collective-permute-start | bytes 344072 | tf_op jit(solution)/shard_map/ppermute | solution.py:282
  37.1 1.3 %collective-permute-start.11 = (f32[5,1536]{1,0:T(8,128)S(1)}, f32[5,1536]{1,0:T(8,128)S(1)}, u32[]{:S(2)}, u32[]{:S(2)}) collective-permute-start(f32[5,1536]{1,0:T(8,128)S(1)} %get-tuple-element.37), channel_id=1, source_target_pairs={{0,8},{1,9},{2,10},{3,11},{4,12},{5,13},{6,14},{7,15},{8,0},{9,1},... | collective-permute-start | bytes 92168 | tf_op jit(solution)/shard_map/ppermute | solution.py:282
  38.4 5.1 %collective-permute-start.14 = (f32[5,1536]{1,0:T(8,128)S(1)}, f32[5,1536]{1,0:T(8,128)S(1)}, u32[]{:S(2)}, u32[]{:S(2)}) collective-permute-start(f32[5,1536]{1,0:T(8,128)S(1)} %add.21), channel_id=1, source_target_pairs={{0,17},{1,16},{2,19},{3,18},{4,21},{5,20},{6,23},{7,22},{8,25},{9,... | collective-permute-start | bytes 92168 | tf_op jit(solution)/shard_map/ppermute | solution.py:282
  40.9 4.1 %collective-permute-start.13 = (f32[5,1536]{1,0:T(8,128)S(1)}, f32[5,1536]{1,0:T(8,128)S(1)}, u32[]{:S(2)}, u32[]{:S(2)}) collective-permute-start(f32[5,1536]{1,0:T(8,128)S(1)} %add.21), channel_id=1, source_target_pairs={{0,1},{1,0},{2,3},{3,2},{4,5},{5,4},{6,7},{7,6},{8,9},{9,8},{10,11... | collective-permute-start | bytes 92168 | tf_op jit(solution)/shard_map/ppermute | solution.py:282
  41.4 4.1 %collective-permute-start.12 = (f32[5,1536]{1,0:T(8,128)S(1)}, f32[5,1536]{1,0:T(8,128)S(1)}, u32[]{:S(2)}, u32[]{:S(2)}) collective-permute-start(f32[5,1536]{1,0:T(8,128)S(1)} %add.21), channel_id=1, source_target_pairs={{0,16},{1,17},{2,18},{3,19},{4,20},{5,21},{6,22},{7,23},{8,24},{9,... | collective-permute-start | bytes 92168 | tf_op jit(solution)/shard_map/ppermute | solution.py:282
  45.5 6.1 %collective-permute-start.17 = (f32[5,1536]{1,0:T(8,128)S(1)}, f32[5,1536]{1,0:T(8,128)S(1)}, u32[]{:S(2)}, u32[]{:S(2)}) collective-permute-start(f32[5,1536]{1,0:T(8,128)S(1)} %add_add_fusion), channel_id=1, source_target_pairs={{0,6},{1,7},{2,4},{3,5},{4,2},{5,3},{6,0},{7,1},{8,14},{9,15},{10,... | collective-permute-start | bytes 92168 | tf_op jit(solution)/shard_map/ppermute | solution.py:282
  48.6 5.0 %collective-permute-start.16 = (f32[5,1536]{1,0:T(8,128)S(1)}, f32[5,1536]{1,0:T(8,128)S(1)}, u32[]{:S(2)}, u32[]{:S(2)}) collective-permute-start(f32[5,1536]{1,0:T(8,128)S(1)} %add_add_fusion), channel_id=1, source_target_pairs={{0,4},{1,5},{2,6},{3,7},{4,0},{5,1},{6,2},{7,3},{8,12},{9,13},{10,... | collective-permute-start | bytes 92168 | tf_op jit(solution)/shard_map/ppermute | solution.py:282
  48.8 4.9 %collective-permute-start.15 = (f32[5,1536]{1,0:T(8,128)S(1)}, f32[5,1536]{1,0:T(8,128)S(1)}, u32[]{:S(2)}, u32[]{:S(2)}) collective-permute-start(f32[5,1536]{1,0:T(8,128)S(1)} %add_add_fusion), channel_id=1, source_target_pairs={{0,2},{1,3},{2,0},{3,1},{4,6},{5,7},{6,4},{7,5},{8,10},{9,11},{10,... | collective-permute-start | bytes 92168 | tf_op jit(solution)/shard_map/ppermute | solution.py:282

commit v7 on v5

--- a/solution.py
+++ b/solution.py
@@ -15,7 +15,7 @@
 TAIL = 4
 HEAD = 3
 TILE = 16
-CUT = 7
+CUT = 8
 VMEM = pl.BlockSpec(memory_space=pltpu.VMEM)
 HBM = pl.BlockSpec(memory_space=pltpu.HBM)
 SMEM = pl.BlockSpec(memory_space=pltpu.SMEM)
@@ -239,36 +239,33 @@
         ends[1:2, to] = jnp.where(keep_right, right, 0.0)
 
 
-def grad_kernel(base, fine, rc_a, rc_b, partial, grad):
-    rows = base.shape[0]
-
-    def flip(n):
-        i = lax.broadcasted_iota(jnp.int32, (n, n), 0)
-        j = lax.broadcasted_iota(jnp.int32, (n, n), 1)
-        return (i + j == n - 1).astype(jnp.bfloat16)
-
-    pieces = [(rows - rc_a.shape[0], rc_a, flip(rc_a.shape[0])), (0, rc_b, flip(rc_b.shape[0]))]
+def grad_kernel(base, fine, rc, *rest, low, chain):
+    partial, grad = rest[-2:]
+    n = rc.shape[0]
+    i = lax.broadcasted_iota(jnp.int32, (n, n), 0)
+    j = lax.broadcasted_iota(jnp.int32, (n, n), 1)
+    turn = (i + j == n - 1).astype(jnp.bfloat16)
     for c in range(fine.shape[0]):
         to = slice(c * LANES, (c + 1) * LANES)
-        sums = [None] * KW
-        for low, rc, turn in pieces:
-            n = rc.shape[0]
-            g = base[low : low + n, to] - jnp.dot(turn, rc[:, to], preferred_element_type=jnp.float32)
-            grad[low : low + n, to] = g
-            for k in range(KW):
-                tap = fine[c, pl.ds(EDGE - 2 + k + 2 * low, n, stride=2), :]
-                term = jnp.sum((g * tap).reshape(n // 8, 8, LANES), axis=0)
-                sums[k] = term if sums[k] is None else sums[k] + term
+        g = base[low : low + n, to] - jnp.dot(turn, rc[:, to], preferred_element_type=jnp.float32)
+        grad[:, to] = g
         for k in range(KW):
-            partial[k : k + 1, to] = jnp.sum(sums[k], axis=0, keepdims=True)
-
-
-def fine_kernel(grad, ends, w, d_fine, wide, padded):
+            tap = fine[c, pl.ds(EDGE - 2 + k + 2 * low, n, stride=2), :]
+            total = jnp.sum((g * tap).reshape(n // 8, 8, LANES), axis=0)
+            total = jnp.sum(total, axis=0, keepdims=True)
+            if chain:
+                total = total + rest[0][k : k + 1, to]
+            partial[k : k + 1, to] = total
+
+
+def fine_kernel(grad_b, grad_a, ends, w, d_fine, wide, padded):
     rows = d_fine.shape[0] // 2
     for c in range(wide.shape[0]):
         to = slice(c * LANES, (c + 1) * LANES)
-        here = grad[:, to]
-        padded[EDGE : EDGE + rows] = here
+        low = grad_b.shape[0]
+        padded[EDGE : EDGE + low] = grad_b[:, to]
+        padded[EDGE + low : EDGE + rows] = grad_a[:, to]
+        here = padded[EDGE : EDGE + rows]
         padded[EDGE - 1 : EDGE] = ends[0:1, to]
         padded[EDGE + rows : EDGE + rows + 1] = ends[1:2, to]
         after = padded[EDGE + 1 : EDGE + 1 + rows]
@@ -402,27 +399,31 @@
         *[near(part) for part in parts],
     )
 
-    partial, grad = pl.pallas_call(
-        grad_kernel,
-        name="grad",
-        out_shape=(pltpu.VMEM((KW, chans), f32), pltpu.VMEM((rows, chans), f32)),
-        in_specs=[VMEM] * 4,
-        out_specs=(VMEM,) * 2,
-        compiler_params=limit(8),
-    )(near(base), near(fine), near(rc_a), near(rc_b))
+    half_grads = []
+    partial = None
+    for low, rc in ((rows - rc_a.shape[0], rc_a), (0, rc_b)):
+        have = [] if partial is None else [near(partial)]
+        partial, part_grad = pl.pallas_call(
+            lambda *refs, low=low, chain=bool(have): grad_kernel(*refs, low=low, chain=chain),
+            out_shape=(pltpu.VMEM((KW, chans), f32), pltpu.VMEM((rc.shape[0], chans), f32)),
+            in_specs=[VMEM] * (3 + len(have)),
+            out_specs=(VMEM,) * 2,
+            compiler_params=limit(8),
+        )(near(base), near(fine), near(rc), *have)
+        half_grads.append(near(part_grad))
 
     d_fine = pl.pallas_call(
         fine_kernel,
         name="fine",
         out_shape=jax.ShapeDtypeStruct((2 * rows, chans), bf16),
-        in_specs=[VMEM] * 3,
+        in_specs=[VMEM] * 4,
         out_specs=VMEM,
         scratch_shapes=[
             pltpu.VMEM((tiles, 2 * rows, LANES), f32),
             pltpu.VMEM((rows + 2 * EDGE, LANES), f32),
         ],
         compiler_params=limit(8),
-    )(near(grad), near(ends), near(w_near))
+    )(*half_grads[::-1], near(ends), near(w_near))
 
     total = partial
     if count == 8 and lax.axis_size("dp") == 4:

time: 53.6 us -> 54.6 us (1.019)
  starting transfers between devices: 22.3 us -> 23.4 us
    ppermute x18, starting transfers between devices: 22.3 us -> 23.4 us  [swap(): lax.ppermute(value, axis, [(i, i ^ mask) for i in range(lax.axis_size(axi...]
  transfers between devices with their start and end apart: 18 -> 18, of which waited for: 10 -> 9; matrix products, arithmetic and copies ran while one was open for 0% -> 0% of each run, Pallas kernels for 14% -> 15%
where the time goes in v7:
time: 54.6 us; the launch traced here: 54.5 us
  starting transfers between devices  23.4 us (43%)
  waiting for transfers between devices  20.1 us (37%)
  Pallas kernels  9.62 us (18%)
  between operations  0.71 us (1%)
  other arithmetic  0.66 us (1%)
    ppermute x18, starting transfers between devices, swap(): lax.ppermute(value, axis, [(i, i ^ mask) for i in range(lax.axis_size(axi...  23.4 us
    ppermute x18, waiting for transfers between devices, swap(): lax.ppermute(value, axis, [(i, i ^ mask) for i in range(lax.axis_size(axi...  20.1 us
    pallas_call x1, Pallas kernels, body(): pl.pallas_call(lambda *refs: attend_kernel(*refs, parts=len(parts), per=r...  2.92 us
    pallas_call x1, Pallas kernels, body(): pl.pallas_call(lambda *refs: first_kernel(*refs, parts=len(early), per=ro...  1.69 us
    pallas_call x1, Pallas kernels, body(): pl.pallas_call(prep_kernel, name='prep', out_shape=(pltpu.VMEM(q.shape, b...  1.66 us
    pallas_call x1, Pallas kernels, body(): pl.pallas_call(fine_kernel, name='fine', out_shape=jax.ShapeDtypeStruct((...  1.38 us
    pallas_call x1, Pallas kernels, body(): pl.pallas_call(pack_kernel, name='pack', out_shape=(pltpu.VMEM((size, LAN...  1.3 us
  transfers between devices with their start and end apart: 18, of which 9 were waited for; matrix products, arithmetic and copies ran while one was open for 0% of the time, Pallas kernels for 15%

profile of v7, /device:TPU:0, one launch (start us, length us, event | category | flops | bytes accessed | tf_op | source)
XLA Modules:
  0.0 54.5 jit_solution(12619260281224573478)
XLA Ops:
  0.6 1.3 %pack.1 = (bf16[448,128]{1,0:T(8,128)(2,1)S(1)}, bf16[64,1536]{1,0:T(8,128)(2,1)S(1)}, bf16[64,1536]{1,0:T(8,128)(2,1)S(1)}) custom-call(bf16[128,128]{1,0:T(8,128)(2,1)} %bitcast.15, bf16[192,128]{1,0:T(8,128)(2,1)} %bitcast.14, bf16[128,1024]{1,0:T(8,128)(2,1)} %bitcast.10, bf16[256,1536]{1,0:T(8,128)(2,1)} %bitcast.8, bf16[128,1536]{1,0:T(8,128)(2,1)} %bitcast.13), custom_call_target="tpu_custom_call" | custom-call | tf_op jit(solution)/shard_map/pack/pallas_call | solution.py:305
  1.9 5.1 %collective-permute-start.9 = (bf16[64,1536]{1,0:T(8,128)(2,1)S(1)}, bf16[64,1536]{1,0:T(8,128)(2,1)S(1)}, u32[]{:S(2)}, u32[]{:S(2)}) collective-permute-start(bf16[64,1536]{1,0:T(8,128)(2,1)S(1)} %get-tuple-element.36), channel_id=1, source_target_pairs={{0,6},{1,7},{2,4},{3,5},{4,2},{5,3},{6,0},{7,1},{8,14},{9,15},{10,... | collective-permute-start | bytes 589832 | tf_op jit(solution)/shard_map/ppermute | solution.py:279
  7.1 1.5 %collective-permute-start.7 = (bf16[64,1536]{1,0:T(8,128)(2,1)S(1)}, bf16[64,1536]{1,0:T(8,128)(2,1)S(1)}, u32[]{:S(2)}, u32[]{:S(2)}) collective-permute-start(bf16[64,1536]{1,0:T(8,128)(2,1)S(1)} %get-tuple-element.35), channel_id=1, source_target_pairs={{0,1},{1,0},{2,3},{3,2},{4,5},{5,4},{6,7},{7,6},{8,9},{9,8},{10,11... | collective-permute-start | bytes 589832 | tf_op jit(solution)/shard_map/ppermute | solution.py:279
  8.6 0.0 collective-permute-start
  8.6 0.5 collective-permute-start.2
  9.1 0.6 %collective-permute-start.1 = (bf16[448,128]{1,0:T(8,128)(2,1)S(1)}, bf16[448,128]{1,0:T(8,128)(2,1)S(1)}, u32[]{:S(2)}, u32[]{:S(2)}) collective-permute-start(bf16[448,128]{1,0:T(8,128)(2,1)S(1)} %get-tuple-element.26.refs_1_.refs_10_), channel_id=1, source_target_pairs={{0,2},{1,3},{2,0},{3,1},{4,6},{5,7},{6,4},{7,5},{8,10},{9,11},{10,... | collective-permute-start | bytes 344072 | tf_op jit(solution)/shard_map/ppermute | solution.py:279
  9.8 10.5 %collective-permute-done.refs_2_.refs_11_ = bf16[448,128]{1,0:T(8,128)(2,1)S(1)} collective-permute-done((bf16[448,128]{1,0:T(8,128)(2,1)S(1)}, bf16[448,128]{1,0:T(8,128)(2,1)S(1)}, u32[]{:S(2)}, u32[]{:S(2)}) %collective-permute-start) | collective-permute-done | bytes 114720 | tf_op jit(solution)/shard_map/ppermute | solution.py:279
  20.3 0.0 collective-permute-start.3
  20.3 0.0 collective-permute-done.9
  20.3 1.5 %collective-permute-start.10 = (bf16[64,1536]{1,0:T(8,128)(2,1)S(1)}, bf16[64,1536]{1,0:T(8,128)(2,1)S(1)}, u32[]{:S(2)}, u32[]{:S(2)}) collective-permute-start(bf16[64,1536]{1,0:T(8,128)(2,1)S(1)} %collective-permute-done.9), channel_id=1, source_target_pairs={{0,1},{1,0},{2,3},{3,2},{4,5},{5,4},{6,7},{7,6},{8,9},{9,8},{10,11... | collective-permute-start | bytes 589832 | tf_op jit(solution)/shard_map/ppermute | solution.py:279
  21.8 0.0 collective-permute-done.7
  21.8 2.5 %collective-permute-start.8 = (bf16[64,1536]{1,0:T(8,128)(2,1)S(1)}, bf16[64,1536]{1,0:T(8,128)(2,1)S(1)}, u32[]{:S(2)}, u32[]{:S(2)}) collective-permute-start(bf16[64,1536]{1,0:T(8,128)(2,1)S(1)} %collective-permute-done.7), channel_id=1, source_target_pairs={{0,6},{1,7},{2,4},{3,5},{4,2},{5,3},{6,0},{7,1},{8,14},{9,15},{10,... | collective-permute-start | bytes 589832 | tf_op jit(solution)/shard_map/ppermute | solution.py:279
  24.3 0.0 collective-permute-done.2.refs_4_.refs_13_
  24.3 0.5 collective-permute-start.5
  24.8 0.0 collective-permute-done.1.refs_3_.refs_12_
  24.8 1.5 %collective-permute-start.4 = (bf16[448,128]{1,0:T(8,128)(2,1)S(1)}, bf16[448,128]{1,0:T(8,128)(2,1)S(1)}, u32[]{:S(2)}, u32[]{:S(2)}) collective-permute-start(bf16[448,128]{1,0:T(8,128)(2,1)S(1)} %collective-permute-done.1.refs_3_.refs_12_), channel_id=1, source_target_pairs={{0,1},{1,0},{2,3},{3,2},{4,5},{5,4},{6,7},{7,6},{8,9},{9,8},{10,11... | collective-permute-start | bytes 344072 | tf_op jit(solution)/shard_map/ppermute | solution.py:279
  26.3 0.0 collective-permute-done.3.refs_14_
  26.3 1.5 %collective-permute-start.6 = (bf16[448,128]{1,0:T(8,128)(2,1)S(1)}, bf16[448,128]{1,0:T(8,128)(2,1)S(1)}, u32[]{:S(2)}, u32[]{:S(2)}) collective-permute-start(bf16[448,128]{1,0:T(8,128)(2,1)S(1)} %collective-permute-done.3.refs_14_), channel_id=1, source_target_pairs={{0,1},{1,0},{2,3},{3,2},{4,5},{5,4},{6,7},{7,6},{8,9},{9,8},{10,11... | collective-permute-start | bytes 344072 | tf_op jit(solution)/shard_map/ppermute | solution.py:279
  27.8 1.7 %prep.1 = (bf16[128,1024]{1,0:T(8,128)(2,1)S(1)}, f32[5,1536]{1,0:T(8,128)S(1)}, f32[128,1536]{1,0:T(8,128)S(1)}, f32[12,272,128]{2,1,0:T(8,128)S(1)}) custom-call(bf16[128,1024]{1,0:T(8,128)(2,1)} %bitcast.11, bf16[256,1536]{1,0:T(8,128)(2,1)} %bitcast.9, f32[5,1536]{1,0:T(8,128)} %w.1), custom_call_target="tpu_custom_call" | custom-call | tf_op jit(solution)/shard_map/prep/pallas_call | solution.py:340
  29.5 1.7 %first.1 = (bf16[512,128]{1,0:T(8,128)(2,1)S(1)}, bf16[256,512]{1,0:T(8,128)(2,1)S(1)}, bf16[256,512]{1,0:T(8,128)(2,1)S(1)}, f32[8,128,128]{2,1,0:T(8,128)S(1)}...) custom-call(bf16[128,1024]{1,0:T(8,128)(2,1)S(1)} %get-tuple-element.22.refs_0_, ...), custom_call_target="tpu_custom_call" | custom-call | tf_op jit(solution)/shard_map/first/pallas_call | solution.py:358
  31.2 1.2 %collective-permute-done.4.refs_15_ = bf16[448,128]{1,0:T(8,128)(2,1)S(1)} collective-permute-done((bf16[448,128]{1,0:T(8,128)(2,1)S(1)}, bf16[448,128]{1,0:T(8,128)(2,1)S(1)}, u32[]{:S(2)}, u32[]{:S(2)}) %collective-permute-start.4) | collective-permute-done | bytes 114720 | tf_op jit(solution)/shard_map/ppermute | solution.py:279
  32.4 0.0 collective-permute-done.5.refs_16_
  32.4 1.2 %collective-permute-done.6.refs_17_ = bf16[448,128]{1,0:T(8,128)(2,1)S(1)} collective-permute-done((bf16[448,128]{1,0:T(8,128)(2,1)S(1)}, bf16[448,128]{1,0:T(8,128)(2,1)S(1)}, u32[]{:S(2)}, u32[]{:S(2)}) %collective-permute-start.6) | collective-permute-done | bytes 114720 | tf_op jit(solution)/shard_map/ppermute | solution.py:279
  33.6 2.9 %attend.1 = (f32[128,1536]{1,0:T(8,128)S(1)}, f32[8,1536]{1,0:T(8,128)S(1)}, f32[12,272,128]{2,1,0:T(8,128)S(1)}) custom-call(bf16[128,1024]{1,0:T(8,128)(2,1)S(1)} %get-tuple-element.22.refs_0_, f32[5,1536]{1,0:T(8,128)S(1)} %get-tuple-element.23.refs_1_.w, ...), custom_call_target="tpu_custom_call", output_to_operand_aliasing={{0}: (2, {}), {2}: (3, {})} | custom-call | tf_op jit(solution)/shard_map/attend/pallas_call | solution.py:374
  36.5 0.0 collective-permute-done.10.refs_2_
  36.6 0.3 shard_map.77
  36.9 0.0 collective-permute-done.8.refs_2_
  36.9 0.3 shard_map.78
  37.2 0.1 collective-permute-start.11
  37.3 1.2 %collective-permute-done.11 = f32[5,1536]{1,0:T(8,128)S(1)} collective-permute-done((f32[5,1536]{1,0:T(8,128)S(1)}, f32[5,1536]{1,0:T(8,128)S(1)}, u32[]{:S(2)}, u32[]{:S(2)}) %collective-permute-start.11) | collective-permute-done | bytes 30752 | tf_op jit(solution)/shard_map/ppermute | solution.py:279
  38.5 2.5 %collective-permute-start.14 = (f32[5,1536]{1,0:T(8,128)S(1)}, f32[5,1536]{1,0:T(8,128)S(1)}, u32[]{:S(2)}, u32[]{:S(2)}) collective-permute-start(f32[5,1536]{1,0:T(8,128)S(1)} %add.21), channel_id=1, source_target_pairs={{0,17},{1,16},{2,19},{3,18},{4,21},{5,20},{6,23},{7,22},{8,25},{9,... | collective-permute-start | bytes 92168 | tf_op jit(solution)/shard_map/ppermute | solution.py:279
  41.1 0.5 collective-permute-start.13
  41.6 0.5 collective-permute-start.12
  42.1 1.5 %collective-permute-done.14 = f32[5,1536]{1,0:T(8,128)S(1)} collective-permute-done((f32[5,1536]{1,0:T(8,128)S(1)}, f32[5,1536]{1,0:T(8,128)S(1)}, u32[]{:S(2)}, u32[]{:S(2)}) %collective-permute-start.14) | collective-permute-done | bytes 30752 | tf_op jit(solution)/shard_map/ppermute | solution.py:279
  43.6 1.5 %collective-permute-done.13 = f32[5,1536]{1,0:T(8,128)S(1)} collective-permute-done((f32[5,1536]{1,0:T(8,128)S(1)}, f32[5,1536]{1,0:T(8,128)S(1)}, u32[]{:S(2)}, u32[]{:S(2)}) %collective-permute-start.13) | collective-permute-done | bytes 30752 | tf_op jit(solution)/shard_map/ppermute | solution.py:279
  45.1 0.5 collective-permute-done.12
  45.7 3.1 %collective-permute-start.17 = (f32[5,1536]{1,0:T(8,128)S(1)}, f32[5,1536]{1,0:T(8,128)S(1)}, u32[]{:S(2)}, u32[]{:S(2)}) collective-permute-start(f32[5,1536]{1,0:T(8,128)S(1)} %add_add_fusion), channel_id=1, source_target_pairs={{0,6},{1,7},{2,4},{3,5},{4,2},{5,3},{6,0},{7,1},{8,14},{9,15},{10,... | collective-permute-start | bytes 92168 | tf_op jit(solution)/shard_map/ppermute | solution.py:279
  48.8 0.1 collective-permute-start.16
  48.9 1.2 %collective-permute-start.15 = (f32[5,1536]{1,0:T(8,128)S(1)}, f32[5,1536]{1,0:T(8,128)S(1)}, u32[]{:S(2)}, u32[]{:S(2)}) collective-permute-start(f32[5,1536]{1,0:T(8,128)S(1)} %add_add_fusion), channel_id=1, source_target_pairs={{0,2},{1,3},{2,0},{3,1},{4,6},{5,7},{6,4},{7,5},{8,10},{9,11},{10,... | collective-permute-start | bytes 92168 | tf_op jit(solution)/shard_map/ppermute | solution.py:279
  50.1 1.4 %fine.1 = bf16[256,1536]{1,0:T(8,128)(2,1)} custom-call(f32[64,1536]{1,0:T(8,128)S(1)} %get-tuple-element.38.grad_b, f32[64,1536]{1,0:T(8,128)S(1)} %get-tuple-element.39.grad_a, f32[8,1536]{1,0:T(8,128)S(1)} %get-tuple-element.40.ends, f32[5,1536]{1,0:T(8,128)S(1)} %get-tuple-element.23.refs_1_.w), custom_call_target="tpu_custom_call" | custom-call | tf_op jit(solution)/shard_map/fine/pallas_call | solution.py:415
  51.5 0.2 collective-permute-done.17
  51.7 2.1 %collective-permute-done.16 = f32[5,1536]{1,0:T(8,128)S(1)} collective-permute-done((f32[5,1536]{1,0:T(8,128)S(1)}, f32[5,1536]{1,0:T(8,128)S(1)}, u32[]{:S(2)}, u32[]{:S(2)}) %collective-permute-start.16) | collective-permute-done | bytes 30752 | tf_op jit(solution)/shard_map/ppermute | solution.py:279
  53.8 0.0 collective-permute-done.15
  53.8 0.6 %add_multiply_fusion = f32[5,1536]{1,0:T(8,128)} fusion(f32[5,1536]{1,0:T(8,128)S(1)} %collective-permute-done.17, f32[5,1536]{1,0:T(8,128)S(1)} %collective-permute-done.16, f32[5,1536]{1,0:T(8,128)S(1)} %add_add_fusion, f32[5,1536]{1,0:T(8,128)S(1)} %collective-permute-done.15), kind=kLoop, calls=%fused_computation | loop fusion | flops 30720 | bytes 153600 | tf_op jit(solution)/shard_map/mul | solution.py:437
  (2 shorter events, 0.0 us)
Async XLA Ops:
  1.9 18.3 %collective-permute-start.9 = (bf16[64,1536]{1,0:T(8,128)(2,1)S(1)}, bf16[64,1536]{1,0:T(8,128)(2,1)S(1)}, u32[]{:S(2)}, u32[]{:S(2)}) collective-permute-start(bf16[64,1536]{1,0:T(8,128)(2,1)S(1)} %get-tuple-element.36), channel_id=1, source_target_pairs={{0,6},{1,7},{2,4},{3,5},{4,2},{5,3},{6,0},{7,1},{8,14},{9,15},{10,... | collective-permute-start | bytes 589832 | tf_op jit(solution)/shard_map/ppermute | solution.py:279
  7.1 14.7 %collective-permute-start.7 = (bf16[64,1536]{1,0:T(8,128)(2,1)S(1)}, bf16[64,1536]{1,0:T(8,128)(2,1)S(1)}, u32[]{:S(2)}, u32[]{:S(2)}) collective-permute-start(bf16[64,1536]{1,0:T(8,128)(2,1)S(1)} %get-tuple-element.35), channel_id=1, source_target_pairs={{0,1},{1,0},{2,3},{3,2},{4,5},{5,4},{6,7},{7,6},{8,9},{9,8},{10,11... | collective-permute-start | bytes 589832 | tf_op jit(solution)/shard_map/ppermute | solution.py:279
  8.6 11.7 %collective-permute-start = (bf16[448,128]{1,0:T(8,128)(2,1)S(1)}, bf16[448,128]{1,0:T(8,128)(2,1)S(1)}, u32[]{:S(2)}, u32[]{:S(2)}) collective-permute-start(bf16[448,128]{1,0:T(8,128)(2,1)S(1)} %get-tuple-element.26.refs_1_.refs_10_), channel_id=1, source_target_pairs={{0,4},{1,5},{2,6},{3,7},{4,0},{5,1},{6,2},{7,3},{8,12},{9,13},{10,... | collective-permute-start | bytes 344072 | tf_op jit(solution)/shard_map/ppermute | solution.py:279
  8.6 15.7 %collective-permute-start.2 = (bf16[448,128]{1,0:T(8,128)(2,1)S(1)}, bf16[448,128]{1,0:T(8,128)(2,1)S(1)}, u32[]{:S(2)}, u32[]{:S(2)}) collective-permute-start(bf16[448,128]{1,0:T(8,128)(2,1)S(1)} %get-tuple-element.26.refs_1_.refs_10_), channel_id=1, source_target_pairs={{0,1},{1,0},{2,3},{3,2},{4,5},{5,4},{6,7},{7,6},{8,9},{9,8},{10,11... | collective-permute-start | bytes 344072 | tf_op jit(solution)/shard_map/ppermute | solution.py:279
  9.1 15.7 %collective-permute-start.1 = (bf16[448,128]{1,0:T(8,128)(2,1)S(1)}, bf16[448,128]{1,0:T(8,128)(2,1)S(1)}, u32[]{:S(2)}, u32[]{:S(2)}) collective-permute-start(bf16[448,128]{1,0:T(8,128)(2,1)S(1)} %get-tuple-element.26.refs_1_.refs_10_), channel_id=1, source_target_pairs={{0,2},{1,3},{2,0},{3,1},{4,6},{5,7},{6,4},{7,5},{8,10},{9,11},{10,... | collective-permute-start | bytes 344072 | tf_op jit(solution)/shard_map/ppermute | solution.py:279
  20.3 6.0 %collective-permute-start.3 = (bf16[448,128]{1,0:T(8,128)(2,1)S(1)}, bf16[448,128]{1,0:T(8,128)(2,1)S(1)}, u32[]{:S(2)}, u32[]{:S(2)}) collective-permute-start(bf16[448,128]{1,0:T(8,128)(2,1)S(1)} %collective-permute-done.refs_2_.refs_11_), channel_id=1, source_target_pairs={{0,2},{1,3},{2,0},{3,1},{4,6},{5,7},{6,4},{7,5},{8,10},{9,11},{10,... | collective-permute-start | bytes 344072 | tf_op jit(solution)/shard_map/ppermute | solution.py:279
  20.3 16.3 %collective-permute-start.10 = (bf16[64,1536]{1,0:T(8,128)(2,1)S(1)}, bf16[64,1536]{1,0:T(8,128)(2,1)S(1)}, u32[]{:S(2)}, u32[]{:S(2)}) collective-permute-start(bf16[64,1536]{1,0:T(8,128)(2,1)S(1)} %collective-permute-done.9), channel_id=1, source_target_pairs={{0,1},{1,0},{2,3},{3,2},{4,5},{5,4},{6,7},{7,6},{8,9},{9,8},{10,11... | collective-permute-start | bytes 589832 | tf_op jit(solution)/shard_map/ppermute | solution.py:279
  21.8 15.1 %collective-permute-start.8 = (bf16[64,1536]{1,0:T(8,128)(2,1)S(1)}, bf16[64,1536]{1,0:T(8,128)(2,1)S(1)}, u32[]{:S(2)}, u32[]{:S(2)}) collective-permute-start(bf16[64,1536]{1,0:T(8,128)(2,1)S(1)} %collective-permute-done.7), channel_id=1, source_target_pairs={{0,6},{1,7},{2,4},{3,5},{4,2},{5,3},{6,0},{7,1},{8,14},{9,15},{10,... | collective-permute-start | bytes 589832 | tf_op jit(solution)/shard_map/ppermute | solution.py:279
  24.3 8.1 %collective-permute-start.5 = (bf16[448,128]{1,0:T(8,128)(2,1)S(1)}, bf16[448,128]{1,0:T(8,128)(2,1)S(1)}, u32[]{:S(2)}, u32[]{:S(2)}) collective-permute-start(bf16[448,128]{1,0:T(8,128)(2,1)S(1)} %collective-permute-done.refs_2_.refs_11_), channel_id=1, source_target_pairs={{0,1},{1,0},{2,3},{3,2},{4,5},{5,4},{6,7},{7,6},{8,9},{9,8},{10,11... | collective-permute-start | bytes 344072 | tf_op jit(solution)/shard_map/ppermute | solution.py:279
  24.8 7.6 %collective-permute-start.4 = (bf16[448,128]{1,0:T(8,128)(2,1)S(1)}, bf16[448,128]{1,0:T(8,128)(2,1)S(1)}, u32[]{:S(2)}, u32[]{:S(2)}) collective-permute-start(bf16[448,128]{1,0:T(8,128)(2,1)S(1)} %collective-permute-done.1.refs_3_.refs_12_), channel_id=1, source_target_pairs={{0,1},{1,0},{2,3},{3,2},{4,5},{5,4},{6,7},{7,6},{8,9},{9,8},{10,11... | collective-permute-start | bytes 344072 | tf_op jit(solution)/shard_map/ppermute | solution.py:279
  26.3 7.3 %collective-permute-start.6 = (bf16[448,128]{1,0:T(8,128)(2,1)S(1)}, bf16[448,128]{1,0:T(8,128)(2,1)S(1)}, u32[]{:S(2)}, u32[]{:S(2)}) collective-permute-start(bf16[448,128]{1,0:T(8,128)(2,1)S(1)} %collective-permute-done.3.refs_14_), channel_id=1, source_target_pairs={{0,1},{1,0},{2,3},{3,2},{4,5},{5,4},{6,7},{7,6},{8,9},{9,8},{10,11... | collective-permute-start | bytes 344072 | tf_op jit(solution)/shard_map/ppermute | solution.py:279
  37.2 1.3 %collective-permute-start.11 = (f32[5,1536]{1,0:T(8,128)S(1)}, f32[5,1536]{1,0:T(8,128)S(1)}, u32[]{:S(2)}, u32[]{:S(2)}) collective-permute-start(f32[5,1536]{1,0:T(8,128)S(1)} %get-tuple-element.41), channel_id=1, source_target_pairs={{0,8},{1,9},{2,10},{3,11},{4,12},{5,13},{6,14},{7,15},{8,0},{9,1},... | collective-permute-start | bytes 92168 | tf_op jit(solution)/shard_map/ppermute | solution.py:279
  38.5 5.1 %collective-permute-start.14 = (f32[5,1536]{1,0:T(8,128)S(1)}, f32[5,1536]{1,0:T(8,128)S(1)}, u32[]{:S(2)}, u32[]{:S(2)}) collective-permute-start(f32[5,1536]{1,0:T(8,128)S(1)} %add.21), channel_id=1, source_target_pairs={{0,17},{1,16},{2,19},{3,18},{4,21},{5,20},{6,23},{7,22},{8,25},{9,... | collective-permute-start | bytes 92168 | tf_op jit(solution)/shard_map/ppermute | solution.py:279
  41.1 4.1 %collective-permute-start.13 = (f32[5,1536]{1,0:T(8,128)S(1)}, f32[5,1536]{1,0:T(8,128)S(1)}, u32[]{:S(2)}, u32[]{:S(2)}) collective-permute-start(f32[5,1536]{1,0:T(8,128)S(1)} %add.21), channel_id=1, source_target_pairs={{0,1},{1,0},{2,3},{3,2},{4,5},{5,4},{6,7},{7,6},{8,9},{9,8},{10,11... | collective-permute-start | bytes 92168 | tf_op jit(solution)/shard_map/ppermute | solution.py:279
  41.6 4.1 %collective-permute-start.12 = (f32[5,1536]{1,0:T(8,128)S(1)}, f32[5,1536]{1,0:T(8,128)S(1)}, u32[]{:S(2)}, u32[]{:S(2)}) collective-permute-start(f32[5,1536]{1,0:T(8,128)S(1)} %add.21), channel_id=1, source_target_pairs={{0,16},{1,17},{2,18},{3,19},{4,20},{5,21},{6,22},{7,23},{8,24},{9,... | collective-permute-start | bytes 92168 | tf_op jit(solution)/shard_map/ppermute | solution.py:279
  45.7 6.1 %collective-permute-start.17 = (f32[5,1536]{1,0:T(8,128)S(1)}, f32[5,1536]{1,0:T(8,128)S(1)}, u32[]{:S(2)}, u32[]{:S(2)}) collective-permute-start(f32[5,1536]{1,0:T(8,128)S(1)} %add_add_fusion), channel_id=1, source_target_pairs={{0,6},{1,7},{2,4},{3,5},{4,2},{5,3},{6,0},{7,1},{8,14},{9,15},{10,... | collective-permute-start | bytes 92168 | tf_op jit(solution)/shard_map/ppermute | solution.py:279
  48.8 5.0 %collective-permute-start.16 = (f32[5,1536]{1,0:T(8,128)S(1)}, f32[5,1536]{1,0:T(8,128)S(1)}, u32[]{:S(2)}, u32[]{:S(2)}) collective-permute-start(f32[5,1536]{1,0:T(8,128)S(1)} %add_add_fusion), channel_id=1, source_target_pairs={{0,4},{1,5},{2,6},{3,7},{4,0},{5,1},{6,2},{7,3},{8,12},{9,13},{10,... | collective-permute-start | bytes 92168 | tf_op jit(solution)/shard_map/ppermute | solution.py:279
  48.9 4.9 %collective-permute-start.15 = (f32[5,1536]{1,0:T(8,128)S(1)}, f32[5,1536]{1,0:T(8,128)S(1)}, u32[]{:S(2)}, u32[]{:S(2)}) collective-permute-start(f32[5,1536]{1,0:T(8,128)S(1)} %add_add_fusion), channel_id=1, source_target_pairs={{0,2},{1,3},{2,0},{3,1},{4,6},{5,7},{6,4},{7,5},{8,10},{9,11},{10,... | collective-permute-start | bytes 92168 | tf_op jit(solution)/shard_map/ppermute | solution.py:279
